TPU v7x, 32 devices: a whole 2x2x4 slice. The times are simulated.
32 devices in a mesh: dp: 8 (over z, x), fsdp: 4 (over y, core).
Axes of the slice: x: 2, y: 2, z: 4, core: 2. Of those that a mesh axis runs over, the one named last changes fastest.
Arguments:
- latents: float32 [96, 256, 384], P(('dp', 'fsdp')), may hold values from -6 to 6
- conditioning: float32 [96, 384], P(('dp', 'fsdp')), may hold values from -6 to 6
- seq_counts: int32 [32], P(('dp', 'fsdp')), may hold values from 1 to 3, as said below
- cotangent: float32 [96, 256, 384], P(('dp', 'fsdp')), may hold values from -6 to 6
- ada_weight: bfloat16 [2, 384, 2304], P(None, 'fsdp'), may hold values from -0.3125 to 0.3125
- ada_bias: bfloat16 [2, 2304], P(None, 'fsdp'), may hold values from -2.390625 to 2.390625
- qkv_weight: bfloat16 [2, 384, 1152], P(None, 'fsdp'), may hold values from -0.3125 to 0.3125
- proj_weight: bfloat16 [2, 384, 384], P(None, 'fsdp'), may hold values from -6 to 6
- proj_bias: bfloat16 [2, 384], P(None, 'fsdp'), may hold values from -3.59375 to 3.59375
- up_weight: bfloat16 [2, 384, 1536], P(None, 'fsdp'), may hold values from -0.3125 to 0.3125
- up_bias: bfloat16 [2, 1536], P(None, 'fsdp'), may hold values from -3.59375 to 3.59375
- down_weight: bfloat16 [2, 1536, 384], P(None, 'fsdp'), may hold values from -0.15625 to 0.15625
- down_bias: bfloat16 [2, 384], P(None, 'fsdp'), may hold values from -3.59375 to 3.59375
Outputs:
- block_out: float32 [96, 256, 384], P(('dp', 'fsdp'))
- grad_latents: float32 [96, 256, 384], P(('dp', 'fsdp'))
- grad_conditioning: float32 [96, 384], P(('dp', 'fsdp'))
- grad_ada_weight: float32 [2, 384, 2304], P(None, 'fsdp')
- grad_ada_bias: float32 [2, 2304], P(None, 'fsdp')
- grad_qkv_weight: float32 [2, 384, 1152], P(None, 'fsdp')
- grad_proj_weight: float32 [2, 384, 384], P(None, 'fsdp')
- grad_proj_bias: float32 [2, 384], P(None, 'fsdp')
- grad_up_weight: float32 [2, 384, 1536], P(None, 'fsdp')
- grad_up_bias: float32 [2, 1536], P(None, 'fsdp')
- grad_down_weight: float32 [2, 1536, 384], P(None, 'fsdp')
- grad_down_bias: float32 [2, 384], P(None, 'fsdp')
Inputs may be any that keep to these rules, and one draw needn't show every extreme that they name: `seq_counts`: number of live sequences of a device; its slots from that number on are padding.
All inputs are finite; a program needn't handle non-finite values.
Results may differ from a plain program's by a relative error of at most 0.014.
Values may be sent and summed in bfloat16 or wider, within the bound.
No kernel may reach another device: no remote copies, remote signals or barrier semaphores. Data moves between devices by JAX's collectives and lax.ppermute only.
A program may use at most 192 MiB of HBM per device.

v0:
```python
import jax
import jax.numpy as jnp
from jax import lax
from jax.sharding import PartitionSpec as P

HEADS = 6
LAYERS = 2


NORM_EPS = 1e-06
GELU_K = 0.7978845608028654
GELU_C = 0.044715


def einsum_mixed(form, left, right):
    return jnp.einsum(form, left, right, preferred_element_type=jnp.float32)


def matmul_last(left, right):
    flat = left.reshape(-1, left.shape[-1])
    return jnp.dot(flat, right, preferred_element_type=jnp.float32).reshape(
        left.shape[:-1] + (right.shape[1],)
    )


def matmul_back(left, right):
    flat = left.reshape(-1, left.shape[-1])
    return jnp.dot(flat, right.T, preferred_element_type=jnp.float32).reshape(
        left.shape[:-1] + (right.shape[0],)
    )


def outer_total(left, right):
    return jnp.dot(
        left.reshape(-1, left.shape[-1]).T,
        right.reshape(-1, right.shape[-1]),
        preferred_element_type=jnp.float32,
    )


def norm_rows(values):
    center = values - jnp.mean(values, axis=-1, keepdims=True)
    inv_std = lax.rsqrt(jnp.mean(center * center, axis=-1, keepdims=True) + NORM_EPS)
    return (center * inv_std, inv_std)


def norm_back(normed, inv_std, grad_normed):
    mean_grad = jnp.mean(grad_normed, axis=-1, keepdims=True)
    mean_prod = jnp.mean(grad_normed * normed, axis=-1, keepdims=True)
    return inv_std * (grad_normed - mean_grad - normed * mean_prod)


def gelu_tanh(values):
    inner = GELU_K * (values + GELU_C * values * values * values)
    return 0.5 * values * (1.0 + jnp.tanh(inner))


def gelu_slope(values):
    tangent = jnp.tanh(GELU_K * (values + GELU_C * values * values * values))
    return 0.5 * (1.0 + tangent) + 0.5 * values * (1.0 - tangent * tangent) * GELU_K * (
        1.0 + 3.0 * GELU_C * values * values
    )


def silu_slope(values):
    sigm = jax.nn.sigmoid(values)
    return sigm * (1.0 + values * (1.0 - sigm))


def split_heads(qkv):
    seq_slots, length, triple = qkv.shape
    width = triple // 3
    split = qkv.reshape(seq_slots, length, 3, HEADS, width // HEADS)
    return (split[:, :, 0], split[:, :, 1], split[:, :, 2])


def attend(qkv):
    queries, keys, values = split_heads(qkv)
    scale = 1.0 / jnp.sqrt(jnp.float32(queries.shape[-1]))
    scores = einsum_mixed("sqhd,skhd->shqk", queries, keys) * scale
    top = jnp.max(scores, axis=-1, keepdims=True)
    expo = jnp.exp(scores - top)
    probs = expo / jnp.sum(expo, axis=-1, keepdims=True)
    probs_low = probs.astype(jnp.bfloat16)
    mixed = einsum_mixed("shqk,skhd->sqhd", probs_low, values).astype(jnp.bfloat16)
    return (probs, probs_low, mixed.reshape(qkv.shape[0], qkv.shape[1], -1))


def attend_back(qkv, probs, probs_low, grad_mixed):
    queries, keys, values = split_heads(qkv)
    scale = 1.0 / jnp.sqrt(jnp.float32(queries.shape[-1]))
    grad_heads = grad_mixed.reshape(values.shape)
    grad_probs = einsum_mixed("sqhd,skhd->shqk", grad_heads, values)
    grad_values = einsum_mixed("shqk,sqhd->skhd", probs_low, grad_heads)
    row_dot = jnp.sum(probs * grad_probs, axis=-1, keepdims=True)
    grad_scores = (probs * (grad_probs - row_dot) * scale).astype(jnp.bfloat16)
    grad_queries = einsum_mixed("shqk,skhd->sqhd", grad_scores, keys)
    grad_keys = einsum_mixed("shqk,sqhd->skhd", grad_scores, queries)
    joined = jnp.stack([grad_queries, grad_keys, grad_values], axis=2)
    return joined.reshape(qkv.shape).astype(jnp.bfloat16)


def layer_parts(resid, cond, weights):
    (
        ada_weight,
        ada_bias,
        qkv_weight,
        proj_weight,
        proj_bias,
        up_weight,
        up_bias,
        down_weight,
        down_bias,
    ) = weights
    width = resid.shape[-1]
    act_low = jax.nn.silu(cond).astype(jnp.bfloat16)
    ada = jnp.dot(act_low, ada_weight, preferred_element_type=jnp.float32) + ada_bias.astype(
        jnp.float32
    )
    mods = [ada[:, None, piece_idx * width : (piece_idx + 1) * width] for piece_idx in range(6)]
    normed_one, inv_one = norm_rows(resid)
    attn_in = (normed_one * (1.0 + mods[1]) + mods[0]).astype(jnp.bfloat16)
    qkv = matmul_last(attn_in, qkv_weight).astype(jnp.bfloat16)
    probs, probs_low, mixed = attend(qkv)
    attn = matmul_last(mixed, proj_weight) + proj_bias.astype(jnp.float32)
    resid_one = resid + mods[2] * attn
    normed_two, inv_two = norm_rows(resid_one)
    mlp_in = (normed_two * (1.0 + mods[4]) + mods[3]).astype(jnp.bfloat16)
    pre_act = matmul_last(mlp_in, up_weight) + up_bias.astype(jnp.float32)
    hidden = gelu_tanh(pre_act).astype(jnp.bfloat16)
    branch = matmul_last(hidden, down_weight) + down_bias.astype(jnp.float32)
    result = resid_one + mods[5] * branch
    return dict(
        act_low=act_low,
        mods=mods,
        normed_one=normed_one,
        inv_one=inv_one,
        attn_in=attn_in,
        qkv=qkv,
        probs=probs,
        probs_low=probs_low,
        mixed=mixed,
        attn=attn,
        normed_two=normed_two,
        inv_two=inv_two,
        mlp_in=mlp_in,
        pre_act=pre_act,
        hidden=hidden,
        branch=branch,
        result=result,
    )


def layer_backward(resid, cond, weights, grad_out):
    (
        ada_weight,
        ada_bias,
        qkv_weight,
        proj_weight,
        proj_bias,
        up_weight,
        up_bias,
        down_weight,
        down_bias,
    ) = weights
    saved = layer_parts(resid, cond, weights)
    mods = saved["mods"]
    grad_gate_two = jnp.sum(grad_out * saved["branch"], axis=1)
    grad_branch = grad_out * mods[5]
    grad_down_bias = jnp.sum(grad_branch, axis=(0, 1))
    branch_low = grad_branch.astype(jnp.bfloat16)
    grad_down_weight = outer_total(saved["hidden"], branch_low)
    grad_pre = matmul_back(branch_low, down_weight) * gelu_slope(saved["pre_act"])
    grad_up_bias = jnp.sum(grad_pre, axis=(0, 1))
    pre_low = grad_pre.astype(jnp.bfloat16)
    grad_up_weight = outer_total(saved["mlp_in"], pre_low)
    grad_mlp = matmul_back(pre_low, up_weight)
    grad_shift_two = jnp.sum(grad_mlp, axis=1)
    grad_scale_two = jnp.sum(grad_mlp * saved["normed_two"], axis=1)
    grad_one = grad_out + norm_back(
        saved["normed_two"], saved["inv_two"], grad_mlp * (1.0 + mods[4])
    )
    grad_gate_one = jnp.sum(grad_one * saved["attn"], axis=1)
    grad_attn = grad_one * mods[2]
    grad_proj_bias = jnp.sum(grad_attn, axis=(0, 1))
    attn_low = grad_attn.astype(jnp.bfloat16)
    grad_proj_weight = outer_total(saved["mixed"], attn_low)
    grad_mixed = matmul_back(attn_low, proj_weight).astype(jnp.bfloat16)
    grad_qkv = attend_back(saved["qkv"], saved["probs"], saved["probs_low"], grad_mixed)
    grad_qkv_weight = outer_total(saved["attn_in"], grad_qkv)
    grad_in = matmul_back(grad_qkv, qkv_weight)
    grad_shift_one = jnp.sum(grad_in, axis=1)
    grad_scale_one = jnp.sum(grad_in * saved["normed_one"], axis=1)
    grad_resid = grad_one + norm_back(
        saved["normed_one"], saved["inv_one"], grad_in * (1.0 + mods[1])
    )
    grad_ada = jnp.concatenate(
        [
            grad_shift_one,
            grad_scale_one,
            grad_gate_one,
            grad_shift_two,
            grad_scale_two,
            grad_gate_two,
        ],
        axis=-1,
    )
    grad_ada_bias = jnp.sum(grad_ada, axis=0)
    ada_low = grad_ada.astype(jnp.bfloat16)
    grad_ada_weight = jnp.dot(saved["act_low"].T, ada_low, preferred_element_type=jnp.float32)
    grad_cond = jnp.dot(ada_low, ada_weight.T, preferred_element_type=jnp.float32) * silu_slope(
        cond
    )
    grads = (
        grad_ada_weight,
        grad_ada_bias,
        grad_qkv_weight,
        grad_proj_weight,
        grad_proj_bias,
        grad_up_weight,
        grad_up_bias,
        grad_down_weight,
        grad_down_bias,
    )
    return (grad_resid, grad_cond, grads)


def gather_forward(stacks, layer_idx):
    (
        ada_weight,
        ada_bias,
        qkv_weight,
        proj_weight,
        proj_bias,
        up_weight,
        up_bias,
        down_weight,
        down_bias,
    ) = stacks
    return (
        lax.all_gather(ada_weight[layer_idx], "fsdp", axis=0, tiled=True),
        lax.all_gather(ada_bias[layer_idx], "fsdp", axis=0, tiled=True),
        lax.all_gather(qkv_weight[layer_idx], "fsdp", axis=0, tiled=True),
        lax.all_gather(proj_weight[layer_idx], "fsdp", axis=0, tiled=True),
        lax.all_gather(proj_bias[layer_idx], "fsdp", axis=0, tiled=True),
        lax.all_gather(up_weight[layer_idx], "fsdp", axis=0, tiled=True),
        lax.all_gather(up_bias[layer_idx], "fsdp", axis=0, tiled=True),
        lax.all_gather(down_weight[layer_idx], "fsdp", axis=0, tiled=True),
        lax.all_gather(down_bias[layer_idx], "fsdp", axis=0, tiled=True),
    )


def gather_backward(stacks, layer_idx):
    (
        ada_weight,
        ada_bias,
        qkv_weight,
        proj_weight,
        proj_bias,
        up_weight,
        up_bias,
        down_weight,
        down_bias,
    ) = stacks
    return (
        lax.all_gather(ada_weight[layer_idx], "fsdp", axis=0, tiled=True),
        lax.all_gather(ada_bias[layer_idx], "fsdp", axis=0, tiled=True),
        lax.all_gather(qkv_weight[layer_idx], "fsdp", axis=0, tiled=True),
        lax.all_gather(proj_weight[layer_idx], "fsdp", axis=0, tiled=True),
        lax.all_gather(proj_bias[layer_idx], "fsdp", axis=0, tiled=True),
        lax.all_gather(up_weight[layer_idx], "fsdp", axis=0, tiled=True),
        lax.all_gather(up_bias[layer_idx], "fsdp", axis=0, tiled=True),
        lax.all_gather(down_weight[layer_idx], "fsdp", axis=0, tiled=True),
        lax.all_gather(down_bias[layer_idx], "fsdp", axis=0, tiled=True),
    )


def reduce_layer(grads):
    shards = (
        lax.psum_scatter(grads[0], "fsdp", scatter_dimension=0, tiled=True),
        lax.psum_scatter(grads[1], "fsdp", scatter_dimension=0, tiled=True),
        lax.psum_scatter(grads[2], "fsdp", scatter_dimension=0, tiled=True),
        lax.psum_scatter(grads[3], "fsdp", scatter_dimension=0, tiled=True),
        lax.psum_scatter(grads[4], "fsdp", scatter_dimension=0, tiled=True),
        lax.psum_scatter(grads[5], "fsdp", scatter_dimension=0, tiled=True),
        lax.psum_scatter(grads[6], "fsdp", scatter_dimension=0, tiled=True),
        lax.psum_scatter(grads[7], "fsdp", scatter_dimension=0, tiled=True),
        lax.psum_scatter(grads[8], "fsdp", scatter_dimension=0, tiled=True),
    )
    return lax.psum(
        (
            shards[0],
            shards[1],
            shards[2],
            shards[3],
            shards[4],
            shards[5],
            shards[6],
            shards[7],
            shards[8],
        ),
        "dp",
    )


def on_device(
    latents,
    conditioning,
    seq_counts,
    cotangent,
    ada_weight,
    ada_bias,
    qkv_weight,
    proj_weight,
    proj_bias,
    up_weight,
    up_bias,
    down_weight,
    down_bias,
):
    stacks = (
        ada_weight,
        ada_bias,
        qkv_weight,
        proj_weight,
        proj_bias,
        up_weight,
        up_bias,
        down_weight,
        down_bias,
    )
    seq_slots = latents.shape[0]
    live = (jnp.arange(seq_slots, dtype=jnp.int32) < seq_counts[0]).astype(jnp.float32)[
        :, None, None
    ]
    inputs = []
    gathered = []
    current = latents
    for layer_idx in range(LAYERS):
        weights = gather_forward(stacks, layer_idx)
        gathered.append(weights)
        inputs.append(current)
        current = layer_parts(current, conditioning, weights)["result"]
    block_out = current * live
    grad = cotangent * live
    grad_cond = jnp.zeros(conditioning.shape, jnp.float32)
    layer_grads = [None] * LAYERS
    for layer_idx in reversed(range(LAYERS)):
        weights = gather_backward(stacks, layer_idx)
        grad, cond_part, grads = layer_backward(inputs[layer_idx], conditioning, weights, grad)
        grad_cond = grad_cond + cond_part
        layer_grads[layer_idx] = reduce_layer(grads)
    finals = [
        jnp.stack([layer_grads[layer_idx][piece_idx] for layer_idx in range(LAYERS)], axis=0)
        for piece_idx in range(9)
    ]
    return (
        block_out,
        grad,
        grad_cond,
        finals[0],
        finals[1],
        finals[2],
        finals[3],
        finals[4],
        finals[5],
        finals[6],
        finals[7],
        finals[8],
    )


def solution(mesh):
    in_specs = (
        P(("dp", "fsdp"), None, None),
        P(("dp", "fsdp"), None),
        P(("dp", "fsdp")),
        P(("dp", "fsdp"), None, None),
        P(None, "fsdp", None),
        P(None, "fsdp"),
        P(None, "fsdp", None),
        P(None, "fsdp", None),
        P(None, "fsdp"),
        P(None, "fsdp", None),
        P(None, "fsdp"),
        P(None, "fsdp", None),
        P(None, "fsdp"),
    )
    out_specs = (
        P(("dp", "fsdp"), None, None),
        P(("dp", "fsdp"), None, None),
        P(("dp", "fsdp"), None),
        P(None, "fsdp", None),
        P(None, "fsdp"),
        P(None, "fsdp", None),
        P(None, "fsdp", None),
        P(None, "fsdp"),
        P(None, "fsdp", None),
        P(None, "fsdp"),
        P(None, "fsdp", None),
        P(None, "fsdp"),
    )
    return jax.shard_map(
        on_device, mesh=mesh, in_specs=in_specs, out_specs=out_specs, check_vma=False
    )
```

profile of v0, /device:TPU:0, one launch (start us, length us, event | category | flops | bytes accessed | tf_op | source)
XLA Modules:
  0.0 732.9 jit_solution(9864900961176631379)
XLA Ops:
  17.1 6.2 all-gather.15
  23.9 5.7 all-gather.6
  31.0 11.7 %all-reduce.17 = (bf16[2304]{0:T(1024)(128)(2,1)S(1)}, bf16[384]{0:T(512)(128)(2,1)S(1)}, bf16[384]{0:T(512)(128)(2,1)S(1)}, bf16[2304]{0:T(1024)(128)(2,1)S(1)}...) all-reduce(bf16[2304]{0:T(1024)(128)(2,1)S(1)} %dynamic-update-slice, ...), channel_id=3, replica_groups=mesh['dp'=8,'fsdp'=4] {'fsdp'}, use_global_device_ids=true, to_apply=%add | all-reduce | flops 6144 | bytes 24576
  43.9 8.0 %all-gather.12 = bf16[1,384,384]{2,1,0:T(8,128)(2,1)} all-gather(bf16[1,96,384]{2,1,0:T(8,128)(2,1)S(1)} %get-tuple-element.91), channel_id=14, replica_groups=mesh['dp'=8,'fsdp'=4] {'fsdp'}, dimensions={1}, use_global_device_ids=true | all-gather | bytes 368640 | tf_op jit(solution)/shard_map/all_gather | solution.py:244
  51.9 7.2 all-gather.3
  59.1 9.7 %all-gather.11 = bf16[1,384,1152]{2,1,0:T(8,128)(2,1)} all-gather(bf16[1,96,1152]{2,1,0:T(8,128)(2,1)S(1)} %get-tuple-element.89), channel_id=13, replica_groups=mesh['dp'=8,'fsdp'=4] {'fsdp'}, dimensions={1}, use_global_device_ids=true | all-gather | bytes 1105920 | tf_op jit(solution)/shard_map/all_gather | solution.py:243
  68.8 13.9 %all-gather.2 = bf16[1,384,1152]{2,1,0:T(8,128)(2,1)S(1)} all-gather(bf16[1,96,1152]{2,1,0:T(8,128)(2,1)S(1)} %get-tuple-element.90), channel_id=4, replica_groups=mesh['dp'=8,'fsdp'=4] {'fsdp'}, dimensions={1}, use_global_device_ids=true | all-gather | bytes 1105920 | tf_op jit(solution)/shard_map/all_gather | solution.py:243
  101.3 4.8 fusion.88
  106.1 5.8 fusion.135
  131.3 5.0 fusion.82
  140.6 7.6 %fusion.148 = (f32[1536]{0:T(1024)}, bf16[3,256,1536]{2,1,0:T(8,128)(2,1)S(1)}) fusion(f32[3,256,1536]{2,1,0:T(8,128)} %fusion.82, f32[1536]{0:T(1024)} %convert_reduce_fusion, bf16[1,1536,384]{2,1,0:T(8,128)(2,1)} %all-gather.35.cloned.1.call-done, f32[3,256,384]{2,1,0:T(8,128)} %param.16, f32[3]{0:T(128)} %compare_convert_fusion, ...), kind=kOutput, calls=%fused_computation.256 | convolution fusion | flops 931625472 | bytes 9454092 | tf_op jit(solution)/shard_map/dot_general | solution.py:28
  152.2 4.5 multiply_reduce_fusion.23
  170.4 9.1 %fusion.67 = bf16[3,256,1,6,64]{1,4,3,0,2:T(8,128)(2,1)} fusion(f32[3,6,256,256]{2,3,1,0:T(8,128)} %fusion.112, bf16[3,256,3,6,64]{1,4,3,2,0:T(8,128)(2,1)} %bitcast.237, f32[3,6,256,256]{2,3,1,0:T(8,128)} %copy-done.18, f32[3,6,256]{2,1,0:T(8,128)} %copy-done.81), kind=kOutput, calls=%fused_computation.80 | convolution fusion | flops 159552256 | bytes 20103168 | tf_op jit(solution)/shard_map/shqk,skhd->sqhd/dot_general | solution.py:16
  179.4 8.9 %fusion.64 = bf16[3,256,1,6,64]{1,4,3,0,2:T(8,128)(2,1)} fusion(f32[3,6,256,256]{2,3,1,0:T(8,128)} %fusion.112, bf16[3,256,3,6,64]{1,4,3,2,0:T(8,128)(2,1)} %bitcast.238, f32[3,6,256,256]{2,3,1,0:T(8,128)} %copy-done.18, f32[3,6,256]{2,1,0:T(8,128)} %copy-done.81), kind=kOutput, calls=%fused_computation.79 | convolution fusion | flops 159552256 | bytes 20103168 | tf_op jit(solution)/shard_map/shqk,sqhd->skhd/dot_general | solution.py:16
  198.5 4.9 fusion.149
  211.4 4.4 convolution_bitcast_fusion.4
  225.1 9.0 %fusion.73 = bf16[3,256,1,6,64]{1,4,3,0,2:T(8,128)(2,1)} fusion(f32[3,6,256,256]{2,3,1,0:T(8,128)} %fusion.110, bf16[3,256,3,6,64]{1,4,3,2,0:T(8,128)(2,1)} %bitcast.232, f32[3,6,256,256]{2,3,1,0:T(8,128)} %copy-done.17, f32[3,6,256]{2,1,0:T(8,128)} %copy-done.80), kind=kOutput, calls=%fused_computation.82 | convolution fusion | flops 159552256 | bytes 20103168 | tf_op jit(solution)/shard_map/shqk,skhd->sqhd/dot_general | solution.py:16
  234.0 9.0 %fusion.70 = bf16[3,256,1,6,64]{1,4,3,0,2:T(8,128)(2,1)} fusion(f32[3,6,256,256]{2,3,1,0:T(8,128)} %fusion.110, bf16[3,256,3,6,64]{1,4,3,2,0:T(8,128)(2,1)} %bitcast.233, f32[3,6,256,256]{2,3,1,0:T(8,128)} %copy-done.17, f32[3,6,256]{2,1,0:T(8,128)} %copy-done.80), kind=kOutput, calls=%fused_computation.81 | convolution fusion | flops 159552256 | bytes 20103168 | tf_op jit(solution)/shard_map/shqk,sqhd->skhd/dot_general | solution.py:16
  250.8 6.5 convolution_bitcast_fusion
  257.3 4.4 convolution_bitcast_fusion.2
  263.0 6.3 convolution_bitcast_fusion.1
  270.0 4.4 convolution_bitcast_fusion.3
  285.6 16.0 %reduce-scatter.15.cloned.1.call-done = f32[96,1152]{1,0:T(8,128)} async-done(((f32[384,1152]{1,0:T(8,128)}), f32[96,1152]{1,0:T(8,128)}) %reduce-scatter.15.cloned.1.call-update) | async-done | bytes 442384 | tf_op jit(solution)/shard_map/reduce_scatter | solution.py:282
  301.7 35.4 %reduce-scatter.29.cloned.1.call-done = f32[384,384]{1,0:T(8,128)} async-done(((f32[1536,384]{1,0:T(8,128)}), f32[384,384]{1,0:T(8,128)}) %reduce-scatter.29.cloned.1.call-update) | async-done | bytes 589840 | tf_op jit(solution)/shard_map/reduce_scatter | solution.py:287
  337.0 35.2 %reduce-scatter.25.cloned.1.call-done = f32[96,1536]{1,0:T(8,128)} async-done(((f32[384,1536]{1,0:T(8,128)}), f32[96,1536]{1,0:T(8,128)}) %reduce-scatter.25.cloned.1.call-update) | async-done | bytes 589840 | tf_op jit(solution)/shard_map/reduce_scatter | solution.py:285
  372.3 35.4 %reduce-scatter.27.cloned.1.call-done = f32[384,384]{1,0:T(8,128)} async-done(((f32[1536,384]{1,0:T(8,128)}), f32[384,384]{1,0:T(8,128)}) %reduce-scatter.27.cloned.1.call-update) | async-done | bytes 589840 | tf_op jit(solution)/shard_map/reduce_scatter | solution.py:287
  407.7 35.2 %reduce-scatter.23.cloned.1.call-done = f32[96,1536]{1,0:T(8,128)} async-done(((f32[384,1536]{1,0:T(8,128)}), f32[96,1536]{1,0:T(8,128)}) %reduce-scatter.23.cloned.1.call-update) | async-done | bytes 589840 | tf_op jit(solution)/shard_map/reduce_scatter | solution.py:285
  442.9 42.8 %reduce-scatter.13.cloned.1.call-done = f32[96,2304]{1,0:T(8,128)} async-done(((f32[384,2304]{1,0:T(8,128)}), f32[96,2304]{1,0:T(8,128)}) %reduce-scatter.13.cloned.1.call-update) | async-done | bytes 884752 | tf_op jit(solution)/shard_map/reduce_scatter | solution.py:280
  485.7 42.8 %reduce-scatter.11.cloned.1.call-done = f32[96,2304]{1,0:T(8,128)} async-done(((f32[384,2304]{1,0:T(8,128)}), f32[96,2304]{1,0:T(8,128)}) %reduce-scatter.11.cloned.1.call-update) | async-done | bytes 884752 | tf_op jit(solution)/shard_map/reduce_scatter | solution.py:280
  530.8 10.6 %all-reduce.16 = (f32[2304]{0:T(1024)S(1)}, f32[2304]{0:T(1024)S(1)}, f32[384]{0:T(512)S(1)}, f32[384]{0:T(512)S(1)}, f32[1536]{0:T(1024)S(1)}, /*index=5*/f32[1536]{0:T(1024)S(1)}, f32[384]{0:T(512)S(1)}, f32[384]{0:T(512)S(1)}) all-reduce(f32[2304]{0:T(1024)S(1)} %reduce_sum.433, ...), channel_id=23, replica_groups=mesh['dp'=8,'fsdp'=4] {'fsdp'}, use_global_device_ids=true, to_apply=%region_42.43.clone | all-reduce | flops 9216 | bytes 73728
  542.1 39.4 %all-reduce.14 = (f32[1,576]{1,0:T(1,128)S(1)}, f32[1,576]{1,0:T(1,128)S(1)}, f32[1,96]{1,0:T(1,128)S(1)}, f32[1,96]{1,0:T(1,128)S(1)}, f32[1,384]{1,0:T(1,128)S...) all-reduce(f32[1,576]{1,0:T(1,128)S(1)} %stack.125, ...), channel_id=1, replica_groups=mesh['dp'=8,'fsdp'=4] {'dp'}, use_global_device_ids=true, to_apply=%region_43.44 | all-reduce | flops 2304 | bytes 18432 | tf_op jit(solution)/shard_map/psum | solution.py:290
  589.9 129.5 %all-reduce.20.cloned.1.call-done = (f32[1,96,2304]{2,1,0:T(8,128)}, f32[1,96,2304]{2,1,0:T(8,128)}, f32[1,96,1152]{2,1,0:T(8,128)}, f32[1,96,1152]{2,1,0:T(8,12...) async-done(((f32[1,96,2304]{2,1,0:T(8,128)}, ...) | async-done | bytes 5308432 | tf_op jit(solution)/shard_map/psum | solution.py:290
  (420 shorter events, 134.4 us)
Async XLA Ops:
  7.2 75.5 %all-gather.25.cloned.1.call-start = ((), (), s32[]{:S(2)}) async-start(), calls=%async_computation.20 | async-start | bytes 2211840 | tf_op jit(solution)/shard_map/all_gather | solution.py:241
  9.5 75.5 %all-gather.31.cloned.1.call-start = ((), (), s32[]{:S(2)}) async-start(), calls=%async_computation.23 | async-start | bytes 2211840 | tf_op jit(solution)/shard_map/all_gather | solution.py:241
  10.3 91.0 %all-gather.27.cloned.1.call-start = ((), (), s32[]{:S(2)}) async-start(), calls=%async_computation.21 | async-start | bytes 1474560 | tf_op jit(solution)/shard_map/all_gather | solution.py:246
  11.2 94.9 %all-gather.29.cloned.1.call-start = ((), (), s32[]{:S(2)}) async-start(), calls=%async_computation.22 | async-start | bytes 1474560 | tf_op jit(solution)/shard_map/all_gather | solution.py:248
  12.1 31.7 %copy-start.52 = (bf16[2,96,384]{2,1,0:T(8,128)(2,1)S(1)}, bf16[2,96,384]{2,1,0:T(8,128)(2,1)}, u32[]{:S(2)}) copy-start(bf16[2,96,384]{2,1,0:T(8,128)(2,1)} %param.20) | copy-start | bytes 442372
  12.2 119.1 %all-gather.33.cloned.1.call-start = ((), (), s32[]{:S(2)}) async-start(), calls=%async_computation.24 | async-start | bytes 1474560 | tf_op jit(solution)/shard_map/all_gather | solution.py:246
  12.8 127.8 %all-gather.35.cloned.1.call-start = ((), (), s32[]{:S(2)}) async-start(), calls=%async_computation.25 | async-start | bytes 1474560 | tf_op jit(solution)/shard_map/all_gather | solution.py:248
  13.3 272.2 %reduce-scatter.21.cloned.1.call-start = ((), (), s32[]{:S(2)}) async-start(), calls=%async_computation.15 | async-start | bytes 737280 | tf_op jit(solution)/shard_map/reduce_scatter | solution.py:283
  16.5 42.6 %copy-start.48 = (bf16[2,96,1152]{2,1,0:T(8,128)(2,1)S(1)}, bf16[2,96,1152]{2,1,0:T(8,128)(2,1)}, u32[]{:S(2)}) copy-start(bf16[2,96,1152]{2,1,0:T(8,128)(2,1)} %param.19) | copy-start | bytes 1327108
  16.7 70.7 %copy-start.66 = (f32[3,256]{1,0:T(4,128)}, f32[3,256]{1,0:T(4,128)S(1)}, u32[]{:S(2)}) copy-start(f32[3,256]{1,0:T(4,128)S(1)} %broadcast_multiply_fusion.11) | copy-start | bytes 9220
  17.1 70.4 %copy-start.82 = (f32[3,256]{1,0:T(4,128)}, f32[3,256]{1,0:T(4,128)S(1)}, u32[]{:S(2)}) copy-start(f32[3,256]{1,0:T(4,128)S(1)} %add_rsqrt_fusion.3) | copy-start | bytes 9220
  29.6 76.5 %copy-start.91 = (f32[1536]{0:T(1024)}, f32[1536]{0:T(1024)S(1)}, u32[]{:S(2)}) copy-start(f32[1536]{0:T(1024)S(1)} %convert_reduce_fusion.1) | copy-start | bytes 18436
  51.9 30.9 %copy-start.49 = (f32[3,384]{1,0:T(4,128)S(1)}, f32[3,384]{1,0:T(4,128)}, u32[]{:S(2)}) copy-start(f32[3,384]{1,0:T(4,128)} %param.14) | copy-start | bytes 13828
  59.1 40.1 %copy-start.19 = (bf16[1,384,384]{2,1,0:T(8,128)(2,1)}, bf16[1,384,384]{2,1,0:T(8,128)(2,1)S(1)}, u32[]{:S(2)}) copy-start(bf16[1,384,384]{2,1,0:T(8,128)(2,1)S(1)} %all-gather.3) | copy-start | bytes 884740
  84.9 14.3 %copy-start.59 = (f32[3,384]{1,0:T(4,128)}, f32[3,384]{1,0:T(4,128)S(1)}, u32[]{:S(2)}) copy-start(f32[3,384]{1,0:T(4,128)S(1)} %get-tuple-element.104) | copy-start | bytes 13828
  84.9 16.3 %copy-start.56 = (f32[3,384]{1,0:T(4,128)}, f32[3,384]{1,0:T(4,128)S(1)}, u32[]{:S(2)}) copy-start(f32[3,384]{1,0:T(4,128)S(1)} %get-tuple-element.101) | copy-start | bytes 13828
  84.9 16.3 %copy-start.61 = (f32[3,384]{1,0:T(4,128)}, f32[3,384]{1,0:T(4,128)S(1)}, u32[]{:S(2)}) copy-start(f32[3,384]{1,0:T(4,128)S(1)} %get-tuple-element.100) | copy-start | bytes 13828
  84.9 21.2 %copy-start.74 = (f32[3,384]{1,0:T(4,128)}, f32[3,384]{1,0:T(4,128)S(1)}, u32[]{:S(2)}) copy-start(f32[3,384]{1,0:T(4,128)S(1)} %get-tuple-element.99) | copy-start | bytes 13828
  87.4 24.8 %copy-start.76 = (f32[3,384]{1,0:T(4,128)}, f32[3,384]{1,0:T(4,128)S(1)}, u32[]{:S(2)}) copy-start(f32[3,384]{1,0:T(4,128)S(1)} %get-tuple-element.97) | copy-start | bytes 13828
  87.4 24.8 %copy-start.99 = (f32[3,384]{1,0:T(4,128)}, f32[3,384]{1,0:T(4,128)S(1)}, u32[]{:S(2)}) copy-start(f32[3,384]{1,0:T(4,128)S(1)} %get-tuple-element.96) | copy-start | bytes 13828
  140.6 9.9 %copy-start.117 = (bf16[1,1536,384]{2,1,0:T(8,128)(2,1)S(1)}, bf16[1,1536,384]{2,1,0:T(8,128)(2,1)}, u32[]{:S(2)}) copy-start(bf16[1,1536,384]{2,1,0:T(8,128)(2,1)} %all-gather.35.cloned.1.call-done) | copy-start | bytes 3538948
  191.5 94.2 %reduce-scatter.19.cloned.1.call-start = ((), (), s32[]{:S(2)}) async-start(), calls=%async_computation.14 | async-start | bytes 737280 | tf_op jit(solution)/shard_map/reduce_scatter | solution.py:283
  211.3 74.3 %reduce-scatter.17.cloned.1.call-start = ((), (), s32[]{:S(2)}) async-start(), calls=%async_computation.13 | async-start | bytes 2211840 | tf_op jit(solution)/shard_map/reduce_scatter | solution.py:282
  215.7 85.9 %reduce-scatter.15.cloned.1.call-start = ((), (), s32[]{:S(2)}) async-start(), calls=%async_computation.12 | async-start | bytes 2211840 | tf_op jit(solution)/shard_map/reduce_scatter | solution.py:282
  250.7 86.3 %reduce-scatter.29.cloned.1.call-start = ((), (), s32[]{:S(2)}) async-start(), calls=%async_computation.19 | async-start | bytes 2949120 | tf_op jit(solution)/shard_map/reduce_scatter | solution.py:287
  257.3 115.0 %reduce-scatter.25.cloned.1.call-start = ((), (), s32[]{:S(2)}) async-start(), calls=%async_computation.17 | async-start | bytes 2949120 | tf_op jit(solution)/shard_map/reduce_scatter | solution.py:285
  261.8 145.9 %reduce-scatter.27.cloned.1.call-start = ((), (), s32[]{:S(2)}) async-start(), calls=%async_computation.18 | async-start | bytes 2949120 | tf_op jit(solution)/shard_map/reduce_scatter | solution.py:287
  269.3 173.6 %reduce-scatter.23.cloned.1.call-start = ((), (), s32[]{:S(2)}) async-start(), calls=%async_computation.16 | async-start | bytes 2949120 | tf_op jit(solution)/shard_map/reduce_scatter | solution.py:285
  274.5 211.3 %reduce-scatter.13.cloned.1.call-start = ((), (), s32[]{:S(2)}) async-start(), calls=%async_computation.11 | async-start | bytes 4423680 | tf_op jit(solution)/shard_map/reduce_scatter | solution.py:280
  277.7 250.9 %reduce-scatter.11.cloned.1.call-start = ((), (), s32[]{:S(2)}) async-start(), calls=%async_computation.10 | async-start | bytes 4423680 | tf_op jit(solution)/shard_map/reduce_scatter | solution.py:280
  285.5 433.9 %all-reduce.20.cloned.1.call-start = ((), (), s32[]{:S(2)}) async-start(), calls=%async_computation.26 | async-start | bytes 10616832 | tf_op jit(solution)/shard_map/psum | solution.py:290
  528.6 57.3 %copy-start.7 = (bf16[1,384,2304]{2,1,0:T(8,128)(2,1)S(1)}, bf16[1,384,2304]{2,1,0:T(8,128)(2,1)}, u32[]{:S(2)}) copy-start(bf16[1,384,2304]{2,1,0:T(8,128)(2,1)} %all-gather.25.cloned.1.call-done) | copy-start | bytes 5308420
  (106 other events, 314.5 us)
Sparse Core Ops, SparseCore 0:
  10.1 23.4 all-gather.24
  35.8 23.4 all-gather.30
  61.5 21.2 all-gather.26
  84.8 17.4 all-gather.28
  103.6 17.4 all-gather.32
  123.1 17.4 all-gather.34
  191.6 22.0 reduce-scatter.20
  216.2 22.0 reduce-scatter.18
  240.8 29.1 reduce-scatter.16
  272.5 29.1 reduce-scatter.14
  304.2 32.8 reduce-scatter.28
  339.4 32.8 reduce-scatter.24
  374.8 32.8 reduce-scatter.26
  410.1 32.8 reduce-scatter.22
  445.3 40.3 reduce-scatter.12
  488.1 40.3 reduce-scatter.10
  533.2 186.1 all-reduce.19
where the time goes:
time: 738 us; the launch traced here: 733 us
  waiting for transfers between devices  379 us (51%)
  matrix products  156 us (21%)
  blocking collectives  112 us (15%)
  local copies, waits for them, and re-layouts  36.4 us (5%)
  other arithmetic  29 us (4%)
  between operations  19.3 us (3%)
    psum x1, waiting for transfers between devices, reduce_layer(): lax.psum((shards[0], shards[1], shards[2], shards[3], shards[4], shards[5...  129 us
    reduce_scatter x2, waiting for transfers between devices, reduce_layer(): lax.psum_scatter(grads[0], 'fsdp', scatter_dimension=0, tiled=True)  85.7 us
    reduce_scatter x2, waiting for transfers between devices, reduce_layer(): lax.psum_scatter(grads[7], 'fsdp', scatter_dimension=0, tiled=True)  70.8 us
    reduce_scatter x2, waiting for transfers between devices, reduce_layer(): lax.psum_scatter(grads[5], 'fsdp', scatter_dimension=0, tiled=True)  70.5 us
    dot_general x12, matrix products, einsum_mixed(): return jnp.einsum(form, left, right, preferred_element_type=jnp.float32)  57.6 us
    psum x1, blocking collectives, reduce_layer(): lax.psum((shards[0], shards[1], shards[2], shards[3], shards[4], shards[5...  39.4 us
    dot_general x8, matrix products, outer_total(): jnp.dot(left.reshape(-1, left.shape[-1]).T, right.reshape(-1, right.shape...  31.1 us
    dot_general x8, matrix products, matmul_last(): jnp.dot(flat, right, preferred_element_type=jnp.float32)  28.2 us
  transfers between devices with their start and end apart: 17, of which 9 were waited for; matrix products, arithmetic and copies ran while one was open for 20% of the time, Pallas kernels for 0%

commit v1 on v0

--- a/solution.py
+++ b/solution.py
@@ -1,3 +1,5 @@
+import functools
+
 import jax
 import jax.numpy as jnp
 from jax import lax
@@ -100,23 +102,9 @@
     return joined.reshape(qkv.shape).astype(jnp.bfloat16)
 
 
-def layer_parts(resid, cond, weights):
-    (
-        ada_weight,
-        ada_bias,
-        qkv_weight,
-        proj_weight,
-        proj_bias,
-        up_weight,
-        up_bias,
-        down_weight,
-        down_bias,
-    ) = weights
+def layer_parts(resid, ada, weights):
+    qkv_weight, proj_weight, proj_bias, up_weight, up_bias, down_weight, down_bias = weights
     width = resid.shape[-1]
-    act_low = jax.nn.silu(cond).astype(jnp.bfloat16)
-    ada = jnp.dot(act_low, ada_weight, preferred_element_type=jnp.float32) + ada_bias.astype(
-        jnp.float32
-    )
     mods = [ada[:, None, piece_idx * width : (piece_idx + 1) * width] for piece_idx in range(6)]
     normed_one, inv_one = norm_rows(resid)
     attn_in = (normed_one * (1.0 + mods[1]) + mods[0]).astype(jnp.bfloat16)
@@ -131,7 +119,6 @@
     branch = matmul_last(hidden, down_weight) + down_bias.astype(jnp.float32)
     result = resid_one + mods[5] * branch
     return dict(
-        act_low=act_low,
         mods=mods,
         normed_one=normed_one,
         inv_one=inv_one,
@@ -151,19 +138,8 @@
     )
 
 
-def layer_backward(resid, cond, weights, grad_out):
-    (
-        ada_weight,
-        ada_bias,
-        qkv_weight,
-        proj_weight,
-        proj_bias,
-        up_weight,
-        up_bias,
-        down_weight,
-        down_bias,
-    ) = weights
-    saved = layer_parts(resid, cond, weights)
+def layer_backward(saved, weights, grad_out):
+    qkv_weight, proj_weight, proj_bias, up_weight, up_bias, down_weight, down_bias = weights
     mods = saved["mods"]
     grad_gate_two = jnp.sum(grad_out * saved["branch"], axis=1)
     grad_branch = grad_out * mods[5]
@@ -205,105 +181,99 @@
         ],
         axis=-1,
     )
-    grad_ada_bias = jnp.sum(grad_ada, axis=0)
-    ada_low = grad_ada.astype(jnp.bfloat16)
-    grad_ada_weight = jnp.dot(saved["act_low"].T, ada_low, preferred_element_type=jnp.float32)
-    grad_cond = jnp.dot(ada_low, ada_weight.T, preferred_element_type=jnp.float32) * silu_slope(
-        cond
-    )
-    grads = (
-        grad_ada_weight,
-        grad_ada_bias,
-        grad_qkv_weight,
-        grad_proj_weight,
-        grad_proj_bias,
-        grad_up_weight,
-        grad_up_bias,
-        grad_down_weight,
-        grad_down_bias,
-    )
-    return (grad_resid, grad_cond, grads)
-
-
-def gather_forward(stacks, layer_idx):
-    (
-        ada_weight,
-        ada_bias,
-        qkv_weight,
-        proj_weight,
-        proj_bias,
-        up_weight,
-        up_bias,
-        down_weight,
-        down_bias,
-    ) = stacks
-    return (
-        lax.all_gather(ada_weight[layer_idx], "fsdp", axis=0, tiled=True),
-        lax.all_gather(ada_bias[layer_idx], "fsdp", axis=0, tiled=True),
-        lax.all_gather(qkv_weight[layer_idx], "fsdp", axis=0, tiled=True),
-        lax.all_gather(proj_weight[layer_idx], "fsdp", axis=0, tiled=True),
-        lax.all_gather(proj_bias[layer_idx], "fsdp", axis=0, tiled=True),
-        lax.all_gather(up_weight[layer_idx], "fsdp", axis=0, tiled=True),
-        lax.all_gather(up_bias[layer_idx], "fsdp", axis=0, tiled=True),
-        lax.all_gather(down_weight[layer_idx], "fsdp", axis=0, tiled=True),
-        lax.all_gather(down_bias[layer_idx], "fsdp", axis=0, tiled=True),
-    )
-
-
-def gather_backward(stacks, layer_idx):
-    (
-        ada_weight,
-        ada_bias,
-        qkv_weight,
-        proj_weight,
-        proj_bias,
-        up_weight,
-        up_bias,
-        down_weight,
-        down_bias,
-    ) = stacks
-    return (
-        lax.all_gather(ada_weight[layer_idx], "fsdp", axis=0, tiled=True),
-        lax.all_gather(ada_bias[layer_idx], "fsdp", axis=0, tiled=True),
-        lax.all_gather(qkv_weight[layer_idx], "fsdp", axis=0, tiled=True),
-        lax.all_gather(proj_weight[layer_idx], "fsdp", axis=0, tiled=True),
-        lax.all_gather(proj_bias[layer_idx], "fsdp", axis=0, tiled=True),
-        lax.all_gather(up_weight[layer_idx], "fsdp", axis=0, tiled=True),
-        lax.all_gather(up_bias[layer_idx], "fsdp", axis=0, tiled=True),
-        lax.all_gather(down_weight[layer_idx], "fsdp", axis=0, tiled=True),
-        lax.all_gather(down_bias[layer_idx], "fsdp", axis=0, tiled=True),
-    )
-
-
-def reduce_layer(grads):
-    shards = (
-        lax.psum_scatter(grads[0], "fsdp", scatter_dimension=0, tiled=True),
-        lax.psum_scatter(grads[1], "fsdp", scatter_dimension=0, tiled=True),
-        lax.psum_scatter(grads[2], "fsdp", scatter_dimension=0, tiled=True),
-        lax.psum_scatter(grads[3], "fsdp", scatter_dimension=0, tiled=True),
-        lax.psum_scatter(grads[4], "fsdp", scatter_dimension=0, tiled=True),
-        lax.psum_scatter(grads[5], "fsdp", scatter_dimension=0, tiled=True),
-        lax.psum_scatter(grads[6], "fsdp", scatter_dimension=0, tiled=True),
-        lax.psum_scatter(grads[7], "fsdp", scatter_dimension=0, tiled=True),
-        lax.psum_scatter(grads[8], "fsdp", scatter_dimension=0, tiled=True),
-    )
-    return lax.psum(
-        (
-            shards[0],
-            shards[1],
-            shards[2],
-            shards[3],
-            shards[4],
-            shards[5],
-            shards[6],
-            shards[7],
-            shards[8],
-        ),
-        "dp",
-    )
+    bias_row = jnp.concatenate([grad_proj_bias, grad_up_bias, grad_down_bias])
+    wide = (grad_qkv_weight, grad_proj_weight, grad_up_weight, grad_down_weight)
+    return grad_resid, grad_ada, bias_row, wide
+
+
+def bits_of(size):
+    assert size & (size - 1) == 0
+    return [1 << k for k in range(size.bit_length() - 1)]
+
+
+def swap(value, axis, size, bit):
+    return lax.ppermute(value, axis, [(i, i ^ bit) for i in range(size)])
+
+
+def has_bit(axis, bit):
+    return (lax.axis_index(axis) & bit) != 0
+
+
+def gather_rel(value, axis, size):
+    pieces = {0: value}
+    for bit in reversed(bits_of(size)):
+        for j in list(pieces):
+            pieces[j ^ bit] = swap(pieces[j], axis, size, bit)
+    return [pieces[j] for j in range(size)]
+
+
+def to_absolute(pieces, axis):
+    me = lax.axis_index(axis)
+    out = jnp.zeros((len(pieces),) + pieces[0].shape, pieces[0].dtype)
+    for j, piece in enumerate(pieces):
+        out = lax.dynamic_update_index_in_dim(out, piece, me ^ j, 0)
+    return out
+
+
+def scatter_sum(blocks, axis, size, wire):
+    blocks = dict(enumerate(blocks))
+    for bit in bits_of(size):
+        keep = [j for j in blocks if not j & bit]
+        sent = jnp.concatenate([blocks[j | bit].astype(wire) for j in keep], axis=0)
+        got = swap(sent, axis, size, bit)
+        rows = got.shape[0] // len(keep)
+        blocks = {
+            j: blocks[j].astype(jnp.float32) + got[n * rows : (n + 1) * rows].astype(jnp.float32)
+            for n, j in enumerate(keep)
+        }
+    return blocks[0]
+
+
+def all_sum(value, axis, size, wire):
+    bits = bits_of(size)
+    trail = []
+    for n, bit in enumerate(bits):
+        width = value.shape[-1]
+        if n < len(bits) - 1 and (width // 2) % 128 == 0:
+            low, high = value[:, : width // 2], value[:, width // 2 :]
+            upper = has_bit(axis, bit)
+            sent = jnp.where(upper, low, high).astype(wire)
+            kept = jnp.where(upper, high, low)
+            value = kept.astype(jnp.float32) + swap(sent, axis, size, bit).astype(jnp.float32)
+            trail.append(bit)
+        else:
+            low = value.astype(wire)
+            value = low.astype(jnp.float32) + swap(low, axis, size, bit).astype(jnp.float32)
+    if not trail:
+        return value
+    value = value.astype(wire)
+    for bit in reversed(trail):
+        other = swap(value, axis, size, bit)
+        upper = has_bit(axis, bit)
+        value = jnp.concatenate(
+            [jnp.where(upper, other, value), jnp.where(upper, value, other)], axis=-1
+        )
+    return value.astype(jnp.float32)
+
+
+def gather_all(value, stages):
+    for axis, size, bit in stages:
+        other = swap(value, axis, size, bit)
+        upper = has_bit(axis, bit)
+        value = jnp.concatenate(
+            [jnp.where(upper, other, value), jnp.where(upper, value, other)], axis=0
+        )
+    return value
+
+
+def pack_rows(qkv, proj, up, down):
+    rows = qkv.shape[0]
+    blocks = [down[n * rows : (n + 1) * rows] for n in range(down.shape[0] // rows)]
+    return jnp.concatenate([qkv, proj, up] + blocks, axis=1)
 
 
 def on_device(
+    sizes,
     latents,
     conditioning,
     seq_counts,
@@ -318,55 +288,146 @@
     down_weight,
     down_bias,
 ):
-    stacks = (
-        ada_weight,
-        ada_bias,
-        qkv_weight,
-        proj_weight,
-        proj_bias,
-        up_weight,
-        up_bias,
-        down_weight,
-        down_bias,
-    )
-    seq_slots = latents.shape[0]
-    live = (jnp.arange(seq_slots, dtype=jnp.int32) < seq_counts[0]).astype(jnp.float32)[
-        :, None, None
+    groups, shards = sizes
+    bf16, f32 = jnp.bfloat16, jnp.float32
+    slots, _, width = latents.shape
+    rows = qkv_weight.shape[1]
+    triple, inner = qkv_weight.shape[2], up_weight.shape[2]
+    wide = ada_weight.shape[2]
+    ratio = inner // width
+    me = lax.axis_index("fsdp")
+
+    packs = [
+        pack_rows(qkv_weight[n], proj_weight[n], up_weight[n], down_weight[n])
+        for n in range(LAYERS)
     ]
-    inputs = []
-    gathered = []
+    fulls = []
+    for n in range(LAYERS):
+        full = to_absolute(gather_rel(packs[n], "fsdp", shards), "fsdp")
+        edge = [0, triple, triple + width, triple + width + inner]
+        down_full = full[:, :, edge[3] :].reshape(shards, rows, ratio, width)
+        fulls.append(
+            (
+                full[:, :, : edge[1]].reshape(width, triple),
+                full[:, :, edge[1] : edge[2]].reshape(width, width),
+                full[:, :, edge[2] : edge[3]].reshape(width, inner),
+                down_full.transpose(0, 2, 1, 3).reshape(inner, width),
+            )
+        )
+
+    act = jax.nn.silu(conditioning).astype(bf16)
+    shard_bias = jnp.concatenate([ada_bias, proj_bias, up_bias, down_bias], axis=1)
+    bias_width = shard_bias.shape[1]
+    small = jnp.concatenate([act.reshape(-1), shard_bias.reshape(-1)])
+    small = to_absolute(gather_rel(small, "fsdp", shards), "fsdp")
+    act_group = small[:, : slots * width].reshape(shards * slots, width)
+    biases = small[:, slots * width :].reshape(shards, LAYERS, bias_width)
+    act_cols = lax.dynamic_slice(act_group, (0, me * rows), (shards * slots, rows))
+    partial = jnp.stack(
+        [jnp.dot(act_cols, ada_weight[n], preferred_element_type=f32) for n in range(LAYERS)]
+    ).reshape(LAYERS, shards, slots, wide)
+    blocks = [
+        lax.dynamic_index_in_dim(partial, me ^ j, 1, keepdims=False).reshape(LAYERS * slots, wide)
+        for j in range(shards)
+    ]
+    ada = scatter_sum(blocks, "fsdp", shards, f32).reshape(LAYERS, slots, wide)
+    cut = [0]
+    for part in (ada_bias, proj_bias, up_bias, down_bias):
+        cut.append(cut[-1] + part.shape[1])
+    bias_of = [
+        [biases[:, n, cut[k] : cut[k + 1]].reshape(-1).astype(f32) for k in range(4)]
+        for n in range(LAYERS)
+    ]
+
+    live = (jnp.arange(slots, dtype=jnp.int32) < seq_counts[0]).astype(f32)[:, None, None]
+    saved, weights = [], []
     current = latents
-    for layer_idx in range(LAYERS):
-        weights = gather_forward(stacks, layer_idx)
-        gathered.append(weights)
-        inputs.append(current)
-        current = layer_parts(current, conditioning, weights)["result"]
+    for n in range(LAYERS):
+        qkv_full, proj_full, up_full, down_full = fulls[n]
+        ada_b, proj_b, up_b, down_b = bias_of[n]
+        weights.append((qkv_full, proj_full, proj_b, up_full, up_b, down_full, down_b))
+        saved.append(layer_parts(current, ada[n] + ada_b, weights[n]))
+        current = saved[n]["result"]
     block_out = current * live
     grad = cotangent * live
-    grad_cond = jnp.zeros(conditioning.shape, jnp.float32)
-    layer_grads = [None] * LAYERS
-    for layer_idx in reversed(range(LAYERS)):
-        weights = gather_backward(stacks, layer_idx)
-        grad, cond_part, grads = layer_backward(inputs[layer_idx], conditioning, weights, grad)
-        grad_cond = grad_cond + cond_part
-        layer_grads[layer_idx] = reduce_layer(grads)
-    finals = [
-        jnp.stack([layer_grads[layer_idx][piece_idx] for layer_idx in range(LAYERS)], axis=0)
-        for piece_idx in range(9)
-    ]
+
+    stages = [("dp", groups, bit) for bit in reversed(bits_of(groups))]
+    stages += [("fsdp", shards, bit) for bit in reversed(bits_of(shards))]
+    sums, gads, bias_rows = [None] * LAYERS, [None] * LAYERS, [None] * LAYERS
+    acts = None
+    for n in reversed(range(LAYERS)):
+        grad, grad_ada, bias_row, (g_qkv, g_proj, g_up, g_down) = layer_backward(
+            saved[n], weights[n], grad
+        )
+        down_rows = g_down.reshape(shards, ratio * rows, width)
+        terms = []
+        for j in range(shards):
+            own = me ^ j
+            terms.append(
+                pack_rows(
+                    lax.dynamic_slice_in_dim(g_qkv, own * rows, rows, 0),
+                    lax.dynamic_slice_in_dim(g_proj, own * rows, rows, 0),
+                    lax.dynamic_slice_in_dim(g_up, own * rows, rows, 0),
+                    lax.dynamic_index_in_dim(down_rows, own, 0, keepdims=False),
+                ).astype(bf16)
+            )
+        shard = scatter_sum(terms, "fsdp", shards, bf16)
+        sums[n] = all_sum(shard, "dp", groups, bf16)
+        rows_out = [grad_ada.astype(bf16), bias_row[None].astype(bf16)]
+        if acts is None:
+            flat = act.reshape(-1)
+            flat = jnp.pad(flat, (0, -flat.shape[0] % wide)).reshape(-1, wide)
+            rows_out.append(flat)
+        message = jnp.concatenate(rows_out, axis=0)
+        every = gather_all(message[None], stages)
+        gads[n] = every[:, :slots]
+        bias_rows[n] = every[:, slots]
+        if acts is None:
+            acts = every[:, slots + 1 :].reshape(every.shape[0], -1)[:, : slots * width]
+            acts = acts.reshape(-1, width)
+
+    acts_cols = lax.dynamic_slice(acts, (0, me * rows), (acts.shape[0], rows))
+    g_ada = jnp.stack(
+        [outer_total(acts_cols, gads[n].reshape(-1, wide)) for n in range(LAYERS)]
+    )
+    g_ada_bias = jnp.stack([jnp.sum(gads[n].astype(f32), axis=(0, 1)) for n in range(LAYERS)])
+    g_bias = jnp.stack([jnp.sum(bias_rows[n].astype(f32), axis=0) for n in range(LAYERS)])
+
+    place = jnp.int32(0)
+    for k, bit in enumerate(reversed(bits_of(groups))):
+        place = place + has_bit("dp", bit).astype(jnp.int32) * (1 << k)
+    total = 0.0
+    for n in range(LAYERS):
+        grid = gads[n].reshape(shards, groups, slots, wide)
+        mine = lax.dynamic_index_in_dim(grid, place, 1, keepdims=False).reshape(-1, wide)
+        total = total + matmul_back(mine, ada_weight[n])
+    total = total.reshape([2] * len(bits_of(shards)) + [slots, rows])
+    order = tuple(reversed(range(len(bits_of(shards)))))
+    total = total.transpose(order + (len(order), len(order) + 1)).reshape(shards, slots, rows)
+    got = [lax.dynamic_index_in_dim(total, me, 0, keepdims=False)]
+    for j in range(1, shards):
+        sent = lax.dynamic_index_in_dim(total, me ^ j, 0, keepdims=False)
+        got.append(swap(sent, "fsdp", shards, j))
+    grad_cond = to_absolute(got, "fsdp").transpose(1, 0, 2).reshape(slots, width)
+    grad_cond = grad_cond * silu_slope(conditioning)
+
+    wide_sum = jnp.stack(sums)
+    edge = [0, triple, triple + width, triple + width + inner]
+    down_sum = wide_sum[:, :, edge[3] :].reshape(LAYERS, rows, ratio, width)
+    own_inner = inner // shards
     return (
         block_out,
         grad,
         grad_cond,
-        finals[0],
-        finals[1],
-        finals[2],
-        finals[3],
-        finals[4],
-        finals[5],
-        finals[6],
-        finals[7],
-        finals[8],
+        g_ada,
+        lax.dynamic_slice_in_dim(g_ada_bias, me * (wide // shards), wide // shards, 1),
+        wide_sum[:, :, : edge[1]],
+        wide_sum[:, :, edge[1] : edge[2]],
+        lax.dynamic_slice_in_dim(g_bias, me * rows, rows, 1),
+        wide_sum[:, :, edge[2] : edge[3]],
+        lax.dynamic_slice_in_dim(g_bias, width + me * own_inner, own_inner, 1),
+        down_sum.transpose(0, 2, 1, 3).reshape(LAYERS, ratio * rows, width),
+        lax.dynamic_slice_in_dim(g_bias, width + inner + me * rows, rows, 1),
     )
 
 
@@ -401,5 +462,5 @@
         P(None, "fsdp"),
     )
     return jax.shard_map(
-        on_device, mesh=mesh, in_specs=in_specs, out_specs=out_specs, check_vma=False
-    )
+        functools.partial(on_device, (mesh.shape["dp"], mesh.shape["fsdp"])), mesh=mesh, in_specs=in_specs, out_specs=out_specs, check_vma=False
+    )

time: 738 us -> 391 us (0.53)
  waiting for transfers between devices: 379 us -> 121 us
  blocking collectives: 112 us -> 0 us
  matrix products: 156 us -> 113 us
  local copies, waits for them, and re-layouts: 36.4 us -> 77 us
  starting transfers between devices: 1.33 us -> 33.1 us
  between operations: 19.3 us -> 3.93 us
  other arithmetic: 29 us -> 38.2 us
    reduce_scatter x10 -> x0, waiting for transfers between devices: 243 us -> none  [the longest x2 85.7 us: reduce_layer(): lax.psum_scatter(grads[0], 'fsdp', scatter_dimension=0, tiled=True)]
    psum x1 -> x0, waiting for transfers between devices: 129 us -> none  [reduce_layer(): lax.psum((shards[0], shards[1], shards[2], shards[3], shards[4], shards[5...]
    ppermute x0 -> x38, waiting for transfers between devices: none -> 121 us  [swap(): return lax.ppermute(value, axis, [(i, i ^ bit) for i in range(size)])]
    all_gather x6 -> x0, blocking collectives: 50.7 us -> none  [the longest x2 23.6 us: gather_forward(): lax.all_gather(qkv_weight[layer_idx], 'fsdp', axis=0, tiled=True)]
    psum x1 -> x0, blocking collectives: 39.4 us -> none  [reduce_layer(): lax.psum((shards[0], shards[1], shards[2], shards[3], shards[4], shards[5...]
    ppermute x0 -> x38, starting transfers between devices: none -> 33.1 us  [swap(): return lax.ppermute(value, axis, [(i, i ^ bit) for i in range(size)])]
    unnamed x2 -> x0, blocking collectives: 22.3 us -> none
    dot_general x8 -> x10, matrix products: 31.1 us -> 14.5 us  [outer_total(): jnp.dot(left.reshape(-1, left.shape[-1]).T, right.reshape(-1, right.shape...]
  transfers between devices with their start and end apart: 17 -> 38, of which waited for: 9 -> 19; matrix products, arithmetic and copies ran while one was open for 20% -> 14% of each run, Pallas kernels for 0% -> 0%
where the time goes in v1:
time: 391 us; the launch traced here: 387 us
  waiting for transfers between devices  121 us (31%)
  matrix products  113 us (29%)
  local copies, waits for them, and re-layouts  77 us (20%)
  other arithmetic  38.2 us (10%)
  starting transfers between devices  33.1 us (8%)
  between operations  3.93 us (1%)
    ppermute x38, waiting for transfers between devices, swap(): return lax.ppermute(value, axis, [(i, i ^ bit) for i in range(size)])  121 us
    dot_general x12, matrix products, einsum_mixed(): return jnp.einsum(form, left, right, preferred_element_type=jnp.float32)  57.4 us
    ppermute x38, starting transfers between devices, swap(): return lax.ppermute(value, axis, [(i, i ^ bit) for i in range(size)])  33.1 us
    unnamed x313, local copies, waits for them, and re-layouts  26.6 us
    dot_general x10, matrix products, matmul_back(): jnp.dot(flat, right.T, preferred_element_type=jnp.float32)  22 us
    dot_general x8, matrix products, matmul_last(): jnp.dot(flat, right, preferred_element_type=jnp.float32)  19.1 us
    dot_general x10, matrix products, outer_total(): jnp.dot(left.reshape(-1, left.shape[-1]).T, right.reshape(-1, right.shape...  14.5 us
    dynamic_update_slice x16, local copies, waits for them, and re-layouts, to_absolute(): out = lax.dynamic_update_index_in_dim(out, piece, me ^ j, 0)  9.58 us
  transfers between devices with their start and end apart: 38, of which 19 were waited for; matrix products, arithmetic and copies ran while one was open for 14% of the time, Pallas kernels for 0%

profile of v1, /device:TPU:0, one launch (start us, length us, event | category | flops | bytes accessed | tf_op | source)
XLA Modules:
  0.0 387.0 jit_solution(1299340661126383311)
XLA Ops:
  31.6 24.9 %collective-permute-done.4 = f32[6,2304]{1,0:T(8,128)S(1)} collective-permute-done((f32[6,2304]{1,0:T(8,128)S(1)}, f32[6,2304]{1,0:T(8,128)S(1)}, u32[]{:S(2)}, u32[]{:S(2)}) %collective-permute-start.4) | collective-permute-done | bytes 55328 | tf_op jit(solution)/shard_map/ppermute | solution.py:195
  77.7 3.6 fusion.151
  86.5 3.9 %multiply_convert_fusion.3 = (bf16[3,256,1536]{2,1,0:T(8,128)(2,1)S(1)}, f32[3,256,1536]{2,1,0:T(8,128)}) fusion(f32[1536]{0:T(1024)S(1)} %copy-done.98, bf16[384,1536,1]{1,0,2:T(8,128)(2,1)S(1)} %bitcast.478, f32[3,256,384]{2,1,0:T(8,128)S(1)} %get-tuple-element.60, f32[3,384]{1,0:T(4,128)S(1)} %copy-done.86, f32[3,384]{1,0:T(4,128)S(1)} %copy-done.71, ...), kind=kOutput, calls=%fused_computation.28 | convolution fusion | flops 919240704 | bytes 9458688 | tf_op jit(solution)/shard_map/dot_general | solution.py:23
  96.4 3.9 %copy.154 = bf16[3,256,1152]{1,2,0:T(8,128)(2,1)} copy(bf16[3,256,1152]{2,1,0:T(8,128)(2,1)} %convolution_convert_fusion) | data formatting | bytes 3538944 | tf_op jit(solution)/shard_map/convert_element_type | solution.py:111
  102.4 3.8 fusion.152
  113.8 3.2 multiply_reduce_fusion.4
  117.0 4.8 %fusion.154 = (bf16[1536]{0:T(1024)(128)(2,1)}, bf16[3,256,1536]{2,1,0:T(8,128)(2,1)S(1)}) fusion(f32[3,256,1536]{2,1,0:T(8,128)S(1)} %get-tuple-element.173, f32[1536]{0:T(1024)S(1)} %copy-done.100, bf16[3,256,384]{2,1,0:T(8,128)(2,1)S(1)} %get-tuple-element.67, bf16[1536,384,1]{1,0,2:T(8,128)(2,1)S(1)} %bitcast.477), kind=kOutput, calls=%fused_computation.490 | convolution fusion | flops 930740736 | bytes 8856576 | tf_op jit(solution)/shard_map/dot_general | solution.py:30
  130.6 4.2 %fusion.71 = f32[3,6,256,256]{2,3,1,0:T(8,128)} fusion(bf16[3,256,6,64]{1,3,2,0:T(8,128)(2,1)} %bitcast.455, bf16[3,256,3,6,64]{1,4,3,2,0:T(8,128)(2,1)} %bitcast.439), kind=kOutput, calls=%fused_computation.184 | convolution fusion | flops 150994944 | bytes 5898240 | tf_op jit(solution)/shard_map/sqhd,skhd->shqk/dot_general | solution.py:18
  134.8 9.2 %fusion.52 = bf16[3,256,1,6,64]{1,4,3,0,2:T(8,128)(2,1)} fusion(f32[3,6,256,256]{2,3,1,0:T(8,128)} %fusion.71, bf16[3,256,3,6,64]{1,4,3,2,0:T(8,128)(2,1)} %bitcast.440, f32[3,6,256,256]{2,3,1,0:T(8,128)} %copy-done.15, f32[3,6,256]{2,1,0:T(8,128)} %copy-done.85), kind=kOutput, calls=%fused_computation.70 | convolution fusion | flops 159257344 | bytes 20103168 | tf_op jit(solution)/shard_map/shqk,skhd->sqhd/dot_general | solution.py:18
  144.0 9.2 %fusion.55 = bf16[3,256,1,6,64]{1,4,3,0,2:T(8,128)(2,1)} fusion(f32[3,6,256,256]{2,3,1,0:T(8,128)} %fusion.71, bf16[3,256,3,6,64]{1,4,3,2,0:T(8,128)(2,1)} %bitcast.441, f32[3,6,256,256]{2,3,1,0:T(8,128)} %copy-done.15, f32[3,6,256]{2,1,0:T(8,128)} %copy-done.85), kind=kOutput, calls=%fused_computation.71 | convolution fusion | flops 159257344 | bytes 20103168 | tf_op jit(solution)/shard_map/shqk,sqhd->skhd/dot_general | solution.py:18
  153.3 3.5 convolution_bitcast_fusion.9
  168.1 4.5 %fusion.153 = (bf16[1536]{0:T(1024)(128)(2,1)}, bf16[3,256,1536]{2,1,0:T(8,128)(2,1)S(1)}) fusion(f32[3,256,1536]{2,1,0:T(8,128)S(1)} %bitcast.499, f32[1536]{0:T(1024)S(1)} %copy-done.99, bf16[3,256,384]{2,1,0:T(8,128)(2,1)S(1)} %multiply_convert_fusion.5, bf16[1536,384,1]{1,0,2:T(8,128)(2,1)S(1)} %bitcast.474), kind=kOutput, calls=%fused_computation.489 | convolution fusion | flops 930740736 | bytes 8856576 | tf_op jit(solution)/shard_map/dot_general | solution.py:30
  181.9 4.1 %fusion.69 = f32[3,6,256,256]{2,3,1,0:T(8,128)} fusion(bf16[3,256,6,64]{1,3,2,0:T(8,128)(2,1)S(1)} %bitcast.457, bf16[3,256,3,6,64]{1,4,3,2,0:T(8,128)(2,1)} %bitcast.434), kind=kOutput, calls=%fused_computation.182 | convolution fusion | flops 150994944 | bytes 5898240 | tf_op jit(solution)/shard_map/sqhd,skhd->shqk/dot_general | solution.py:18
  185.9 9.1 %fusion.46 = bf16[3,256,1,6,64]{1,4,3,0,2:T(8,128)(2,1)} fusion(f32[3,6,256,256]{2,3,1,0:T(8,128)} %fusion.69, bf16[3,256,3,6,64]{1,4,3,2,0:T(8,128)(2,1)} %bitcast.435, f32[3,6,256,256]{2,3,1,0:T(8,128)} %copy-done.14, f32[3,6,256]{2,1,0:T(8,128)} %copy-done.84), kind=kOutput, calls=%fused_computation.68 | convolution fusion | flops 159257344 | bytes 20103168 | tf_op jit(solution)/shard_map/shqk,skhd->sqhd/dot_general | solution.py:18
  195.1 9.2 %fusion.49 = bf16[3,256,1,6,64]{1,4,3,0,2:T(8,128)(2,1)} fusion(f32[3,6,256,256]{2,3,1,0:T(8,128)} %fusion.69, bf16[3,256,3,6,64]{1,4,3,2,0:T(8,128)(2,1)} %bitcast.436, f32[3,6,256,256]{2,3,1,0:T(8,128)} %copy-done.14, f32[3,6,256]{2,1,0:T(8,128)} %copy-done.84), kind=kOutput, calls=%fused_computation.69 | convolution fusion | flops 159257344 | bytes 20103168 | tf_op jit(solution)/shard_map/shqk,sqhd->skhd/dot_general | solution.py:18
  204.2 3.3 convolution_bitcast_fusion.8
  210.6 3.1 multiply_reduce_fusion.11
  213.8 4.3 %copy.191 = bf16[1536,768]{1,0:T(8,128)(2,1)} copy(bf16[1536,768]{0,1:T(8,128)(2,1)} %bitcast.464) | data formatting | bytes 4718592 | tf_op jit(solution)/shard_map/dot_general | solution.py:36
  218.0 4.6 %copy.186 = bf16[1536,768]{1,0:T(8,128)(2,1)} copy(bf16[1536,768]{0,1:T(8,128)(2,1)} %bitcast.463) | data formatting | bytes 4718592 | tf_op jit(solution)/shard_map/dot_general | solution.py:36
  236.7 2.7 collective-permute-start.11
  243.3 3.0 collective-permute-done.16
  256.7 3.4 collective-permute-done.14
  260.6 3.3 collective-permute-done.19
  285.2 19.0 %collective-permute-done.25 = bf16[96,4608]{1,0:T(8,128)(2,1)S(1)} collective-permute-done((bf16[96,4608]{1,0:T(8,128)(2,1)S(1)}, bf16[96,4608]{1,0:T(8,128)(2,1)S(1)}, u32[]{:S(2)}, u32[]{:S(2)}) %collective-permute-start.25) | collective-permute-done | bytes 884768 | tf_op jit(solution)/shard_map/ppermute | solution.py:195
  307.4 15.6 %collective-permute-done.32 = bf16[96,4608]{1,0:T(8,128)(2,1)S(1)} collective-permute-done((bf16[96,4608]{1,0:T(8,128)(2,1)S(1)}, bf16[96,4608]{1,0:T(8,128)(2,1)S(1)}, u32[]{:S(2)}, u32[]{:S(2)}) %collective-permute-start.32) | collective-permute-done | bytes 884768 | tf_op jit(solution)/shard_map/ppermute | solution.py:195
  327.5 9.1 %collective-permute-done.33 = bf16[96,2304]{1,0:T(8,128)(2,1)S(1)} collective-permute-done((bf16[96,2304]{1,0:T(8,128)(2,1)S(1)}, bf16[96,2304]{1,0:T(8,128)(2,1)S(1)}, u32[]{:S(2)}, u32[]{:S(2)}) %collective-permute-start.33) | collective-permute-done | bytes 442400 | tf_op jit(solution)/shard_map/ppermute | solution.py:195
  339.0 7.1 %collective-permute-done.34 = bf16[96,1152]{1,0:T(8,128)(2,1)S(1)} collective-permute-done((bf16[96,1152]{1,0:T(8,128)(2,1)S(1)}, bf16[96,1152]{1,0:T(8,128)(2,1)S(1)}, u32[]{:S(2)}, u32[]{:S(2)}) %collective-permute-start.34) | collective-permute-done | bytes 221216 | tf_op jit(solution)/shard_map/ppermute | solution.py:195
  347.6 8.5 %collective-permute-done.28 = bf16[96,1152]{1,0:T(8,128)(2,1)S(1)} collective-permute-done((bf16[96,1152]{1,0:T(8,128)(2,1)S(1)}, bf16[96,1152]{1,0:T(8,128)(2,1)S(1)}, u32[]{:S(2)}, u32[]{:S(2)}) %collective-permute-start.28) | collective-permute-done | bytes 221216 | tf_op jit(solution)/shard_map/ppermute | solution.py:195
  356.2 3.0 collective-permute-done.35
  359.4 4.4 %collective-permute-done.29 = bf16[96,1152]{1,0:T(8,128)(2,1)S(1)} collective-permute-done((bf16[96,1152]{1,0:T(8,128)(2,1)S(1)}, bf16[96,1152]{1,0:T(8,128)(2,1)S(1)}, u32[]{:S(2)}, u32[]{:S(2)}) %collective-permute-start.29) | collective-permute-done | bytes 221216 | tf_op jit(solution)/shard_map/ppermute | solution.py:195
  368.5 8.0 %collective-permute-done.30 = bf16[96,2304]{1,0:T(8,128)(2,1)S(1)} collective-permute-done((bf16[96,2304]{1,0:T(8,128)(2,1)S(1)}, bf16[96,2304]{1,0:T(8,128)(2,1)S(1)}, u32[]{:S(2)}, u32[]{:S(2)}) %collective-permute-start.30) | collective-permute-done | bytes 442400 | tf_op jit(solution)/shard_map/ppermute | solution.py:195
  376.6 5.1 %collective-permute-done.37 = bf16[96,2304]{1,0:T(8,128)(2,1)S(1)} collective-permute-done((bf16[96,2304]{1,0:T(8,128)(2,1)S(1)}, bf16[96,2304]{1,0:T(8,128)(2,1)S(1)}, u32[]{:S(2)}, u32[]{:S(2)}) %collective-permute-start.37) | collective-permute-done | bytes 442400 | tf_op jit(solution)/shard_map/ppermute | solution.py:195
  (604 shorter events, 174.6 us)
Async XLA Ops:
  2.8 19.6 %collective-permute-start = (bf16[3456]{0:T(1024)(128)(2,1)S(1)}, bf16[3456]{0:T(1024)(128)(2,1)S(1)}, u32[]{:S(2)}, u32[]{:S(2)}) collective-permute-start(bf16[3456]{0:T(1024)(128)(2,1)S(1)} %dynamic-update-slice.83), channel_id=1, source_target_pairs={{0,1},{1,0},{2,3},{3,2},{4,5},{5,4},{6,7},{7,6},{8,9},{9,8},{10,11... | collective-permute-start | bytes 20744 | tf_op jit(solution)/shard_map/ppermute | solution.py:195
  3.4 17.2 %collective-permute-start.1 = (bf16[3456]{0:T(1024)(128)(2,1)S(1)}, bf16[3456]{0:T(1024)(128)(2,1)S(1)}, u32[]{:S(2)}, u32[]{:S(2)}) collective-permute-start(bf16[3456]{0:T(1024)(128)(2,1)S(1)} %dynamic-update-slice.83), channel_id=1, source_target_pairs={{0,2},{1,3},{2,0},{3,1},{4,6},{5,7},{6,4},{7,5},{8,10},{9,11},{10,... | collective-permute-start | bytes 20744 | tf_op jit(solution)/shard_map/ppermute | solution.py:195
  13.7 44.7 %collective-permute-start.5 = (bf16[96,4608]{1,0:T(8,128)(2,1)}, bf16[96,4608]{1,0:T(8,128)(2,1)}, u32[]{:S(2)}, u32[]{:S(2)}) collective-permute-start(bf16[96,4608]{1,0:T(8,128)(2,1)} %get-tuple-element.104), channel_id=1, source_target_pairs={{0,1},{1,0},{2,3},{3,2},{4,5},{5,4},{6,7},{7,6},{8,9},{9,8},{10,11... | collective-permute-start | bytes 2654216 | tf_op jit(solution)/shard_map/ppermute | solution.py:195
  13.8 44.0 %collective-permute-start.6 = (bf16[96,4608]{1,0:T(8,128)(2,1)}, bf16[96,4608]{1,0:T(8,128)(2,1)}, u32[]{:S(2)}, u32[]{:S(2)}) collective-permute-start(bf16[96,4608]{1,0:T(8,128)(2,1)} %get-tuple-element.104), channel_id=1, source_target_pairs={{0,2},{1,3},{2,0},{3,1},{4,6},{5,7},{6,4},{7,5},{8,10},{9,11},{10,... | collective-permute-start | bytes 2654216 | tf_op jit(solution)/shard_map/ppermute | solution.py:195
  14.1 48.9 %collective-permute-start.8 = (bf16[96,4608]{1,0:T(8,128)(2,1)S(1)}, bf16[96,4608]{1,0:T(8,128)(2,1)}, u32[]{:S(2)}, u32[]{:S(2)}) collective-permute-start(bf16[96,4608]{1,0:T(8,128)(2,1)S(1)} %get-tuple-element.103), channel_id=1, source_target_pairs={{0,1},{1,0},{2,3},{3,2},{4,5},{5,4},{6,7},{7,6},{8,9},{9,8},{10,11... | collective-permute-start | bytes 2654216 | tf_op jit(solution)/shard_map/ppermute | solution.py:195
  22.4 35.5 %collective-permute-start.9 = (bf16[96,4608]{1,0:T(8,128)(2,1)S(1)}, bf16[96,4608]{1,0:T(8,128)(2,1)}, u32[]{:S(2)}, u32[]{:S(2)}) collective-permute-start(bf16[96,4608]{1,0:T(8,128)(2,1)S(1)} %get-tuple-element.103), channel_id=1, source_target_pairs={{0,2},{1,3},{2,0},{3,1},{4,6},{5,7},{6,4},{7,5},{8,10},{9,11},{10,... | collective-permute-start | bytes 2654216 | tf_op jit(solution)/shard_map/ppermute | solution.py:195
  27.7 28.8 %collective-permute-start.4 = (f32[6,2304]{1,0:T(8,128)S(1)}, f32[6,2304]{1,0:T(8,128)S(1)}, u32[]{:S(2)}, u32[]{:S(2)}) collective-permute-start(f32[6,2304]{1,0:T(8,128)S(1)} %slice_add_fusion), channel_id=1, source_target_pairs={{0,2},{1,3},{2,0},{3,1},{4,6},{5,7},{6,4},{7,5},{8,10},{9,11},{10,... | collective-permute-start | bytes 165896 | tf_op jit(solution)/shard_map/ppermute | solution.py:195
  57.8 7.9 %collective-permute-start.7 = (bf16[96,4608]{1,0:T(8,128)(2,1)}, bf16[96,4608]{1,0:T(8,128)(2,1)S(1)}, u32[]{:S(2)}, u32[]{:S(2)}) collective-permute-start(bf16[96,4608]{1,0:T(8,128)(2,1)} %collective-permute-done.6), channel_id=1, source_target_pairs={{0,1},{1,0},{2,3},{3,2},{4,5},{5,4},{6,7},{7,6},{8,9},{9,8},{10,11... | collective-permute-start | bytes 2654216 | tf_op jit(solution)/shard_map/ppermute | solution.py:195
  57.9 10.4 %collective-permute-start.10 = (bf16[96,4608]{1,0:T(8,128)(2,1)}, bf16[96,4608]{1,0:T(8,128)(2,1)S(1)}, u32[]{:S(2)}, u32[]{:S(2)}) collective-permute-start(bf16[96,4608]{1,0:T(8,128)(2,1)} %collective-permute-done.9), channel_id=1, source_target_pairs={{0,1},{1,0},{2,3},{3,2},{4,5},{5,4},{6,7},{7,6},{8,9},{9,8},{10,11... | collective-permute-start | bytes 2654216 | tf_op jit(solution)/shard_map/ppermute | solution.py:195
  233.9 46.4 %collective-permute-start.24 = (bf16[192,4608]{1,0:T(8,128)(2,1)}, bf16[192,4608]{1,0:T(8,128)(2,1)}, u32[]{:S(2)}, u32[]{:S(2)}) collective-permute-start(bf16[192,4608]{1,0:T(8,128)(2,1)} %pad_maximum_fusion.1), channel_id=1, source_target_pairs={{0,1},{1,0},{2,3},{3,2},{4,5},{5,4},{6,7},{7,6},{8,9},{9,8},{10,11... | collective-permute-start | bytes 5308424 | tf_op jit(solution)/shard_map/ppermute | solution.py:195
  235.8 46.5 %collective-permute-start.31 = (bf16[192,4608]{1,0:T(8,128)(2,1)}, bf16[192,4608]{1,0:T(8,128)(2,1)}, u32[]{:S(2)}, u32[]{:S(2)}) collective-permute-start(bf16[192,4608]{1,0:T(8,128)(2,1)} %pad_maximum_fusion.2), channel_id=1, source_target_pairs={{0,1},{1,0},{2,3},{3,2},{4,5},{5,4},{6,7},{7,6},{8,9},{9,8},{10,11... | collective-permute-start | bytes 5308424 | tf_op jit(solution)/shard_map/ppermute | solution.py:195
  241.2 5.1 %collective-permute-start.16 = (bf16[1,5,2304]{2,1,0:T(8,128)(2,1)S(1)}, bf16[1,5,2304]{2,1,0:T(8,128)(2,1)S(1)}, u32[]{:S(2)}, u32[]{:S(2)}) collective-permute-start(bf16[1,5,2304]{2,1,0:T(8,128)(2,1)S(1)} %maximum_bitcast_fusion), channel_id=1, source_target_pairs={{0,16},{4,20},{8,24},{12,28},{16,0},{20,4},{24,8},{28,12},{1,17},{... | collective-permute-start | bytes 69128 | tf_op jit(solution)/shard_map/ppermute | solution.py:195
  241.7 6.1 %collective-permute-start.12 = (bf16[2,4,2304]{2,1,0:T(4,128)(2,1)S(1)}, bf16[2,4,2304]{2,1,0:T(4,128)(2,1)S(1)}, u32[]{:S(2)}, u32[]{:S(2)}) collective-permute-start(bf16[2,4,2304]{2,1,0:T(4,128)(2,1)S(1)} %pad_maximum_fusion.15), channel_id=1, source_target_pairs={{0,8},{4,12},{8,0},{12,4},{16,24},{20,28},{24,16},{28,20},{1,9},{5... | collective-permute-start | bytes 110600 | tf_op jit(solution)/shard_map/ppermute | solution.py:195
  247.9 5.2 %collective-permute-start.13 = (bf16[4,4,2304]{2,1,0:T(4,128)(2,1)S(1)}, bf16[4,4,2304]{2,1,0:T(4,128)(2,1)S(1)}, u32[]{:S(2)}, u32[]{:S(2)}) collective-permute-start(bf16[4,4,2304]{2,1,0:T(4,128)(2,1)S(1)} %pad_maximum_fusion.13), channel_id=1, source_target_pairs={{0,4},{4,0},{8,12},{12,8},{16,20},{20,16},{24,28},{28,24},{1,5},{5... | collective-permute-start | bytes 221192 | tf_op jit(solution)/shard_map/ppermute | solution.py:195
  250.8 5.2 %collective-permute-start.18 = (bf16[4,5,2304]{2,1,0:T(8,128)(2,1)S(1)}, bf16[4,5,2304]{2,1,0:T(8,128)(2,1)S(1)}, u32[]{:S(2)}, u32[]{:S(2)}) collective-permute-start(bf16[4,5,2304]{2,1,0:T(8,128)(2,1)S(1)} %pad_maximum_fusion.12), channel_id=1, source_target_pairs={{0,4},{4,0},{8,12},{12,8},{16,20},{20,16},{24,28},{28,24},{1,5},{5... | collective-permute-start | bytes 276488 | tf_op jit(solution)/shard_map/ppermute | solution.py:195
  253.3 6.8 %collective-permute-start.14 = (bf16[8,4,2304]{2,1,0:T(4,128)(2,1)S(1)}, bf16[8,4,2304]{2,1,0:T(4,128)(2,1)S(1)}, u32[]{:S(2)}, u32[]{:S(2)}) collective-permute-start(bf16[8,4,2304]{2,1,0:T(4,128)(2,1)S(1)} %pad_maximum_fusion.11), channel_id=1, source_target_pairs={{0,2},{1,3},{2,0},{3,1},{4,6},{5,7},{6,4},{7,5},{8,10},{9,11},{10,... | collective-permute-start | bytes 442376 | tf_op jit(solution)/shard_map/ppermute | solution.py:195
  256.1 7.7 %collective-permute-start.19 = (bf16[8,5,2304]{2,1,0:T(8,128)(2,1)S(1)}, bf16[8,5,2304]{2,1,0:T(8,128)(2,1)S(1)}, u32[]{:S(2)}, u32[]{:S(2)}) collective-permute-start(bf16[8,5,2304]{2,1,0:T(8,128)(2,1)S(1)} %pad_maximum_fusion.9), channel_id=1, source_target_pairs={{0,2},{1,3},{2,0},{3,1},{4,6},{5,7},{6,4},{7,5},{8,10},{9,11},{10,... | collective-permute-start | bytes 552968 | tf_op jit(solution)/shard_map/ppermute | solution.py:195
  271.7 7.7 %collective-permute-start.21 = (f32[3,96]{1,0:T(4,128)S(1)}, f32[3,96]{1,0:T(4,128)S(1)}, u32[]{:S(2)}, u32[]{:S(2)}) collective-permute-start(f32[3,96]{1,0:T(4,128)S(1)} %bitcast.491), channel_id=1, source_target_pairs={{0,1},{1,0},{2,3},{3,2},{4,5},{5,4},{6,7},{7,6},{8,9},{9,8},{10,11... | collective-permute-start | bytes 3464 | tf_op jit(solution)/shard_map/ppermute | solution.py:195
  272.3 7.1 %collective-permute-start.22 = (f32[3,96]{1,0:T(4,128)S(1)}, f32[3,96]{1,0:T(4,128)S(1)}, u32[]{:S(2)}, u32[]{:S(2)}) collective-permute-start(f32[3,96]{1,0:T(4,128)S(1)} %bitcast.493), channel_id=1, source_target_pairs={{0,2},{1,3},{2,0},{3,1},{4,6},{5,7},{6,4},{7,5},{8,10},{9,11},{10,... | collective-permute-start | bytes 3464 | tf_op jit(solution)/shard_map/ppermute | solution.py:195
  272.7 6.7 %collective-permute-start.23 = (f32[3,96]{1,0:T(4,128)S(1)}, f32[3,96]{1,0:T(4,128)S(1)}, u32[]{:S(2)}, u32[]{:S(2)}) collective-permute-start(f32[3,96]{1,0:T(4,128)S(1)} %bitcast.495), channel_id=1, source_target_pairs={{0,3},{1,2},{2,1},{3,0},{4,7},{5,6},{6,5},{7,4},{8,11},{9,10},{10,... | collective-permute-start | bytes 3464 | tf_op jit(solution)/shard_map/ppermute | solution.py:195
  281.7 22.6 %collective-permute-start.25 = (bf16[96,4608]{1,0:T(8,128)(2,1)S(1)}, bf16[96,4608]{1,0:T(8,128)(2,1)S(1)}, u32[]{:S(2)}, u32[]{:S(2)}) collective-permute-start(bf16[96,4608]{1,0:T(8,128)(2,1)S(1)} %add_convert_fusion.1), channel_id=1, source_target_pairs={{0,2},{1,3},{2,0},{3,1},{4,6},{5,7},{6,4},{7,5},{8,10},{9,11},{10,... | collective-permute-start | bytes 2654216 | tf_op jit(solution)/shard_map/ppermute | solution.py:195
  283.7 39.2 %collective-permute-start.32 = (bf16[96,4608]{1,0:T(8,128)(2,1)S(1)}, bf16[96,4608]{1,0:T(8,128)(2,1)S(1)}, u32[]{:S(2)}, u32[]{:S(2)}) collective-permute-start(bf16[96,4608]{1,0:T(8,128)(2,1)S(1)} %add_convert_fusion), channel_id=1, source_target_pairs={{0,2},{1,3},{2,0},{3,1},{4,6},{5,7},{6,4},{7,5},{8,10},{9,11},{10,... | collective-permute-start | bytes 2654216 | tf_op jit(solution)/shard_map/ppermute | solution.py:195
  305.8 20.2 %collective-permute-start.26 = (bf16[96,2304]{1,0:T(8,128)(2,1)S(1)}, bf16[96,2304]{1,0:T(8,128)(2,1)S(1)}, u32[]{:S(2)}, u32[]{:S(2)}) collective-permute-start(bf16[96,2304]{1,0:T(8,128)(2,1)S(1)} %select_convert_fusion.1), channel_id=1, source_target_pairs={{0,4},{4,0},{8,12},{12,8},{16,20},{20,16},{24,28},{28,24},{1,5},{5... | collective-permute-start | bytes 1327112 | tf_op jit(solution)/shard_map/ppermute | solution.py:195
  324.5 12.0 %collective-permute-start.33 = (bf16[96,2304]{1,0:T(8,128)(2,1)S(1)}, bf16[96,2304]{1,0:T(8,128)(2,1)S(1)}, u32[]{:S(2)}, u32[]{:S(2)}) collective-permute-start(bf16[96,2304]{1,0:T(8,128)(2,1)S(1)} %select_convert_fusion), channel_id=1, source_target_pairs={{0,4},{4,0},{8,12},{12,8},{16,20},{20,16},{24,28},{28,24},{1,5},{5... | collective-permute-start | bytes 1327112 | tf_op jit(solution)/shard_map/ppermute | solution.py:195
  326.2 11.7 %collective-permute-start.27 = (bf16[96,1152]{1,0:T(8,128)(2,1)S(1)}, bf16[96,1152]{1,0:T(8,128)(2,1)S(1)}, u32[]{:S(2)}, u32[]{:S(2)}) collective-permute-start(bf16[96,1152]{1,0:T(8,128)(2,1)S(1)} %select_convert_fusion.3), channel_id=1, source_target_pairs={{0,8},{4,12},{8,0},{12,4},{16,24},{20,28},{24,16},{28,20},{1,9},{5... | collective-permute-start | bytes 663560 | tf_op jit(solution)/shard_map/ppermute | solution.py:195
  336.7 9.4 %collective-permute-start.34 = (bf16[96,1152]{1,0:T(8,128)(2,1)S(1)}, bf16[96,1152]{1,0:T(8,128)(2,1)S(1)}, u32[]{:S(2)}, u32[]{:S(2)}) collective-permute-start(bf16[96,1152]{1,0:T(8,128)(2,1)S(1)} %select_convert_fusion.2), channel_id=1, source_target_pairs={{0,8},{4,12},{8,0},{12,4},{16,24},{20,28},{24,16},{28,20},{1,9},{5... | collective-permute-start | bytes 663560 | tf_op jit(solution)/shard_map/ppermute | solution.py:195
  337.9 18.1 %collective-permute-start.28 = (bf16[96,1152]{1,0:T(8,128)(2,1)S(1)}, bf16[96,1152]{1,0:T(8,128)(2,1)S(1)}, u32[]{:S(2)}, u32[]{:S(2)}) collective-permute-start(bf16[96,1152]{1,0:T(8,128)(2,1)S(1)} %add_convert_fusion.9), channel_id=1, source_target_pairs={{0,16},{4,20},{8,24},{12,28},{16,0},{20,4},{24,8},{28,12},{1,17},{... | collective-permute-start | bytes 663560 | tf_op jit(solution)/shard_map/ppermute | solution.py:195
  346.2 13.0 %collective-permute-start.35 = (bf16[96,1152]{1,0:T(8,128)(2,1)S(1)}, bf16[96,1152]{1,0:T(8,128)(2,1)S(1)}, u32[]{:S(2)}, u32[]{:S(2)}) collective-permute-start(bf16[96,1152]{1,0:T(8,128)(2,1)S(1)} %add_convert_fusion.7), channel_id=1, source_target_pairs={{0,16},{4,20},{8,24},{12,28},{16,0},{20,4},{24,8},{28,12},{1,17},{... | collective-permute-start | bytes 663560 | tf_op jit(solution)/shard_map/ppermute | solution.py:195
  356.1 7.7 %collective-permute-start.29 = (bf16[96,1152]{1,0:T(8,128)(2,1)S(1)}, bf16[96,1152]{1,0:T(8,128)(2,1)S(1)}, u32[]{:S(2)}, u32[]{:S(2)}) collective-permute-start(bf16[96,1152]{1,0:T(8,128)(2,1)S(1)} %add_convert_fusion.8), channel_id=1, source_target_pairs={{0,8},{4,12},{8,0},{12,4},{16,24},{20,28},{24,16},{28,20},{1,9},{5... | collective-permute-start | bytes 663560 | tf_op jit(solution)/shard_map/ppermute | solution.py:195
  359.3 7.6 %collective-permute-start.36 = (bf16[96,1152]{1,0:T(8,128)(2,1)S(1)}, bf16[96,1152]{1,0:T(8,128)(2,1)S(1)}, u32[]{:S(2)}, u32[]{:S(2)}) collective-permute-start(bf16[96,1152]{1,0:T(8,128)(2,1)S(1)} %add_convert_fusion.6), channel_id=1, source_target_pairs={{0,8},{4,12},{8,0},{12,4},{16,24},{20,28},{24,16},{28,20},{1,9},{5... | collective-permute-start | bytes 663560 | tf_op jit(solution)/shard_map/ppermute | solution.py:195
  363.9 12.6 %collective-permute-start.30 = (bf16[96,2304]{1,0:T(8,128)(2,1)S(1)}, bf16[96,2304]{1,0:T(8,128)(2,1)S(1)}, u32[]{:S(2)}, u32[]{:S(2)}) collective-permute-start(bf16[96,2304]{1,0:T(8,128)(2,1)S(1)} %pad_maximum_fusion.4), channel_id=1, source_target_pairs={{0,4},{4,0},{8,12},{12,8},{16,20},{20,16},{24,28},{28,24},{1,5},{5... | collective-permute-start | bytes 1327112 | tf_op jit(solution)/shard_map/ppermute | solution.py:195
  367.0 14.8 %collective-permute-start.37 = (bf16[96,2304]{1,0:T(8,128)(2,1)S(1)}, bf16[96,2304]{1,0:T(8,128)(2,1)S(1)}, u32[]{:S(2)}, u32[]{:S(2)}) collective-permute-start(bf16[96,2304]{1,0:T(8,128)(2,1)S(1)} %pad_maximum_fusion.5), channel_id=1, source_target_pairs={{0,4},{4,0},{8,12},{12,8},{16,20},{20,16},{24,28},{28,24},{1,5},{5... | collective-permute-start | bytes 1327112 | tf_op jit(solution)/shard_map/ppermute | solution.py:195
  (136 other events, 581.2 us)

commit v2 on v1

--- a/solution.py
+++ b/solution.py
@@ -3,26 +3,18 @@
 import jax
 import jax.numpy as jnp
 from jax import lax
+from jax.experimental import pallas as pl
+from jax.experimental.pallas import tpu as pltpu
 from jax.sharding import PartitionSpec as P
 
 HEADS = 6
 LAYERS = 2
+VMEM_GRANT = 60 * 1024 * 1024
 
 
 NORM_EPS = 1e-06
 GELU_K = 0.7978845608028654
 GELU_C = 0.044715
-
-
-def einsum_mixed(form, left, right):
-    return jnp.einsum(form, left, right, preferred_element_type=jnp.float32)
-
-
-def matmul_last(left, right):
-    flat = left.reshape(-1, left.shape[-1])
-    return jnp.dot(flat, right, preferred_element_type=jnp.float32).reshape(
-        left.shape[:-1] + (right.shape[1],)
-    )
 
 
 def matmul_back(left, right):
@@ -57,133 +49,335 @@
     return 0.5 * values * (1.0 + jnp.tanh(inner))
 
 
-def gelu_slope(values):
-    tangent = jnp.tanh(GELU_K * (values + GELU_C * values * values * values))
-    return 0.5 * (1.0 + tangent) + 0.5 * values * (1.0 - tangent * tangent) * GELU_K * (
-        1.0 + 3.0 * GELU_C * values * values
-    )
-
-
 def silu_slope(values):
     sigm = jax.nn.sigmoid(values)
     return sigm * (1.0 + values * (1.0 - sigm))
 
 
-def split_heads(qkv):
-    seq_slots, length, triple = qkv.shape
-    width = triple // 3
-    split = qkv.reshape(seq_slots, length, 3, HEADS, width // HEADS)
-    return (split[:, :, 0], split[:, :, 1], split[:, :, 2])
-
-
-def attend(qkv):
-    queries, keys, values = split_heads(qkv)
-    scale = 1.0 / jnp.sqrt(jnp.float32(queries.shape[-1]))
-    scores = einsum_mixed("sqhd,skhd->shqk", queries, keys) * scale
-    top = jnp.max(scores, axis=-1, keepdims=True)
-    expo = jnp.exp(scores - top)
-    probs = expo / jnp.sum(expo, axis=-1, keepdims=True)
-    probs_low = probs.astype(jnp.bfloat16)
-    mixed = einsum_mixed("shqk,skhd->sqhd", probs_low, values).astype(jnp.bfloat16)
-    return (probs, probs_low, mixed.reshape(qkv.shape[0], qkv.shape[1], -1))
-
-
-def attend_back(qkv, probs, probs_low, grad_mixed):
-    queries, keys, values = split_heads(qkv)
-    scale = 1.0 / jnp.sqrt(jnp.float32(queries.shape[-1]))
-    grad_heads = grad_mixed.reshape(values.shape)
-    grad_probs = einsum_mixed("sqhd,skhd->shqk", grad_heads, values)
-    grad_values = einsum_mixed("shqk,sqhd->skhd", probs_low, grad_heads)
-    row_dot = jnp.sum(probs * grad_probs, axis=-1, keepdims=True)
-    grad_scores = (probs * (grad_probs - row_dot) * scale).astype(jnp.bfloat16)
-    grad_queries = einsum_mixed("shqk,skhd->sqhd", grad_scores, keys)
-    grad_keys = einsum_mixed("shqk,sqhd->skhd", grad_scores, queries)
-    joined = jnp.stack([grad_queries, grad_keys, grad_values], axis=2)
-    return joined.reshape(qkv.shape).astype(jnp.bfloat16)
-
-
-def layer_parts(resid, ada, weights):
-    qkv_weight, proj_weight, proj_bias, up_weight, up_bias, down_weight, down_bias = weights
-    width = resid.shape[-1]
-    mods = [ada[:, None, piece_idx * width : (piece_idx + 1) * width] for piece_idx in range(6)]
-    normed_one, inv_one = norm_rows(resid)
-    attn_in = (normed_one * (1.0 + mods[1]) + mods[0]).astype(jnp.bfloat16)
-    qkv = matmul_last(attn_in, qkv_weight).astype(jnp.bfloat16)
-    probs, probs_low, mixed = attend(qkv)
-    attn = matmul_last(mixed, proj_weight) + proj_bias.astype(jnp.float32)
-    resid_one = resid + mods[2] * attn
-    normed_two, inv_two = norm_rows(resid_one)
-    mlp_in = (normed_two * (1.0 + mods[4]) + mods[3]).astype(jnp.bfloat16)
-    pre_act = matmul_last(mlp_in, up_weight) + up_bias.astype(jnp.float32)
-    hidden = gelu_tanh(pre_act).astype(jnp.bfloat16)
-    branch = matmul_last(hidden, down_weight) + down_bias.astype(jnp.float32)
-    result = resid_one + mods[5] * branch
-    return dict(
-        mods=mods,
-        normed_one=normed_one,
-        inv_one=inv_one,
-        attn_in=attn_in,
-        qkv=qkv,
-        probs=probs,
-        probs_low=probs_low,
-        mixed=mixed,
-        attn=attn,
-        normed_two=normed_two,
-        inv_two=inv_two,
-        mlp_in=mlp_in,
-        pre_act=pre_act,
-        hidden=hidden,
-        branch=branch,
-        result=result,
-    )
-
-
-def layer_backward(saved, weights, grad_out):
-    qkv_weight, proj_weight, proj_bias, up_weight, up_bias, down_weight, down_bias = weights
-    mods = saved["mods"]
-    grad_gate_two = jnp.sum(grad_out * saved["branch"], axis=1)
-    grad_branch = grad_out * mods[5]
-    grad_down_bias = jnp.sum(grad_branch, axis=(0, 1))
-    branch_low = grad_branch.astype(jnp.bfloat16)
-    grad_down_weight = outer_total(saved["hidden"], branch_low)
-    grad_pre = matmul_back(branch_low, down_weight) * gelu_slope(saved["pre_act"])
-    grad_up_bias = jnp.sum(grad_pre, axis=(0, 1))
-    pre_low = grad_pre.astype(jnp.bfloat16)
-    grad_up_weight = outer_total(saved["mlp_in"], pre_low)
-    grad_mlp = matmul_back(pre_low, up_weight)
-    grad_shift_two = jnp.sum(grad_mlp, axis=1)
-    grad_scale_two = jnp.sum(grad_mlp * saved["normed_two"], axis=1)
-    grad_one = grad_out + norm_back(
-        saved["normed_two"], saved["inv_two"], grad_mlp * (1.0 + mods[4])
-    )
-    grad_gate_one = jnp.sum(grad_one * saved["attn"], axis=1)
-    grad_attn = grad_one * mods[2]
-    grad_proj_bias = jnp.sum(grad_attn, axis=(0, 1))
-    attn_low = grad_attn.astype(jnp.bfloat16)
-    grad_proj_weight = outer_total(saved["mixed"], attn_low)
-    grad_mixed = matmul_back(attn_low, proj_weight).astype(jnp.bfloat16)
-    grad_qkv = attend_back(saved["qkv"], saved["probs"], saved["probs_low"], grad_mixed)
-    grad_qkv_weight = outer_total(saved["attn_in"], grad_qkv)
-    grad_in = matmul_back(grad_qkv, qkv_weight)
-    grad_shift_one = jnp.sum(grad_in, axis=1)
-    grad_scale_one = jnp.sum(grad_in * saved["normed_one"], axis=1)
-    grad_resid = grad_one + norm_back(
-        saved["normed_one"], saved["inv_one"], grad_in * (1.0 + mods[1])
-    )
-    grad_ada = jnp.concatenate(
-        [
-            grad_shift_one,
-            grad_scale_one,
-            grad_gate_one,
-            grad_shift_two,
-            grad_scale_two,
-            grad_gate_two,
-        ],
-        axis=-1,
-    )
-    bias_row = jnp.concatenate([grad_proj_bias, grad_up_bias, grad_down_bias])
-    wide = (grad_qkv_weight, grad_proj_weight, grad_up_weight, grad_down_weight)
-    return grad_resid, grad_ada, bias_row, wide
+def _nt(left, right):
+    return lax.dot_general(
+        left, right, (((1,), (1,)), ((), ())), preferred_element_type=jnp.float32
+    )
+
+
+def _nn(left, right):
+    return jnp.dot(left, right, preferred_element_type=jnp.float32)
+
+
+def _tn(left, right):
+    return lax.dot_general(
+        left, right, (((0,), (0,)), ((), ())), preferred_element_type=jnp.float32
+    )
+
+
+def halves(pair):
+    lane = lax.broadcasted_iota(jnp.int32, (1, pair), 1)
+    first = (lane < pair // 2).astype(jnp.float32)
+    return first.astype(jnp.bfloat16), (1.0 - first).astype(jnp.bfloat16)
+
+
+def load_plan(pieces, full, sems, me):
+    qkv, proj, up, down = full
+    shards = len(pieces)
+    rows = qkv.shape[0] // shards
+    width, triple, inner = proj.shape[1], qkv.shape[1], up.shape[1]
+    ratio = down.shape[0] // (shards * rows)
+    plan = [[], [], [], []]
+    for j, piece in enumerate(pieces):
+        own = me ^ j
+        at = pl.ds(pl.multiple_of(own * rows, rows), rows)
+        col = 0
+        for n, (target, size) in enumerate(((qkv, triple), (proj, width), (up, inner))):
+            plan[n].append(
+                pltpu.make_async_copy(
+                    piece.at[:, pl.ds(col, size)], target.at[at, :], sems.at[j, n]
+                )
+            )
+            col += size
+        for q in range(ratio):
+            start = pl.multiple_of((own * ratio + q) * rows, rows)
+            plan[3].append(
+                pltpu.make_async_copy(
+                    piece.at[:, pl.ds(col, width)], down.at[pl.ds(start, rows), :], sems.at[j, 3 + q]
+                )
+            )
+            col += width
+    return plan
+
+
+def forward_kernel(
+    shards, heads, info, resid, ada, biases, *rest
+):
+    pieces = rest[:shards]
+    result, one_out, qkv_out, probs_out, mixed_out, attn_out, pre_out, branch_out = rest[
+        shards : shards + 8
+    ]
+    w_qkv, w_proj, w_up, w_down, sems = rest[shards + 8 :]
+    f32, bf16 = jnp.float32, jnp.bfloat16
+    slot = pl.program_id(0)
+    width, inner = w_proj.shape[1], w_up.shape[1]
+    plan = load_plan(pieces, (w_qkv, w_proj, w_up, w_down), sems, info[1])
+
+    @pl.when(slot == 0)
+    def _():
+        for group in plan:
+            for copy in group:
+                copy.start()
+        for group in plan:
+            for copy in group:
+                copy.wait()
+
+    @pl.when(slot < info[0])
+    def _():
+        mods = ada[0]
+        value = resid[0]
+        normed, _ = norm_rows(value)
+        attn_in = (normed * (1.0 + mods[1:2]) + mods[0:1]).astype(bf16)
+        qkv_out[0] = _nn(attn_in, w_qkv[...]).astype(bf16)
+        pair = 2 * width // heads
+        scale = 1.0 / (width // heads) ** 0.5
+        masks = halves(pair)
+        for p in range(heads // 2):
+            query = qkv_out[0, :, p * pair : (p + 1) * pair]
+            key = qkv_out[0, :, width + p * pair : width + (p + 1) * pair]
+            val = qkv_out[0, :, 2 * width + p * pair : 2 * width + (p + 1) * pair]
+            total = None
+            for h in range(2):
+                scores = _nt(query * masks[h], key) * scale
+                expo = jnp.exp(scores - jnp.max(scores, axis=-1, keepdims=True))
+                probs = (expo * (1.0 / jnp.sum(expo, axis=-1, keepdims=True))).astype(bf16)
+                probs_out[0, 2 * p + h] = probs
+                term = _nn(probs, val * masks[h])
+                total = term if total is None else total + term
+            mixed_out[0, :, p * pair : (p + 1) * pair] = total.astype(bf16)
+        attn = _nn(mixed_out[0], w_proj[...]) + biases[:, :width]
+        attn_out[0] = attn.astype(bf16)
+        one = value + mods[2:3] * attn
+        one_out[0] = one
+        normed, _ = norm_rows(one)
+        mlp_in = (normed * (1.0 + mods[4:5]) + mods[3:4]).astype(bf16)
+        pre = _nn(mlp_in, w_up[...]) + biases[:, width : width + inner]
+        pre_out[0] = pre
+        hidden = gelu_tanh(pre).astype(bf16)
+        branch = _nn(hidden, w_down[...]) + biases[:, width + inner :]
+        branch_out[0] = branch.astype(bf16)
+        result[0] = one + mods[5:6] * branch
+
+    @pl.when(slot >= info[0])
+    def _():
+        result[0] = jnp.zeros_like(result[0])
+
+
+def backward_kernel(shards, heads, info, grad, resid, one, ada, qkv, probs, mixed, attn, pre, branch, *rest):
+    pieces = rest[:shards]
+    grad_out, gada_out, bias_out, keep_out, send_out = rest[shards : shards + 5]
+    w_qkv, w_proj, w_up, w_down, a_qkv, a_proj, a_up, a_down, g_heads, sems = rest[shards + 5 :]
+    f32, bf16 = jnp.float32, jnp.bfloat16
+    slot = pl.program_id(0)
+    width, inner = w_proj.shape[1], w_up.shape[1]
+    me = info[1]
+    plan = load_plan(pieces, (w_qkv, w_proj, w_up, w_down), sems, me)
+
+    @pl.when(slot == 0)
+    def _():
+        for group in plan:
+            for copy in group:
+                copy.start()
+        a_qkv[...] = jnp.zeros_like(a_qkv)
+        a_proj[...] = jnp.zeros_like(a_proj)
+        a_up[...] = jnp.zeros_like(a_up)
+        a_down[...] = jnp.zeros_like(a_down)
+        bias_out[...] = jnp.zeros_like(bias_out)
+        for group in plan:
+            for copy in group:
+                copy.wait()
+
+    @pl.when(slot < info[0])
+    def _():
+        mods = ada[0]
+        g = grad[0]
+        gada_out[0, 5:6, :] = jnp.sum(g * branch[0].astype(f32), axis=0, keepdims=True)
+        gbranch = g * mods[5:6]
+        bias_out[:, width + inner :] += jnp.sum(gbranch, axis=0, keepdims=True)
+        gb = gbranch.astype(bf16)
+        u = pre[0]
+        square = u * u
+        tangent = jnp.tanh(GELU_K * (u + GELU_C * square * u))
+        half = 0.5 * (1.0 + tangent)
+        hidden = (u * half).astype(bf16)
+        slope = half + 0.5 * u * (1.0 - tangent * tangent) * (
+            GELU_K + (3.0 * GELU_C * GELU_K) * square
+        )
+        a_down[...] += _tn(hidden, gb)
+        gpre = _nt(gb, w_down[...]) * slope
+        bias_out[:, width : width + inner] += jnp.sum(gpre, axis=0, keepdims=True)
+        gp = gpre.astype(bf16)
+        normed, inv = norm_rows(one[0])
+        mlp_in = (normed * (1.0 + mods[4:5]) + mods[3:4]).astype(bf16)
+        a_up[...] += _tn(mlp_in, gp)
+        gmlp = _nt(gp, w_up[...])
+        gada_out[0, 3:4, :] = jnp.sum(gmlp, axis=0, keepdims=True)
+        gada_out[0, 4:5, :] = jnp.sum(gmlp * normed, axis=0, keepdims=True)
+        g1 = g + norm_back(normed, inv, gmlp * (1.0 + mods[4:5]))
+        gada_out[0, 2:3, :] = jnp.sum(g1 * attn[0].astype(f32), axis=0, keepdims=True)
+        gattn = g1 * mods[2:3]
+        bias_out[:, :width] += jnp.sum(gattn, axis=0, keepdims=True)
+        ga = gattn.astype(bf16)
+        a_proj[...] += _tn(mixed[0], ga)
+        gmixed = _nt(ga, w_proj[...]).astype(bf16)
+        pair = 2 * width // heads
+        scale = 1.0 / (width // heads) ** 0.5
+        masks = halves(pair)
+        for p in range(heads // 2):
+            cut = slice(p * pair, (p + 1) * pair)
+            query = qkv[0, :, p * pair : (p + 1) * pair]
+            key = qkv[0, :, width + p * pair : width + (p + 1) * pair]
+            val = qkv[0, :, 2 * width + p * pair : 2 * width + (p + 1) * pair]
+            gm = gmixed[:, cut]
+            gq, gk, gv = 0.0, 0.0, 0.0
+            for h in range(2):
+                low = probs[0, 2 * p + h]
+                gm_h = gm * masks[h]
+                gprobs = _nt(gm_h, val)
+                wide = low.astype(f32)
+                dot = jnp.sum(wide * gprobs, axis=-1, keepdims=True)
+                gscores = (wide * (gprobs - dot) * scale).astype(bf16)
+                gv = gv + _tn(low, gm_h)
+                gq = gq + _nn(gscores, key * masks[h])
+                gk = gk + _tn(gscores, query * masks[h])
+            g_heads[:, p * pair : (p + 1) * pair] = gq.astype(bf16)
+            g_heads[:, width + p * pair : width + (p + 1) * pair] = gk.astype(bf16)
+            g_heads[:, 2 * width + p * pair : 2 * width + (p + 1) * pair] = gv.astype(bf16)
+        normed, inv = norm_rows(resid[0])
+        attn_in = (normed * (1.0 + mods[1:2]) + mods[0:1]).astype(bf16)
+        a_qkv[...] += _tn(attn_in, g_heads[...])
+        gin = _nt(g_heads[...], w_qkv[...])
+        gada_out[0, 0:1, :] = jnp.sum(gin, axis=0, keepdims=True)
+        gada_out[0, 1:2, :] = jnp.sum(gin * normed, axis=0, keepdims=True)
+        grad_out[0] = g1 + norm_back(normed, inv, gin * (1.0 + mods[1:2]))
+
+    @pl.when(slot >= info[0])
+    def _():
+        grad_out[0] = jnp.zeros_like(grad_out[0])
+        gada_out[0] = jnp.zeros_like(gada_out[0])
+
+    @pl.when(slot == pl.num_programs(0) - 1)
+    def _():
+        rows = a_qkv.shape[0] // shards
+        ratio = a_down.shape[0] // (shards * rows)
+        for j in range(shards):
+            out = send_out if j & 1 else keep_out
+            own = me ^ j
+            at = pl.ds(pl.multiple_of(own * rows, rows), rows)
+            col = 0
+            for acc in (a_qkv, a_proj, a_up):
+                size = acc.shape[1]
+                out[j >> 1, :, col : col + size] = acc[at, :].astype(bf16)
+                col += size
+            for q in range(ratio):
+                start = pl.multiple_of((own * ratio + q) * rows, rows)
+                out[j >> 1, :, col : col + width] = a_down[pl.ds(start, rows), :].astype(bf16)
+                col += width
+
+
+def per_slot(shape):
+    rest = (0,) * (len(shape) - 1)
+    return pl.BlockSpec((1,) + tuple(shape[1:]), lambda slot, info: (slot,) + rest)
+
+
+def whole_block(shape):
+    zeros = (0,) * len(shape)
+    return pl.BlockSpec(tuple(shape), lambda slot, info: zeros)
+
+
+def forward_call(info, resid, ada, biases, pieces, dims):
+    slots, length, width, triple, inner, heads = dims
+    shards = len(pieces)
+    f32, bf16 = jnp.float32, jnp.bfloat16
+    shapes = [
+        ((slots, length, width), f32),
+        ((slots, length, width), f32),
+        ((slots, length, triple), bf16),
+        ((slots, heads, length, length), bf16),
+        ((slots, length, width), bf16),
+        ((slots, length, width), bf16),
+        ((slots, length, inner), f32),
+        ((slots, length, width), bf16),
+    ]
+    return pl.pallas_call(
+        functools.partial(forward_kernel, shards, heads),
+        out_shape=[jax.ShapeDtypeStruct(s, d) for s, d in shapes],
+        grid_spec=pltpu.PrefetchScalarGridSpec(
+            num_scalar_prefetch=1,
+            grid=(slots,),
+            in_specs=[per_slot(resid.shape), per_slot(ada.shape), whole_block(biases.shape)]
+            + [pl.BlockSpec(memory_space=pl.ANY)] * shards,
+            out_specs=[per_slot(s) for s, _ in shapes],
+            scratch_shapes=[
+                pltpu.VMEM((width, triple), bf16),
+                pltpu.VMEM((width, width), bf16),
+                pltpu.VMEM((width, inner), bf16),
+                pltpu.VMEM((inner, width), bf16),
+                pltpu.SemaphoreType.DMA((shards, 3 + inner // width)),
+            ],
+        ),
+        compiler_params=pltpu.CompilerParams(vmem_limit_bytes=VMEM_GRANT),
+        cost_estimate=pl.CostEstimate(
+            flops=2 * slots * length * width * (triple + width + 2 * inner),
+            bytes_accessed=slots * length * inner * 16,
+            transcendentals=slots * length * (inner + heads * length),
+        ),
+        name="block_forward",
+    )(info, resid, ada, biases, *pieces)
+
+
+def backward_call(info, grad, resid, ada, saved, pieces, dims):
+    slots, length, width, triple, inner, heads = dims
+    one, qkv, probs, mixed, attn, pre, branch = saved
+    shards = len(pieces)
+    rows = width // shards
+    f32, bf16 = jnp.float32, jnp.bfloat16
+    columns = triple + width + 2 * inner
+    half = (shards // 2, rows, columns)
+    shapes = [
+        ((slots, length, width), f32),
+        (ada.shape, f32),
+        ((1, 2 * width + inner), f32),
+        (half, bf16),
+        (half, bf16),
+    ]
+    args = (grad, resid, one, ada, qkv, probs, mixed, attn, pre, branch)
+    return pl.pallas_call(
+        functools.partial(backward_kernel, shards, heads),
+        out_shape=[jax.ShapeDtypeStruct(s, d) for s, d in shapes],
+        grid_spec=pltpu.PrefetchScalarGridSpec(
+            num_scalar_prefetch=1,
+            grid=(slots,),
+            in_specs=[per_slot(a.shape) for a in args]
+            + [pl.BlockSpec(memory_space=pl.ANY)] * shards,
+            out_specs=[per_slot(shapes[0][0]), per_slot(ada.shape)]
+            + [whole_block(s) for s, _ in shapes[2:]],
+            scratch_shapes=[
+                pltpu.VMEM((width, triple), bf16),
+                pltpu.VMEM((width, width), bf16),
+                pltpu.VMEM((width, inner), bf16),
+                pltpu.VMEM((inner, width), bf16),
+                pltpu.VMEM((width, triple), f32),
+                pltpu.VMEM((width, width), f32),
+                pltpu.VMEM((width, inner), f32),
+                pltpu.VMEM((inner, width), f32),
+                pltpu.VMEM((length, triple), bf16),
+                pltpu.SemaphoreType.DMA((shards, 3 + inner // width)),
+            ],
+        ),
+        compiler_params=pltpu.CompilerParams(vmem_limit_bytes=VMEM_GRANT),
+        cost_estimate=pl.CostEstimate(
+            flops=4 * slots * length * width * (triple + width + 2 * inner),
+            bytes_accessed=slots * length * inner * 16,
+            transcendentals=slots * length * inner,
+        ),
+        name="block_backward",
+    )(info, *args, *pieces)
 
 
 def bits_of(size):
@@ -224,6 +418,23 @@
         rows = got.shape[0] // len(keep)
         blocks = {
             j: blocks[j].astype(jnp.float32) + got[n * rows : (n + 1) * rows].astype(jnp.float32)
+            for n, j in enumerate(keep)
+        }
+    return blocks[0]
+
+
+def scatter_pair(kept, sent, axis, size, wire):
+    got = swap(sent, axis, size, 1)
+    count = kept.shape[0]
+    blocks = [kept[n].astype(jnp.float32) + got[n].astype(jnp.float32) for n in range(count)]
+    blocks = {n << 1: block for n, block in enumerate(blocks)}
+    for bit in bits_of(size)[1:]:
+        keep = [j for j in blocks if not j & bit]
+        going = jnp.concatenate([blocks[j | bit].astype(wire) for j in keep], axis=0)
+        back = swap(going, axis, size, bit)
+        rows = back.shape[0] // len(keep)
+        blocks = {
+            j: blocks[j] + back[n * rows : (n + 1) * rows].astype(jnp.float32)
             for n, j in enumerate(keep)
         }
     return blocks[0]
@@ -301,19 +512,7 @@
         pack_rows(qkv_weight[n], proj_weight[n], up_weight[n], down_weight[n])
         for n in range(LAYERS)
     ]
-    fulls = []
-    for n in range(LAYERS):
-        full = to_absolute(gather_rel(packs[n], "fsdp", shards), "fsdp")
-        edge = [0, triple, triple + width, triple + width + inner]
-        down_full = full[:, :, edge[3] :].reshape(shards, rows, ratio, width)
-        fulls.append(
-            (
-                full[:, :, : edge[1]].reshape(width, triple),
-                full[:, :, edge[1] : edge[2]].reshape(width, width),
-                full[:, :, edge[2] : edge[3]].reshape(width, inner),
-                down_full.transpose(0, 2, 1, 3).reshape(inner, width),
-            )
-        )
+    pieces = [gather_rel(pack, "fsdp", shards) for pack in packs]
 
     act = jax.nn.silu(conditioning).astype(bf16)
     shard_bias = jnp.concatenate([ada_bias, proj_bias, up_bias, down_bias], axis=1)
@@ -339,41 +538,33 @@
         for n in range(LAYERS)
     ]
 
-    live = (jnp.arange(slots, dtype=jnp.int32) < seq_counts[0]).astype(f32)[:, None, None]
-    saved, weights = [], []
+    length = latents.shape[1]
+    dims = (slots, length, width, triple, inner, HEADS)
+    info = jnp.stack([seq_counts[0], me.astype(jnp.int32)])
+    modulation, saved, inputs = [], [], []
     current = latents
     for n in range(LAYERS):
-        qkv_full, proj_full, up_full, down_full = fulls[n]
         ada_b, proj_b, up_b, down_b = bias_of[n]
-        weights.append((qkv_full, proj_full, proj_b, up_full, up_b, down_full, down_b))
-        saved.append(layer_parts(current, ada[n] + ada_b, weights[n]))
-        current = saved[n]["result"]
-    block_out = current * live
-    grad = cotangent * live
+        modulation.append((ada[n] + ada_b).reshape(slots, 6, width))
+        row = jnp.concatenate([proj_b, up_b, down_b])[None]
+        inputs.append(current)
+        current, *kept = forward_call(info, current, modulation[n], row, pieces[n], dims)
+        saved.append(kept)
+    block_out = current
+    grad = cotangent
 
     stages = [("dp", groups, bit) for bit in reversed(bits_of(groups))]
     stages += [("fsdp", shards, bit) for bit in reversed(bits_of(shards))]
     sums, gads, bias_rows = [None] * LAYERS, [None] * LAYERS, [None] * LAYERS
     acts = None
     for n in reversed(range(LAYERS)):
-        grad, grad_ada, bias_row, (g_qkv, g_proj, g_up, g_down) = layer_backward(
-            saved[n], weights[n], grad
+        grad, grad_ada, bias_row, stay, go = backward_call(
+            info, grad, inputs[n], modulation[n], saved[n], pieces[n], dims
         )
-        down_rows = g_down.reshape(shards, ratio * rows, width)
-        terms = []
-        for j in range(shards):
-            own = me ^ j
-            terms.append(
-                pack_rows(
-                    lax.dynamic_slice_in_dim(g_qkv, own * rows, rows, 0),
-                    lax.dynamic_slice_in_dim(g_proj, own * rows, rows, 0),
-                    lax.dynamic_slice_in_dim(g_up, own * rows, rows, 0),
-                    lax.dynamic_index_in_dim(down_rows, own, 0, keepdims=False),
-                ).astype(bf16)
-            )
-        shard = scatter_sum(terms, "fsdp", shards, bf16)
+        grad_ada = grad_ada.reshape(slots, wide)
+        shard = scatter_pair(stay, go, "fsdp", shards, bf16)
         sums[n] = all_sum(shard, "dp", groups, bf16)
-        rows_out = [grad_ada.astype(bf16), bias_row[None].astype(bf16)]
+        rows_out = [grad_ada.astype(bf16), bias_row.astype(bf16)]
         if acts is None:
             flat = act.reshape(-1)
             flat = jnp.pad(flat, (0, -flat.shape[0] % wide)).reshape(-1, wide)

time: 391 us -> 296 us (0.76); the launches traced: 387 us -> 297 us
  matrix products: 113 us -> 1.55 us
  Pallas kernels: 0 us -> 67.1 us
  local copies, waits for them, and re-layouts: 77 us -> 20.5 us
  starting transfers between devices: 33.1 us -> 55 us
  other arithmetic: 38.2 us -> 24.6 us
  waiting for transfers between devices: 121 us -> 126 us
    dot_general x20 -> x0, matrix products: 76.5 us -> none  [the longest x12 57.4 us: einsum_mixed(): return jnp.einsum(form, left, right, preferred_element_type=jnp.float32)]
    pallas_call x0 -> x4, Pallas kernels: none -> 67.1 us  [the longest x2 38.6 us: backward_call(): pl.pallas_call(functools.partial(backward_kernel, shards, heads), out_sha...]
    ppermute x38, starting transfers between devices: 33.1 us -> 55 us  [swap(): return lax.ppermute(value, axis, [(i, i ^ bit) for i in range(size)])]
    dot_general x10 -> x2, matrix products: 22 us -> 0.41 us  [matmul_back(): jnp.dot(flat, right.T, preferred_element_type=jnp.float32)]
    unnamed x313 -> x34, local copies, waits for them, and re-layouts: 26.6 us -> 5.45 us
    dot_general x10 -> x2, matrix products: 14.5 us -> 0.78 us  [outer_total(): jnp.dot(left.reshape(-1, left.shape[-1]).T, right.reshape(-1, right.shape...]
    convert_element_type x8 -> x0, local copies, waits for them, and re-layouts: 11.3 us -> none  [the longest x2 6.51 us: layer_parts(): qkv = matmul_last(attn_in, qkv_weight).astype(jnp.bfloat16)]
    dot_general x2 -> x0, local copies, waits for them, and re-layouts: 8.83 us -> none  [outer_total(): jnp.dot(left.reshape(-1, left.shape[-1]).T, right.reshape(-1, right.shape...]
  transfers between devices with their start and end apart: 38 -> 38, of which waited for: 19 -> 20; matrix products, arithmetic and copies ran while one was open for 14% -> 12% of each run, Pallas kernels for 0% -> 5%
where the time goes in v2:
time: 296 us; the launch traced here: 297 us
  waiting for transfers between devices  126 us (43%)
  Pallas kernels  67.1 us (23%)
  starting transfers between devices  55 us (19%)
  other arithmetic  24.6 us (8%)
  local copies, waits for them, and re-layouts  20.5 us (7%)
    ppermute x38, waiting for transfers between devices, swap(): return lax.ppermute(value, axis, [(i, i ^ bit) for i in range(size)])  126 us
    ppermute x38, starting transfers between devices, swap(): return lax.ppermute(value, axis, [(i, i ^ bit) for i in range(size)])  55 us
    pallas_call x2, Pallas kernels, backward_call(): pl.pallas_call(functools.partial(backward_kernel, shards, heads), out_sha...  38.6 us
    pallas_call x2, Pallas kernels, forward_call(): pl.pallas_call(functools.partial(forward_kernel, shards, heads), out_shap...  28.5 us
  transfers between devices with their start and end apart: 38, of which 20 were waited for; matrix products, arithmetic and copies ran while one was open for 12% of the time, Pallas kernels for 5%

profile of v2, /device:TPU:0, one launch (start us, length us, event | category | flops | bytes accessed | tf_op | source)
XLA Modules:
  0.0 297.3 jit_solution(18128478438900622524)
XLA Ops:
  3.3 2.6 collective-permute-start.1
  11.9 1.8 collective-permute-start.9
  19.0 33.0 %collective-permute-done.4 = f32[6,2304]{1,0:T(8,128)S(1)} collective-permute-done((f32[6,2304]{1,0:T(8,128)S(1)}, f32[6,2304]{1,0:T(8,128)S(1)}, u32[]{:S(2)}, u32[]{:S(2)}) %collective-permute-start.4) | collective-permute-done | bytes 55328 | tf_op jit(solution)/shard_map/ppermute | solution.py:389
  54.9 14.3 %block_forward.2 = (f32[3,256,384]{2,1,0:T(8,128)}, f32[3,256,384]{2,1,0:T(8,128)}, bf16[3,256,1152]{2,1,0:T(8,128)(2,1)}, bf16[3,6,256,256]{3,2,1,0:T(8,128)(2,...) custom-call(s32[2]{0:T(128)} %pad_add_fusion.info, ...), custom_call_target="tpu_custom_call" | custom-call | flops 2717908992 | bytes 18874368 | tf_op jit(solution)/shard_map/block_forward/pallas_call | solution.py:307
  69.2 14.2 %block_forward.3 = (f32[3,256,384]{2,1,0:T(8,128)}, f32[3,256,384]{2,1,0:T(8,128)}, bf16[3,256,1152]{2,1,0:T(8,128)(2,1)}, bf16[3,6,256,256]{3,2,1,0:T(8,128)(2,...) custom-call(s32[2]{0:T(128)} %pad_add_fusion.info, ...), custom_call_target="tpu_custom_call" | custom-call | flops 2717908992 | bytes 18874368 | tf_op jit(solution)/shard_map/block_forward/pallas_call | solution.py:307
  83.4 19.2 %block_backward.2 = (f32[3,256,384]{2,1,0:T(8,128)}, f32[3,6,384]{2,1,0:T(8,128)}, f32[1,2304]{1,0:T(1,128)}, bf16[2,96,4608]{2,1,0:T(8,128)(2,1)}, bf16[2,96,4608]{2,1,0:T(8,128)(2,1)}) custom-call(s32[2]{0:T(128)} %pad_add_fusion.info, f32[3,256,384]{2,1,0:T(8,128)} %grad.1, f32[3,256,384]{2,1,0:T(8,128)} %get-tuple-element.38.resid, ...), custom_call_target="tpu_custom_call" | custom-call | flops 5435817984 | bytes 18874368 | tf_op jit(solution)/shard_map/block_backward/pallas_call | solution.py:350
  104.1 19.4 %block_backward.3 = (f32[3,256,384]{2,1,0:T(8,128)}, f32[3,6,384]{2,1,0:T(8,128)}, f32[1,2304]{1,0:T(1,128)}, bf16[2,96,4608]{2,1,0:T(8,128)(2,1)}, bf16[2,96,4608]{2,1,0:T(8,128)(2,1)}) custom-call(s32[2]{0:T(128)} %pad_add_fusion.info, f32[3,256,384]{2,1,0:T(8,128)} %get-tuple-element.47.grad, f32[3,256,384]{2,1,0:T(8,128)} %resid.3, ...), custom_call_target="tpu_custom_call" | custom-call | flops 5435817984 | bytes 18874368 | tf_op jit(solution)/shard_map/block_backward/pallas_call | solution.py:350
  125.0 17.5 %collective-permute-start.11 = (bf16[1,4,2304]{2,1,0:T(4,128)(2,1)S(1)}, bf16[1,4,2304]{2,1,0:T(4,128)(2,1)S(1)}, u32[]{:S(2)}, u32[]{:S(2)}) collective-permute-start(bf16[1,4,2304]{2,1,0:T(4,128)(2,1)S(1)} %maximum_bitcast_fusion.1), channel_id=1, source_target_pairs={{0,16},{4,20},{8,24},{12,28},{16,0},{20,4},{24,8},{28,12},{1,17},{... | collective-permute-start | bytes 55304 | tf_op jit(solution)/shard_map/ppermute | solution.py:389
  144.4 2.0 collective-permute-start.12
  148.5 1.9 collective-permute-start.13
  150.4 1.6 collective-permute-done.17
  152.1 1.9 collective-permute-start.18
  155.3 2.0 collective-permute-done.18
  157.5 3.4 %collective-permute-done.14 = bf16[8,4,2304]{2,1,0:T(4,128)(2,1)S(1)} collective-permute-done((bf16[8,4,2304]{2,1,0:T(4,128)(2,1)S(1)}, bf16[8,4,2304]{2,1,0:T(4,128)(2,1)S(1)}, u32[]{:S(2)}, u32[]{:S(2)}) %collective-permute-start.14) | collective-permute-done | bytes 147488 | tf_op jit(solution)/shard_map/ppermute | solution.py:389
  161.4 3.6 %collective-permute-done.19 = bf16[8,5,2304]{2,1,0:T(8,128)(2,1)S(1)} collective-permute-done((bf16[8,5,2304]{2,1,0:T(8,128)(2,1)S(1)}, bf16[8,5,2304]{2,1,0:T(8,128)(2,1)S(1)}, u32[]{:S(2)}, u32[]{:S(2)}) %collective-permute-start.19) | collective-permute-done | bytes 184352 | tf_op jit(solution)/shard_map/ppermute | solution.py:389
  191.8 19.1 %collective-permute-done.32 = bf16[96,4608]{1,0:T(8,128)(2,1)S(1)} collective-permute-done((bf16[96,4608]{1,0:T(8,128)(2,1)S(1)}, bf16[96,4608]{1,0:T(8,128)(2,1)S(1)}, u32[]{:S(2)}, u32[]{:S(2)}) %collective-permute-start.32) | collective-permute-done | bytes 884768 | tf_op jit(solution)/shard_map/ppermute | solution.py:389
  210.9 1.5 bitcast_add_fusion
  212.4 1.8 collective-permute-start.33
  214.2 15.4 %collective-permute-done.25 = bf16[96,4608]{1,0:T(8,128)(2,1)S(1)} collective-permute-done((bf16[96,4608]{1,0:T(8,128)(2,1)S(1)}, bf16[96,4608]{1,0:T(8,128)(2,1)S(1)}, u32[]{:S(2)}, u32[]{:S(2)}) %collective-permute-start.25) | collective-permute-done | bytes 884768 | tf_op jit(solution)/shard_map/ppermute | solution.py:389
  229.6 1.5 bitcast_add_fusion.1
  231.2 1.8 collective-permute-start.26
  233.1 2.2 collective-permute-start.34
  235.3 7.9 %collective-permute-done.26 = bf16[96,2304]{1,0:T(8,128)(2,1)S(1)} collective-permute-done((bf16[96,2304]{1,0:T(8,128)(2,1)S(1)}, bf16[96,2304]{1,0:T(8,128)(2,1)S(1)}, u32[]{:S(2)}, u32[]{:S(2)}) %collective-permute-start.26) | collective-permute-done | bytes 442400 | tf_op jit(solution)/shard_map/ppermute | solution.py:389
  243.4 2.1 collective-permute-start.27
  245.6 1.5 collective-permute-start.35
  247.1 7.8 %collective-permute-done.27 = bf16[96,1152]{1,0:T(8,128)(2,1)S(1)} collective-permute-done((bf16[96,1152]{1,0:T(8,128)(2,1)S(1)}, bf16[96,1152]{1,0:T(8,128)(2,1)S(1)}, u32[]{:S(2)}, u32[]{:S(2)}) %collective-permute-start.27) | collective-permute-done | bytes 221216 | tf_op jit(solution)/shard_map/ppermute | solution.py:389
  255.6 8.4 %collective-permute-start.36 = (bf16[96,1152]{1,0:T(8,128)(2,1)S(1)}, bf16[96,1152]{1,0:T(8,128)(2,1)S(1)}, u32[]{:S(2)}, u32[]{:S(2)}) collective-permute-start(bf16[96,1152]{1,0:T(8,128)(2,1)S(1)} %add_convert_fusion.2), channel_id=1, source_target_pairs={{0,8},{4,12},{8,0},{12,4},{16,24},{20,28},{24,16},{28,20},{1,9},{5... | collective-permute-start | bytes 663560 | tf_op jit(solution)/shard_map/ppermute | solution.py:389
  263.9 3.3 %collective-permute-done.28 = bf16[96,1152]{1,0:T(8,128)(2,1)S(1)} collective-permute-done((bf16[96,1152]{1,0:T(8,128)(2,1)S(1)}, bf16[96,1152]{1,0:T(8,128)(2,1)S(1)}, u32[]{:S(2)}, u32[]{:S(2)}) %collective-permute-start.28) | collective-permute-done | bytes 221216 | tf_op jit(solution)/shard_map/ppermute | solution.py:389
  267.4 4.6 %collective-permute-done.36 = bf16[96,1152]{1,0:T(8,128)(2,1)S(1)} collective-permute-done((bf16[96,1152]{1,0:T(8,128)(2,1)S(1)}, bf16[96,1152]{1,0:T(8,128)(2,1)S(1)}, u32[]{:S(2)}, u32[]{:S(2)}) %collective-permute-start.36) | collective-permute-done | bytes 221216 | tf_op jit(solution)/shard_map/ppermute | solution.py:389
  272.2 3.8 %collective-permute-done.29 = bf16[96,1152]{1,0:T(8,128)(2,1)S(1)} collective-permute-done((bf16[96,1152]{1,0:T(8,128)(2,1)S(1)}, bf16[96,1152]{1,0:T(8,128)(2,1)S(1)}, u32[]{:S(2)}, u32[]{:S(2)}) %collective-permute-start.29) | collective-permute-done | bytes 221216 | tf_op jit(solution)/shard_map/ppermute | solution.py:389
  276.4 8.8 %collective-permute-done.37 = bf16[96,2304]{1,0:T(8,128)(2,1)S(1)} collective-permute-done((bf16[96,2304]{1,0:T(8,128)(2,1)S(1)}, bf16[96,2304]{1,0:T(8,128)(2,1)S(1)}, u32[]{:S(2)}, u32[]{:S(2)}) %collective-permute-start.37) | collective-permute-done | bytes 442400 | tf_op jit(solution)/shard_map/ppermute | solution.py:389
  285.3 7.0 %collective-permute-done.30 = bf16[96,2304]{1,0:T(8,128)(2,1)S(1)} collective-permute-done((bf16[96,2304]{1,0:T(8,128)(2,1)S(1)}, bf16[96,2304]{1,0:T(8,128)(2,1)S(1)}, u32[]{:S(2)}, u32[]{:S(2)}) %collective-permute-start.30) | collective-permute-done | bytes 442400 | tf_op jit(solution)/shard_map/ppermute | solution.py:389
  (223 shorter events, 58.3 us)
Async XLA Ops:
  2.8 9.1 %collective-permute-start = (bf16[3456]{0:T(1024)(128)(2,1)S(1)}, bf16[3456]{0:T(1024)(128)(2,1)S(1)}, u32[]{:S(2)}, u32[]{:S(2)}) collective-permute-start(bf16[3456]{0:T(1024)(128)(2,1)S(1)} %dynamic-update-slice.15), channel_id=1, source_target_pairs={{0,1},{1,0},{2,3},{3,2},{4,5},{5,4},{6,7},{7,6},{8,9},{9,8},{10,11... | collective-permute-start | bytes 20744 | tf_op jit(solution)/shard_map/ppermute | solution.py:389
  3.3 7.2 %collective-permute-start.1 = (bf16[3456]{0:T(1024)(128)(2,1)S(1)}, bf16[3456]{0:T(1024)(128)(2,1)S(1)}, u32[]{:S(2)}, u32[]{:S(2)}) collective-permute-start(bf16[3456]{0:T(1024)(128)(2,1)S(1)} %dynamic-update-slice.15), channel_id=1, source_target_pairs={{0,2},{1,3},{2,0},{3,1},{4,6},{5,7},{6,4},{7,5},{8,10},{9,11},{10,... | collective-permute-start | bytes 20744 | tf_op jit(solution)/shard_map/ppermute | solution.py:389
  9.3 44.6 %collective-permute-start.5 = (bf16[96,4608]{1,0:T(8,128)(2,1)S(1)}, bf16[96,4608]{1,0:T(8,128)(2,1)}, u32[]{:S(2)}, u32[]{:S(2)}) collective-permute-start(bf16[96,4608]{1,0:T(8,128)(2,1)S(1)} %get-tuple-element.85.rest_0_), channel_id=1, source_target_pairs={{0,1},{1,0},{2,3},{3,2},{4,5},{5,4},{6,7},{7,6},{8,9},{9,8},{10,11... | collective-permute-start | bytes 2654216 | tf_op jit(solution)/shard_map/ppermute | solution.py:389
  9.5 42.5 %collective-permute-start.6 = (bf16[96,4608]{1,0:T(8,128)(2,1)S(1)}, bf16[96,4608]{1,0:T(8,128)(2,1)}, u32[]{:S(2)}, u32[]{:S(2)}) collective-permute-start(bf16[96,4608]{1,0:T(8,128)(2,1)S(1)} %get-tuple-element.85.rest_0_), channel_id=1, source_target_pairs={{0,2},{1,3},{2,0},{3,1},{4,6},{5,7},{6,4},{7,5},{8,10},{9,11},{10,... | collective-permute-start | bytes 2654216 | tf_op jit(solution)/shard_map/ppermute | solution.py:389
  9.8 59.3 %collective-permute-start.8 = (bf16[96,4608]{1,0:T(8,128)(2,1)S(1)}, bf16[96,4608]{1,0:T(8,128)(2,1)}, u32[]{:S(2)}, u32[]{:S(2)}) collective-permute-start(bf16[96,4608]{1,0:T(8,128)(2,1)S(1)} %get-tuple-element.84.rest_0_), channel_id=1, source_target_pairs={{0,1},{1,0},{2,3},{3,2},{4,5},{5,4},{6,7},{7,6},{8,9},{9,8},{10,11... | collective-permute-start | bytes 2654216 | tf_op jit(solution)/shard_map/ppermute | solution.py:389
  11.9 40.2 %collective-permute-start.9 = (bf16[96,4608]{1,0:T(8,128)(2,1)S(1)}, bf16[96,4608]{1,0:T(8,128)(2,1)}, u32[]{:S(2)}, u32[]{:S(2)}) collective-permute-start(bf16[96,4608]{1,0:T(8,128)(2,1)S(1)} %get-tuple-element.84.rest_0_), channel_id=1, source_target_pairs={{0,2},{1,3},{2,0},{3,1},{4,6},{5,7},{6,4},{7,5},{8,10},{9,11},{10,... | collective-permute-start | bytes 2654216 | tf_op jit(solution)/shard_map/ppermute | solution.py:389
  17.2 34.8 %collective-permute-start.4 = (f32[6,2304]{1,0:T(8,128)S(1)}, f32[6,2304]{1,0:T(8,128)S(1)}, u32[]{:S(2)}, u32[]{:S(2)}) collective-permute-start(f32[6,2304]{1,0:T(8,128)S(1)} %slice_add_fusion), channel_id=1, source_target_pairs={{0,2},{1,3},{2,0},{3,1},{4,6},{5,7},{6,4},{7,5},{8,10},{9,11},{10,... | collective-permute-start | bytes 165896 | tf_op jit(solution)/shard_map/ppermute | solution.py:389
  52.1 17.1 %collective-permute-start.10 = (bf16[96,4608]{1,0:T(8,128)(2,1)}, bf16[96,4608]{1,0:T(8,128)(2,1)}, u32[]{:S(2)}, u32[]{:S(2)}) collective-permute-start(bf16[96,4608]{1,0:T(8,128)(2,1)} %collective-permute-done.9.rest_2_), channel_id=1, source_target_pairs={{0,1},{1,0},{2,3},{3,2},{4,5},{5,4},{6,7},{7,6},{8,9},{9,8},{10,11... | collective-permute-start | bytes 2654216 | tf_op jit(solution)/shard_map/ppermute | solution.py:389
  125.0 19.3 %collective-permute-start.11 = (bf16[1,4,2304]{2,1,0:T(4,128)(2,1)S(1)}, bf16[1,4,2304]{2,1,0:T(4,128)(2,1)S(1)}, u32[]{:S(2)}, u32[]{:S(2)}) collective-permute-start(bf16[1,4,2304]{2,1,0:T(4,128)(2,1)S(1)} %maximum_bitcast_fusion.1), channel_id=1, source_target_pairs={{0,16},{4,20},{8,24},{12,28},{16,0},{20,4},{24,8},{28,12},{1,17},{... | collective-permute-start | bytes 55304 | tf_op jit(solution)/shard_map/ppermute | solution.py:389
  142.6 4.9 %collective-permute-start.16 = (bf16[1,5,2304]{2,1,0:T(8,128)(2,1)S(1)}, bf16[1,5,2304]{2,1,0:T(8,128)(2,1)S(1)}, u32[]{:S(2)}, u32[]{:S(2)}) collective-permute-start(bf16[1,5,2304]{2,1,0:T(8,128)(2,1)S(1)} %maximum_bitcast_fusion), channel_id=1, source_target_pairs={{0,16},{4,20},{8,24},{12,28},{16,0},{20,4},{24,8},{28,12},{1,17},{... | collective-permute-start | bytes 69128 | tf_op jit(solution)/shard_map/ppermute | solution.py:389
  142.7 44.2 %collective-permute-start.31 = (bf16[2,96,4608]{2,1,0:T(8,128)(2,1)}, bf16[2,96,4608]{2,1,0:T(8,128)(2,1)}, u32[]{:S(2)}, u32[]{:S(2)}) collective-permute-start(bf16[2,96,4608]{2,1,0:T(8,128)(2,1)} %get-tuple-element.63), channel_id=1, source_target_pairs={{0,1},{1,0},{2,3},{3,2},{4,5},{5,4},{6,7},{7,6},{8,9},{9,8},{10,11... | collective-permute-start | bytes 5308424 | tf_op jit(solution)/shard_map/ppermute | solution.py:389
  142.8 46.5 %collective-permute-start.24 = (bf16[2,96,4608]{2,1,0:T(8,128)(2,1)}, bf16[2,96,4608]{2,1,0:T(8,128)(2,1)}, u32[]{:S(2)}, u32[]{:S(2)}) collective-permute-start(bf16[2,96,4608]{2,1,0:T(8,128)(2,1)} %get-tuple-element.61), channel_id=1, source_target_pairs={{0,1},{1,0},{2,3},{3,2},{4,5},{5,4},{6,7},{7,6},{8,9},{9,8},{10,11... | collective-permute-start | bytes 5308424 | tf_op jit(solution)/shard_map/ppermute | solution.py:389
  147.6 4.4 %collective-permute-start.17 = (bf16[2,5,2304]{2,1,0:T(8,128)(2,1)S(1)}, bf16[2,5,2304]{2,1,0:T(8,128)(2,1)S(1)}, u32[]{:S(2)}, u32[]{:S(2)}) collective-permute-start(bf16[2,5,2304]{2,1,0:T(8,128)(2,1)S(1)} %pad_maximum_fusion.12), channel_id=1, source_target_pairs={{0,8},{4,12},{8,0},{12,4},{16,24},{20,28},{24,16},{28,20},{1,9},{5... | collective-permute-start | bytes 138248 | tf_op jit(solution)/shard_map/ppermute | solution.py:389
  148.5 5.4 %collective-permute-start.13 = (bf16[4,4,2304]{2,1,0:T(4,128)(2,1)S(1)}, bf16[4,4,2304]{2,1,0:T(4,128)(2,1)S(1)}, u32[]{:S(2)}, u32[]{:S(2)}) collective-permute-start(bf16[4,4,2304]{2,1,0:T(4,128)(2,1)S(1)} %pad_maximum_fusion.11), channel_id=1, source_target_pairs={{0,4},{4,0},{8,12},{12,8},{16,20},{20,16},{24,28},{28,24},{1,5},{5... | collective-permute-start | bytes 221192 | tf_op jit(solution)/shard_map/ppermute | solution.py:389
  152.1 5.2 %collective-permute-start.18 = (bf16[4,5,2304]{2,1,0:T(8,128)(2,1)S(1)}, bf16[4,5,2304]{2,1,0:T(8,128)(2,1)S(1)}, u32[]{:S(2)}, u32[]{:S(2)}) collective-permute-start(bf16[4,5,2304]{2,1,0:T(8,128)(2,1)S(1)} %pad_maximum_fusion.10), channel_id=1, source_target_pairs={{0,4},{4,0},{8,12},{12,8},{16,20},{20,16},{24,28},{28,24},{1,5},{5... | collective-permute-start | bytes 276488 | tf_op jit(solution)/shard_map/ppermute | solution.py:389
  154.1 6.8 %collective-permute-start.14 = (bf16[8,4,2304]{2,1,0:T(4,128)(2,1)S(1)}, bf16[8,4,2304]{2,1,0:T(4,128)(2,1)S(1)}, u32[]{:S(2)}, u32[]{:S(2)}) collective-permute-start(bf16[8,4,2304]{2,1,0:T(4,128)(2,1)S(1)} %pad_maximum_fusion.9), channel_id=1, source_target_pairs={{0,2},{1,3},{2,0},{3,1},{4,6},{5,7},{6,4},{7,5},{8,10},{9,11},{10,... | collective-permute-start | bytes 442376 | tf_op jit(solution)/shard_map/ppermute | solution.py:389
  157.4 7.6 %collective-permute-start.19 = (bf16[8,5,2304]{2,1,0:T(8,128)(2,1)S(1)}, bf16[8,5,2304]{2,1,0:T(8,128)(2,1)S(1)}, u32[]{:S(2)}, u32[]{:S(2)}) collective-permute-start(bf16[8,5,2304]{2,1,0:T(8,128)(2,1)S(1)} %pad_maximum_fusion.7), channel_id=1, source_target_pairs={{0,2},{1,3},{2,0},{3,1},{4,6},{5,7},{6,4},{7,5},{8,10},{9,11},{10,... | collective-permute-start | bytes 552968 | tf_op jit(solution)/shard_map/ppermute | solution.py:389
  172.9 9.0 %collective-permute-start.21 = (f32[3,96]{1,0:T(4,128)}, f32[3,96]{1,0:T(4,128)}, u32[]{:S(2)}, u32[]{:S(2)}) collective-permute-start(f32[3,96]{1,0:T(4,128)} %bitcast.131), channel_id=1, source_target_pairs={{0,1},{1,0},{2,3},{3,2},{4,5},{5,4},{6,7},{7,6},{8,9},{9,8},{10,11... | collective-permute-start | bytes 3464 | tf_op jit(solution)/shard_map/ppermute | solution.py:389
  177.2 5.4 %collective-permute-start.22 = (f32[3,96]{1,0:T(4,128)}, f32[3,96]{1,0:T(4,128)}, u32[]{:S(2)}, u32[]{:S(2)}) collective-permute-start(f32[3,96]{1,0:T(4,128)} %bitcast.130), channel_id=1, source_target_pairs={{0,2},{1,3},{2,0},{3,1},{4,6},{5,7},{6,4},{7,5},{8,10},{9,11},{10,... | collective-permute-start | bytes 3464 | tf_op jit(solution)/shard_map/ppermute | solution.py:389
  178.7 4.6 %collective-permute-start.23 = (f32[3,96]{1,0:T(4,128)}, f32[3,96]{1,0:T(4,128)}, u32[]{:S(2)}, u32[]{:S(2)}) collective-permute-start(f32[3,96]{1,0:T(4,128)} %bitcast.129), channel_id=1, source_target_pairs={{0,3},{1,2},{2,1},{3,0},{4,7},{5,6},{6,5},{7,4},{8,11},{9,10},{10,... | collective-permute-start | bytes 3464 | tf_op jit(solution)/shard_map/ppermute | solution.py:389
  188.3 22.6 %collective-permute-start.32 = (bf16[96,4608]{1,0:T(8,128)(2,1)S(1)}, bf16[96,4608]{1,0:T(8,128)(2,1)S(1)}, u32[]{:S(2)}, u32[]{:S(2)}) collective-permute-start(bf16[96,4608]{1,0:T(8,128)(2,1)S(1)} %fusion.1), channel_id=1, source_target_pairs={{0,2},{1,3},{2,0},{3,1},{4,6},{5,7},{6,4},{7,5},{8,10},{9,11},{10,... | collective-permute-start | bytes 2654216 | tf_op jit(solution)/shard_map/ppermute | solution.py:389
  190.6 39.0 %collective-permute-start.25 = (bf16[96,4608]{1,0:T(8,128)(2,1)S(1)}, bf16[96,4608]{1,0:T(8,128)(2,1)S(1)}, u32[]{:S(2)}, u32[]{:S(2)}) collective-permute-start(bf16[96,4608]{1,0:T(8,128)(2,1)S(1)} %fusion), channel_id=1, source_target_pairs={{0,2},{1,3},{2,0},{3,1},{4,6},{5,7},{6,4},{7,5},{8,10},{9,11},{10,... | collective-permute-start | bytes 2654216 | tf_op jit(solution)/shard_map/ppermute | solution.py:389
  212.4 20.5 %collective-permute-start.33 = (bf16[96,2304]{1,0:T(8,128)(2,1)S(1)}, bf16[96,2304]{1,0:T(8,128)(2,1)S(1)}, u32[]{:S(2)}, u32[]{:S(2)}) collective-permute-start(bf16[96,2304]{1,0:T(8,128)(2,1)S(1)} %select_convert_fusion), channel_id=1, source_target_pairs={{0,4},{4,0},{8,12},{12,8},{16,20},{20,16},{24,28},{28,24},{1,5},{5... | collective-permute-start | bytes 1327112 | tf_op jit(solution)/shard_map/ppermute | solution.py:389
  231.2 12.0 %collective-permute-start.26 = (bf16[96,2304]{1,0:T(8,128)(2,1)S(1)}, bf16[96,2304]{1,0:T(8,128)(2,1)S(1)}, u32[]{:S(2)}, u32[]{:S(2)}) collective-permute-start(bf16[96,2304]{1,0:T(8,128)(2,1)S(1)} %select_convert_fusion.1), channel_id=1, source_target_pairs={{0,4},{4,0},{8,12},{12,8},{16,20},{20,16},{24,28},{28,24},{1,5},{5... | collective-permute-start | bytes 1327112 | tf_op jit(solution)/shard_map/ppermute | solution.py:389
  233.1 12.4 %collective-permute-start.34 = (bf16[96,1152]{1,0:T(8,128)(2,1)S(1)}, bf16[96,1152]{1,0:T(8,128)(2,1)S(1)}, u32[]{:S(2)}, u32[]{:S(2)}) collective-permute-start(bf16[96,1152]{1,0:T(8,128)(2,1)S(1)} %select_convert_fusion.2), channel_id=1, source_target_pairs={{0,8},{4,12},{8,0},{12,4},{16,24},{20,28},{24,16},{28,20},{1,9},{5... | collective-permute-start | bytes 663560 | tf_op jit(solution)/shard_map/ppermute | solution.py:389
  243.4 11.5 %collective-permute-start.27 = (bf16[96,1152]{1,0:T(8,128)(2,1)S(1)}, bf16[96,1152]{1,0:T(8,128)(2,1)S(1)}, u32[]{:S(2)}, u32[]{:S(2)}) collective-permute-start(bf16[96,1152]{1,0:T(8,128)(2,1)S(1)} %select_convert_fusion.3), channel_id=1, source_target_pairs={{0,8},{4,12},{8,0},{12,4},{16,24},{20,28},{24,16},{28,20},{1,9},{5... | collective-permute-start | bytes 663560 | tf_op jit(solution)/shard_map/ppermute | solution.py:389
  245.6 9.9 %collective-permute-start.35 = (bf16[96,1152]{1,0:T(8,128)(2,1)S(1)}, bf16[96,1152]{1,0:T(8,128)(2,1)S(1)}, u32[]{:S(2)}, u32[]{:S(2)}) collective-permute-start(bf16[96,1152]{1,0:T(8,128)(2,1)S(1)} %add_convert_fusion.3), channel_id=1, source_target_pairs={{0,16},{4,20},{8,24},{12,28},{16,0},{20,4},{24,8},{28,12},{1,17},{... | collective-permute-start | bytes 663560 | tf_op jit(solution)/shard_map/ppermute | solution.py:389
  255.0 12.2 %collective-permute-start.28 = (bf16[96,1152]{1,0:T(8,128)(2,1)S(1)}, bf16[96,1152]{1,0:T(8,128)(2,1)S(1)}, u32[]{:S(2)}, u32[]{:S(2)}) collective-permute-start(bf16[96,1152]{1,0:T(8,128)(2,1)S(1)} %add_convert_fusion.5), channel_id=1, source_target_pairs={{0,16},{4,20},{8,24},{12,28},{16,0},{20,4},{24,8},{28,12},{1,17},{... | collective-permute-start | bytes 663560 | tf_op jit(solution)/shard_map/ppermute | solution.py:389
  255.6 16.4 %collective-permute-start.36 = (bf16[96,1152]{1,0:T(8,128)(2,1)S(1)}, bf16[96,1152]{1,0:T(8,128)(2,1)S(1)}, u32[]{:S(2)}, u32[]{:S(2)}) collective-permute-start(bf16[96,1152]{1,0:T(8,128)(2,1)S(1)} %add_convert_fusion.2), channel_id=1, source_target_pairs={{0,8},{4,12},{8,0},{12,4},{16,24},{20,28},{24,16},{28,20},{1,9},{5... | collective-permute-start | bytes 663560 | tf_op jit(solution)/shard_map/ppermute | solution.py:389
  267.3 8.7 %collective-permute-start.29 = (bf16[96,1152]{1,0:T(8,128)(2,1)S(1)}, bf16[96,1152]{1,0:T(8,128)(2,1)S(1)}, u32[]{:S(2)}, u32[]{:S(2)}) collective-permute-start(bf16[96,1152]{1,0:T(8,128)(2,1)S(1)} %add_convert_fusion.4), channel_id=1, source_target_pairs={{0,8},{4,12},{8,0},{12,4},{16,24},{20,28},{24,16},{28,20},{1,9},{5... | collective-permute-start | bytes 663560 | tf_op jit(solution)/shard_map/ppermute | solution.py:389
  272.1 13.1 %collective-permute-start.37 = (bf16[96,2304]{1,0:T(8,128)(2,1)S(1)}, bf16[96,2304]{1,0:T(8,128)(2,1)S(1)}, u32[]{:S(2)}, u32[]{:S(2)}) collective-permute-start(bf16[96,2304]{1,0:T(8,128)(2,1)S(1)} %pad_maximum_fusion.3), channel_id=1, source_target_pairs={{0,4},{4,0},{8,12},{12,8},{16,20},{20,16},{24,28},{28,24},{1,5},{5... | collective-permute-start | bytes 1327112 | tf_op jit(solution)/shard_map/ppermute | solution.py:389
  276.1 16.2 %collective-permute-start.30 = (bf16[96,2304]{1,0:T(8,128)(2,1)S(1)}, bf16[96,2304]{1,0:T(8,128)(2,1)S(1)}, u32[]{:S(2)}, u32[]{:S(2)}) collective-permute-start(bf16[96,2304]{1,0:T(8,128)(2,1)S(1)} %pad_maximum_fusion.2), channel_id=1, source_target_pairs={{0,4},{4,0},{8,12},{12,8},{16,20},{20,16},{24,28},{28,24},{1,5},{5... | collective-permute-start | bytes 1327112 | tf_op jit(solution)/shard_map/ppermute | solution.py:389
  (16 other events, 157.8 us)

commit v3 on v1

v3 whole, which is shorter than its diff:
```python
import functools

import jax
import jax.numpy as jnp
from jax import lax
from jax.experimental import pallas as pl
from jax.experimental.pallas import tpu as pltpu
from jax.sharding import PartitionSpec as P


HEADS = 6
LAYERS = 2
VMEM_GRANT = 60 * 1024 * 1024


NORM_EPS = 1e-06
GELU_K = 0.7978845608028654
GELU_C = 0.044715


def matmul_back(left, right):
    flat = left.reshape(-1, left.shape[-1])
    return jnp.dot(flat, right.T, preferred_element_type=jnp.float32).reshape(
        left.shape[:-1] + (right.shape[0],)
    )


def outer_total(left, right):
    return jnp.dot(
        left.reshape(-1, left.shape[-1]).T,
        right.reshape(-1, right.shape[-1]),
        preferred_element_type=jnp.float32,
    )


def norm_rows(values):
    center = values - jnp.mean(values, axis=-1, keepdims=True)
    inv_std = lax.rsqrt(jnp.mean(center * center, axis=-1, keepdims=True) + NORM_EPS)
    return (center * inv_std, inv_std)


def norm_back(normed, inv_std, grad_normed):
    mean_grad = jnp.mean(grad_normed, axis=-1, keepdims=True)
    mean_prod = jnp.mean(grad_normed * normed, axis=-1, keepdims=True)
    return inv_std * (grad_normed - mean_grad - normed * mean_prod)


def silu_slope(values):
    sigm = jax.nn.sigmoid(values)
    return sigm * (1.0 + values * (1.0 - sigm))


def bits_of(size):
    assert size & (size - 1) == 0
    return [1 << k for k in range(size.bit_length() - 1)]


def swap(value, axis, size, bit):
    return lax.ppermute(value, axis, [(i, i ^ bit) for i in range(size)])


def has_bit(axis, bit):
    return (lax.axis_index(axis) & bit) != 0


def _nt(left, right):
    return lax.dot_general(
        left, right, (((1,), (1,)), ((), ())), preferred_element_type=jnp.float32
    )


def _nn(left, right):
    return jnp.dot(left, right, preferred_element_type=jnp.float32)


def _tn(left, right):
    return lax.dot_general(
        left, right, (((0,), (0,)), ((), ())), preferred_element_type=jnp.float32
    )


def lane_halves(pair):
    lane = lax.broadcasted_iota(jnp.int32, (1, pair), 1)
    first = (lane < pair // 2).astype(jnp.float32)
    return first.astype(jnp.bfloat16), (1.0 - first).astype(jnp.bfloat16)


def block_order(shards):
    bits = shards.bit_length() - 1
    return [sum(((n >> k) & 1) << (bits - 1 - k) for k in range(bits)) for n in range(shards)]


def attn_plan(pieces, w_qkv, w_proj, sems, me):
    rows = w_qkv.shape[0] // len(pieces)
    triple, width = w_qkv.shape[1], w_proj.shape[1]
    plan = [[], []]
    for j, piece in enumerate(pieces):
        at = pl.ds(pl.multiple_of((me ^ j) * rows, rows), rows)
        for n, (target, col, size) in enumerate(((w_qkv, 0, triple), (w_proj, triple, width))):
            source = piece.at[:, pl.ds(col, size)]
            plan[n].append(pltpu.make_async_copy(source, target.at[at, :], sems.at[j, n]))
    return plan


def mlp_plan(pieces, w_up, w_down, sems, me):
    rows = w_up.shape[0] // len(pieces)
    inner, width = w_down.shape
    ratio = inner // width
    plan = [[], []]
    for j, piece in enumerate(pieces):
        own = me ^ j
        at = pl.ds(pl.multiple_of(own * rows, rows), rows)
        source = piece.at[:, pl.ds(0, inner)]
        plan[0].append(pltpu.make_async_copy(source, w_up.at[at, :], sems.at[j, 0]))
        for q in range(ratio):
            at = pl.ds(pl.multiple_of((own * ratio + q) * rows, rows), rows)
            source = piece.at[:, pl.ds(inner + q * width, width)]
            plan[1].append(pltpu.make_async_copy(source, w_down.at[at, :], sems.at[j, 1 + q]))
    return plan


def start_all(plan):
    for group in plan:
        for copy in group:
            copy.start()


def wait_first(slot, group):
    @pl.when(slot == 0)
    def _():
        for copy in group:
            copy.wait()


def forward_body(slot, heads, value, mods, biases, weights, plans, saved):
    w_qkv, w_proj, w_up, w_down = weights
    one_out, qkv, probs_out, mixed, attn_out, hidden_out, slope_out, branch_out = saved
    bf16 = jnp.bfloat16
    width, inner = w_proj.shape[1], w_up.shape[1]
    normed, _ = norm_rows(value)
    attn_in = (normed * (1.0 + mods[1:2]) + mods[0:1]).astype(bf16)
    wait_first(slot, plans[0][0])
    qkv[...] = _nn(attn_in, w_qkv[...]).astype(bf16)
    pair = 2 * width // heads
    scale = 1.0 / (width // heads) ** 0.5
    masks = lane_halves(pair)
    for p in range(heads // 2):
        query = qkv[:, p * pair : (p + 1) * pair]
        key = qkv[:, width + p * pair : width + (p + 1) * pair]
        val = qkv[:, 2 * width + p * pair : 2 * width + (p + 1) * pair]
        total = None
        for h in range(2):
            scores = _nt(query * masks[h], key) * scale
            expo = jnp.exp(scores - jnp.max(scores, axis=-1, keepdims=True))
            probs = (expo * (1.0 / jnp.sum(expo, axis=-1, keepdims=True))).astype(bf16)
            probs_out[2 * p + h] = probs
            term = _nn(probs, val * masks[h])
            total = term if total is None else total + term
        mixed[:, p * pair : (p + 1) * pair] = total.astype(bf16)
    wait_first(slot, plans[0][1])
    attn = _nn(mixed[...], w_proj[...]) + biases[:, :width]
    attn_out[...] = attn.astype(bf16)
    one = value + mods[2:3] * attn
    one_out[...] = one
    normed, _ = norm_rows(one)
    mlp_in = (normed * (1.0 + mods[4:5]) + mods[3:4]).astype(bf16)
    wait_first(slot, plans[1][0])
    u = _nn(mlp_in, w_up[...]) + biases[:, width : width + inner]
    square = u * u
    tangent = jnp.tanh(GELU_K * (u + GELU_C * square * u))
    half = 0.5 * (1.0 + tangent)
    hidden_out[...] = (u * half).astype(bf16)
    slope = half + 0.5 * u * (1.0 - tangent * tangent) * (
        GELU_K + (3.0 * GELU_C * GELU_K) * square
    )
    slope_out[...] = slope.astype(bf16)
    wait_first(slot, plans[1][1])
    branch = _nn(hidden_out[...], w_down[...]) + biases[:, width + inner :]
    branch_out[...] = branch.astype(bf16)
    return one + mods[5:6] * branch


def mlp_back_body(slot, g, mods, one, hidden, slope, branch, weights, plan, sums, gada, bias_up, bias_down):
    w_up, w_down = weights
    a_up, a_down = sums
    f32, bf16 = jnp.float32, jnp.bfloat16
    gada[2:3, :] = jnp.sum(g * branch[...].astype(f32), axis=0, keepdims=True)
    gbranch = g * mods[5:6]
    bias_down[...] += jnp.sum(gbranch, axis=0, keepdims=True)
    gb = gbranch.astype(bf16)
    a_down[...] += _tn(hidden[...], gb)
    wait_first(slot, plan[1])
    gpre = _nt(gb, w_down[...]) * slope[...].astype(f32)
    bias_up[...] += jnp.sum(gpre, axis=0, keepdims=True)
    gp = gpre.astype(bf16)
    normed, inv = norm_rows(one[...])
    mlp_in = (normed * (1.0 + mods[4:5]) + mods[3:4]).astype(bf16)
    a_up[...] += _tn(mlp_in, gp)
    wait_first(slot, plan[0])
    gmlp = _nt(gp, w_up[...])
    gada[0:1, :] = jnp.sum(gmlp, axis=0, keepdims=True)
    gada[1:2, :] = jnp.sum(gmlp * normed, axis=0, keepdims=True)
    return g + norm_back(normed, inv, gmlp * (1.0 + mods[4:5]))


def attn_back_body(slot, heads, g1, mods, resid, qkv, probs, mixed, attn, weights, plan, sums, g_heads, gada, bias_proj):
    w_qkv, w_proj = weights
    a_qkv, a_proj = sums
    f32, bf16 = jnp.float32, jnp.bfloat16
    width = w_proj.shape[1]
    gada[2:3, :] = jnp.sum(g1 * attn[...].astype(f32), axis=0, keepdims=True)
    gattn = g1 * mods[2:3]
    bias_proj[...] += jnp.sum(gattn, axis=0, keepdims=True)
    ga = gattn.astype(bf16)
    a_proj[...] += _tn(mixed[...], ga)
    wait_first(slot, plan[1])
    gmixed = _nt(ga, w_proj[...]).astype(bf16)
    pair = 2 * width // heads
    scale = 1.0 / (width // heads) ** 0.5
    masks = lane_halves(pair)
    for p in range(heads // 2):
        query = qkv[:, p * pair : (p + 1) * pair]
        key = qkv[:, width + p * pair : width + (p + 1) * pair]
        val = qkv[:, 2 * width + p * pair : 2 * width + (p + 1) * pair]
        gm = gmixed[:, p * pair : (p + 1) * pair]
        gq, gk, gv = 0.0, 0.0, 0.0
        for h in range(2):
            low = probs[2 * p + h]
            gm_h = gm * masks[h]
            gprobs = _nt(gm_h, val)
            full = low.astype(f32)
            dot = jnp.sum(full * gprobs, axis=-1, keepdims=True)
            gscores = (full * (gprobs - dot) * scale).astype(bf16)
            gv = gv + _tn(low, gm_h)
            gq = gq + _nn(gscores, key * masks[h])
            gk = gk + _tn(gscores, query * masks[h])
        g_heads[:, p * pair : (p + 1) * pair] = gq.astype(bf16)
        g_heads[:, width + p * pair : width + (p + 1) * pair] = gk.astype(bf16)
        g_heads[:, 2 * width + p * pair : 2 * width + (p + 1) * pair] = gv.astype(bf16)
    normed, inv = norm_rows(resid)
    attn_in = (normed * (1.0 + mods[1:2]) + mods[0:1]).astype(bf16)
    a_qkv[...] += _tn(attn_in, g_heads[...])
    wait_first(slot, plan[0])
    gin = _nt(g_heads[...], w_qkv[...])
    gada[0:1, :] = jnp.sum(gin, axis=0, keepdims=True)
    gada[1:2, :] = jnp.sum(gin * normed, axis=0, keepdims=True)
    return g1 + norm_back(normed, inv, gin * (1.0 + mods[1:2]))


def emit_attn(shards, me, a_qkv, a_proj, keep, send):
    rows, triple = a_qkv.shape[0] // shards, a_qkv.shape[1]
    for n, j in enumerate(block_order(shards)):
        out, row = (keep, n) if n < shards // 2 else (send, n - shards // 2)
        at = pl.ds(pl.multiple_of((me ^ j) * rows, rows), rows)
        out[row, :, :triple] = a_qkv[at, :].astype(jnp.bfloat16)
        out[row, :, triple:] = a_proj[at, :].astype(jnp.bfloat16)


def emit_mlp(shards, me, a_up, a_down, keep, send):
    rows, inner = a_up.shape[0] // shards, a_up.shape[1]
    width = a_down.shape[1]
    ratio = inner // width
    for n, j in enumerate(block_order(shards)):
        out, row = (keep, n) if n < shards // 2 else (send, n - shards // 2)
        own = me ^ j
        at = pl.ds(pl.multiple_of(own * rows, rows), rows)
        out[row, :, :inner] = a_up[at, :].astype(jnp.bfloat16)
        for q in range(ratio):
            at = pl.ds(pl.multiple_of((own * ratio + q) * rows, rows), rows)
            col = inner + q * width
            out[row, :, col : col + width] = a_down[at, :].astype(jnp.bfloat16)


def clear(*refs):
    for ref in refs:
        ref[...] = jnp.zeros_like(ref[...])


def forward_kernel(shards, heads, info, resid, ada, biases, *rest):
    attn_pieces, mlp_pieces, rest = rest[:shards], rest[shards : 2 * shards], rest[2 * shards :]
    result, saved, rest = rest[0], rest[1:9], rest[9:]
    w_qkv, w_proj, w_up, w_down, attn_sems, mlp_sems = rest
    slot = pl.program_id(0)
    plans = (
        attn_plan(attn_pieces, w_qkv, w_proj, attn_sems, info[1]),
        mlp_plan(mlp_pieces, w_up, w_down, mlp_sems, info[1]),
    )

    @pl.when(slot == 0)
    def _():
        start_all(plans[0])
        start_all(plans[1])

    @pl.when(slot < info[0])
    def _():
        result[0] = forward_body(
            slot,
            heads,
            resid[0],
            ada[0],
            biases,
            (w_qkv, w_proj, w_up, w_down),
            plans,
            [ref.at[0] for ref in saved],
        )

    @pl.when(slot >= info[0])
    def _():
        clear(result)


def last_block_kernel(shards, heads, info, resid, grad, ada, biases, *rest):
    attn_pieces, mlp_pieces, rest = rest[:shards], rest[shards : 2 * shards], rest[2 * shards :]
    result, grad_out, gada_attn, gada_mlp, bias_proj, bias_up, bias_down = rest[:7]
    attn_keep, attn_send, mlp_keep, mlp_send = rest[7:11]
    w_qkv, w_proj, w_up, w_down, a_qkv, a_proj, a_up, a_down, g_heads = rest[11:20]
    saved, attn_sems, mlp_sems = rest[20:28], rest[28], rest[29]
    one, qkv, probs, mixed, attn, hidden, slope, branch = saved
    slot, me = pl.program_id(0), info[1]
    plans = (
        attn_plan(attn_pieces, w_qkv, w_proj, attn_sems, me),
        mlp_plan(mlp_pieces, w_up, w_down, mlp_sems, me),
    )
    done = [[], []]

    @pl.when(slot == 0)
    def _():
        start_all(plans[0])
        start_all(plans[1])
        clear(a_qkv, a_proj, a_up, a_down, bias_proj, bias_up, bias_down)

    @pl.when(slot < info[0])
    def _():
        mods, value = ada[0], resid[0]
        weights = (w_qkv, w_proj, w_up, w_down)
        result[0] = forward_body(slot, heads, value, mods, biases, weights, plans, saved)
        g1 = mlp_back_body(
            slot, grad[0], mods, one, hidden, slope, branch, weights[2:], done, (a_up, a_down),
            gada_mlp.at[0], bias_up, bias_down,
        )
        grad_out[0] = attn_back_body(
            slot, heads, g1, mods, value, qkv, probs, mixed, attn, weights[:2], done,
            (a_qkv, a_proj), g_heads, gada_attn.at[0], bias_proj,
        )

    @pl.when(slot >= info[0])
    def _():
        clear(result, grad_out, gada_attn, gada_mlp)

    @pl.when(slot == pl.num_programs(0) - 1)
    def _():
        emit_attn(shards, me, a_qkv, a_proj, attn_keep, attn_send)
        emit_mlp(shards, me, a_up, a_down, mlp_keep, mlp_send)


def mlp_back_kernel(shards, heads, info, grad, ada, one, hidden, slope, branch, *rest):
    pieces, rest = rest[:shards], rest[shards:]
    grad_out, gada, bias_up, bias_down, keep, send, w_up, w_down, a_up, a_down, sems = rest
    slot, me = pl.program_id(0), info[1]
    plan = mlp_plan(pieces, w_up, w_down, sems, me)

    @pl.when(slot == 0)
    def _():
        start_all(plan)
        clear(a_up, a_down, bias_up, bias_down)

    @pl.when(slot < info[0])
    def _():
        grad_out[0] = mlp_back_body(
            slot, grad[0], ada[0], one.at[0], hidden.at[0], slope.at[0], branch.at[0],
            (w_up, w_down), plan, (a_up, a_down), gada.at[0], bias_up, bias_down,
        )

    @pl.when(slot >= info[0])
    def _():
        clear(gada)

    @pl.when(slot == pl.num_programs(0) - 1)
    def _():
        emit_mlp(shards, me, a_up, a_down, keep, send)


def attn_back_kernel(shards, heads, info, grad, resid, ada, qkv, probs, mixed, attn, *rest):
    pieces, rest = rest[:shards], rest[shards:]
    grad_out, gada, bias_proj, keep, send, w_qkv, w_proj, a_qkv, a_proj, g_heads, sems = rest
    slot, me = pl.program_id(0), info[1]
    plan = attn_plan(pieces, w_qkv, w_proj, sems, me)

    @pl.when(slot == 0)
    def _():
        start_all(plan)
        clear(a_qkv, a_proj, bias_proj)

    @pl.when(slot < info[0])
    def _():
        grad_out[0] = attn_back_body(
            slot, heads, grad[0], ada[0], resid[0], qkv.at[0], probs.at[0], mixed.at[0],
            attn.at[0], (w_qkv, w_proj), plan, (a_qkv, a_proj), g_heads, gada.at[0], bias_proj,
        )

    @pl.when(slot >= info[0])
    def _():
        clear(grad_out, gada)

    @pl.when(slot == pl.num_programs(0) - 1)
    def _():
        emit_attn(shards, me, a_qkv, a_proj, keep, send)


def per_slot(shape):
    rest = (0,) * (len(shape) - 1)
    return pl.BlockSpec((1,) + tuple(shape[1:]), lambda slot, info: (slot,) + rest)


def whole_block(shape):
    zeros = (0,) * len(shape)
    return pl.BlockSpec(tuple(shape), lambda slot, info: zeros)


def run_kernel(kernel, dims, info, blocked, fixed, pieces, outs, fixed_outs, scratch, passes):
    slots, length, width, triple, inner, heads, shards = dims
    shapes = list(outs) + list(fixed_outs)
    return pl.pallas_call(
        functools.partial(kernel, shards, heads),
        out_shape=[jax.ShapeDtypeStruct(s, d) for s, d in shapes],
        grid_spec=pltpu.PrefetchScalarGridSpec(
            num_scalar_prefetch=1,
            grid=(slots,),
            in_specs=[per_slot(a.shape) for a in blocked]
            + [whole_block(a.shape) for a in fixed]
            + [pl.BlockSpec(memory_space=pl.ANY)] * len(pieces),
            out_specs=[per_slot(s) for s, _ in outs] + [whole_block(s) for s, _ in fixed_outs],
            scratch_shapes=scratch,
        ),
        compiler_params=pltpu.CompilerParams(vmem_limit_bytes=VMEM_GRANT),
        cost_estimate=pl.CostEstimate(
            flops=passes * slots * length * width * (triple + width + 2 * inner),
            bytes_accessed=passes * slots * length * inner * 4,
            transcendentals=slots * length * inner,
        ),
    )(info, *blocked, *fixed, *pieces)


def kernel_parts(dims):
    slots, length, width, triple, inner, heads, shards = dims
    f32, bf16 = jnp.float32, jnp.bfloat16
    rows, ratio = width // shards, inner // width
    saved = [
        ((length, width), f32),
        ((length, triple), bf16),
        ((heads, length, length), bf16),
        ((length, width), bf16),
        ((length, width), bf16),
        ((length, inner), bf16),
        ((length, inner), bf16),
        ((length, width), bf16),
    ]
    w_attn = [pltpu.VMEM((width, triple), bf16), pltpu.VMEM((width, width), bf16)]
    w_mlp = [pltpu.VMEM((width, inner), bf16), pltpu.VMEM((inner, width), bf16)]
    a_attn = [pltpu.VMEM((width, triple), f32), pltpu.VMEM((width, width), f32)]
    a_mlp = [pltpu.VMEM((width, inner), f32), pltpu.VMEM((inner, width), f32)]
    heads_buf = [pltpu.VMEM((length, triple), bf16)]
    sems = [pltpu.SemaphoreType.DMA((shards, 2)), pltpu.SemaphoreType.DMA((shards, 1 + ratio))]
    rows_of = ((slots, length, width), f32)
    gada = ((slots, 3, width), f32)
    bias = [((1, width), f32), ((1, inner), f32), ((1, width), f32)]
    half = (shards // 2, rows)
    out_attn = [(half + (triple + width,), bf16)] * 2
    out_mlp = [(half + (2 * inner,), bf16)] * 2
    return saved, w_attn, w_mlp, a_attn, a_mlp, heads_buf, sems, rows_of, gada, bias, out_attn, out_mlp


def forward_call(dims, info, resid, ada, biases, attn_pieces, mlp_pieces):
    saved, w_attn, w_mlp, _, _, _, sems, rows_of, *_ = kernel_parts(dims)
    outs = [rows_of] + [((dims[0],) + s, d) for s, d in saved]
    return run_kernel(
        forward_kernel, dims, info, (resid, ada), (biases,),
        attn_pieces + mlp_pieces, outs, [], w_attn + w_mlp + sems, 2,
    )


def last_block_call(dims, info, resid, grad, ada, biases, attn_pieces, mlp_pieces):
    parts = kernel_parts(dims)
    saved, w_attn, w_mlp, a_attn, a_mlp, heads_buf, sems, rows_of, gada, bias, out_attn, out_mlp = parts
    scratch = w_attn + w_mlp + a_attn + a_mlp + heads_buf
    scratch += [pltpu.VMEM(s, d) for s, d in saved] + sems
    return run_kernel(
        last_block_kernel, dims, info, (resid, grad, ada), (biases,),
        attn_pieces + mlp_pieces, [rows_of, rows_of, gada, gada], bias + out_attn + out_mlp,
        scratch, 6,
    )


def mlp_back_call(dims, info, grad, ada, one, hidden, slope, branch, pieces):
    parts = kernel_parts(dims)
    _, _, w_mlp, _, a_mlp, _, sems, rows_of, gada, bias, _, out_mlp = parts
    return run_kernel(
        mlp_back_kernel, dims, info, (grad, ada, one, hidden, slope, branch), (),
        pieces, [rows_of, gada], bias[1:] + out_mlp, w_mlp + a_mlp + sems[1:], 2,
    )


def attn_back_call(dims, info, grad, resid, ada, qkv, probs, mixed, attn, pieces):
    parts = kernel_parts(dims)
    _, w_attn, _, a_attn, _, heads_buf, sems, rows_of, gada, bias, out_attn, _ = parts
    return run_kernel(
        attn_back_kernel, dims, info,
        (grad, resid, ada, qkv, probs, mixed, attn), (), pieces, [rows_of, gada],
        bias[:1] + out_attn, w_attn + a_attn + heads_buf + sems[:1], 2,
    )


def gather_rel(value, axis, size):
    pieces = {0: value}
    for bit in reversed(bits_of(size)):
        for j in list(pieces):
            pieces[j ^ bit] = swap(pieces[j], axis, size, bit)
    return [pieces[j] for j in range(size)]


def gather_all(value, stages):
    for axis, size, bit in stages:
        other = swap(value, axis, size, bit)
        upper = has_bit(axis, bit)
        value = jnp.concatenate(
            [jnp.where(upper, other, value), jnp.where(upper, value, other)], axis=0
        )
    return value


def to_absolute(pieces, axis):
    me = lax.axis_index(axis)
    out = jnp.zeros((len(pieces),) + pieces[0].shape, pieces[0].dtype)
    for j, piece in enumerate(pieces):
        out = lax.dynamic_update_index_in_dim(out, piece, me ^ j, 0)
    return out


def scatter_sum(blocks, axis, size):
    blocks = dict(enumerate(blocks))
    for bit in bits_of(size):
        keep = [j for j in blocks if not j & bit]
        got = swap(jnp.stack([blocks[j | bit] for j in keep]), axis, size, bit)
        blocks = {j: blocks[j] + got[n] for n, j in enumerate(keep)}
    return blocks[0]


def reduce_message(kept, sent, plan):
    f32, wire = jnp.float32, kept.dtype
    value, trail = kept, []
    for n, (axis, size, bit, kind) in enumerate(plan):
        if kind == "rows":
            if n == 0:
                stay, go = kept, sent
            else:
                half = value.shape[0] // 2
                stay, go = value[:half], value[half:]
        elif kind == "columns":
            half = value.shape[-1] // 2
            upper = has_bit(axis, bit)
            low, high = value[..., :half], value[..., half:]
            stay, go = jnp.where(upper, high, low), jnp.where(upper, low, high)
            trail.append((axis, size, bit))
        else:
            stay, go = value, value
        got = swap(go, axis, size, bit)
        value = (stay.astype(f32) + got.astype(f32)).astype(wire)
    value = value[0]
    for axis, size, bit in reversed(trail):
        other = swap(value, axis, size, bit)
        upper = has_bit(axis, bit)
        value = jnp.concatenate(
            [jnp.where(upper, other, value), jnp.where(upper, value, other)], axis=-1
        )
    return value


def message_plan(groups, shards, columns, dp_early):
    shard_stages = [("fsdp", shards, bit, "rows") for bit in bits_of(shards)]
    group_stages = []
    for bit in bits_of(groups):
        if 2 * bit < groups and (columns // 2) % 128 == 0:
            columns //= 2
            group_stages.append(("dp", groups, bit, "columns"))
        else:
            group_stages.append(("dp", groups, bit, "full"))
    if dp_early:
        return shard_stages[:1] + group_stages[:1] + shard_stages[1:] + group_stages[1:]
    return shard_stages + group_stages


def on_device(
    sizes,
    latents,
    conditioning,
    seq_counts,
    cotangent,
    ada_weight,
    ada_bias,
    qkv_weight,
    proj_weight,
    proj_bias,
    up_weight,
    up_bias,
    down_weight,
    down_bias,
):
    groups, shards = sizes
    bf16, f32 = jnp.bfloat16, jnp.float32
    slots, length, width = latents.shape
    rows = qkv_weight.shape[1]
    triple, inner = qkv_weight.shape[2], up_weight.shape[2]
    wide = ada_weight.shape[2]
    ratio = inner // width
    me = lax.axis_index("fsdp")
    shard_stages = [("fsdp", shards, bit) for bit in bits_of(shards)]

    act = jax.nn.silu(conditioning).astype(bf16)
    shard_bias = jnp.concatenate([ada_bias, proj_bias, up_bias, down_bias], axis=1)
    bias_width = shard_bias.shape[1]
    small = jnp.concatenate([act.reshape(-1), shard_bias.reshape(-1)])[None]
    small = gather_all(small, shard_stages)

    attn_pieces, mlp_pieces = [], []
    for n in range(LAYERS):
        pack = jnp.concatenate([qkv_weight[n], proj_weight[n]], axis=1)
        attn_pieces.append(gather_rel(pack, "fsdp", shards))
        blocks = [down_weight[n, q * rows : (q + 1) * rows] for q in range(ratio)]
        pack = jnp.concatenate([up_weight[n]] + blocks, axis=1)
        mlp_pieces.append(gather_rel(pack, "fsdp", shards))

    act_group = small[:, : slots * width].reshape(shards * slots, width)
    biases = small[:, slots * width :].reshape(shards, LAYERS, bias_width)
    act_cols = lax.dynamic_slice(act_group, (0, me * rows), (shards * slots, rows))
    partial = jnp.stack(
        [jnp.dot(act_cols, ada_weight[n], preferred_element_type=f32) for n in range(LAYERS)]
    ).reshape(LAYERS, shards, slots, wide)
    blocks = [
        lax.dynamic_index_in_dim(partial, me ^ j, 1, keepdims=False).reshape(LAYERS * slots, wide)
        for j in range(shards)
    ]
    ada = scatter_sum(blocks, "fsdp", shards).reshape(LAYERS, slots, wide)
    cut = [0]
    for part in (ada_bias, proj_bias, up_bias, down_bias):
        cut.append(cut[-1] + part.shape[1])
    bias_of = [
        [biases[:, n, cut[k] : cut[k + 1]].reshape(-1).astype(f32) for k in range(4)]
        for n in range(LAYERS)
    ]
    modulation = [(ada[n] + bias_of[n][0]).reshape(slots, 6, width) for n in range(LAYERS)]
    bias_rows = [jnp.concatenate(bias_of[n][1:])[None] for n in range(LAYERS)]

    dims = (slots, length, width, triple, inner, HEADS, shards)
    info = jnp.stack([seq_counts[0], me.astype(jnp.int32)])
    top = LAYERS - 1
    inputs, saved = [], []
    current = latents
    for n in range(top):
        inputs.append(current)
        current, *kept = forward_call(
            dims, info, current, modulation[n], bias_rows[n], attn_pieces[n], mlp_pieces[n]
        )
        saved.append(kept)
    sums = [None] * LAYERS
    small_rows = [None] * LAYERS
    attn_stages = message_plan(groups, shards, triple + width, True)
    mlp_stages = message_plan(groups, shards, 2 * inner, False)

    def reduce_layer(n, attn_pair, mlp_pair):
        mlp = reduce_message(*mlp_pair, mlp_stages)
        attn = reduce_message(*attn_pair, attn_stages)
        sums[n] = (attn, mlp)

    def note_rows(n, gada_attn, gada_mlp, bias_grads):
        flat = jnp.concatenate([gada_attn, gada_mlp], axis=1).reshape(slots, wide)
        small_rows[n] = jnp.concatenate([flat, jnp.concatenate(bias_grads, axis=1)], axis=0)

    outs = last_block_call(
        dims, info, current, cotangent, modulation[top], bias_rows[top],
        attn_pieces[top], mlp_pieces[top],
    )
    block_out, grad, gada_attn, gada_mlp, b_proj, b_up, b_down = outs[:7]
    reduce_layer(top, outs[7:9], outs[9:11])
    note_rows(top, gada_attn, gada_mlp, (b_proj, b_up, b_down))
    for n in reversed(range(top)):
        one, qkv, probs, mixed, attn, hidden, slope, branch = saved[n]
        g1, gada_mlp, b_up, b_down, *mlp_pair = mlp_back_call(
            dims, info, grad, modulation[n], one, hidden, slope, branch, mlp_pieces[n]
        )
        grad, gada_attn, b_proj, *attn_pair = attn_back_call(
            dims, info, g1, inputs[n], modulation[n], qkv, probs, mixed, attn, attn_pieces[n]
        )
        reduce_layer(n, attn_pair, mlp_pair)
        note_rows(n, gada_attn, gada_mlp, (b_proj, b_up, b_down))

    flat = act.reshape(-1)
    flat = jnp.pad(flat, (0, -flat.shape[0] % wide)).reshape(-1, wide)
    message = jnp.concatenate([row.astype(bf16) for row in small_rows] + [flat], axis=0)
    stages = [("dp", groups, bit) for bit in reversed(bits_of(groups))]
    stages += [("fsdp", shards, bit) for bit in reversed(bits_of(shards))]
    every = gather_all(message[None], stages)
    per_layer = slots + 1
    gads = [every[:, n * per_layer : n * per_layer + slots] for n in range(LAYERS)]
    acts = every[:, LAYERS * per_layer :].reshape(every.shape[0], -1)[:, : slots * width]
    acts = acts.reshape(-1, width)
    acts_cols = lax.dynamic_slice(acts, (0, me * rows), (acts.shape[0], rows))
    g_ada = jnp.stack([outer_total(acts_cols, gads[n].reshape(-1, wide)) for n in range(LAYERS)])
    totals = jnp.sum(every[:, : LAYERS * per_layer].astype(f32), axis=0)
    totals = totals.reshape(LAYERS, per_layer, wide)
    g_ada_bias = jnp.sum(totals[:, :slots], axis=1)
    g_bias = totals[:, slots]

    place = jnp.int32(0)
    for k, bit in enumerate(reversed(bits_of(groups))):
        place = place + has_bit("dp", bit).astype(jnp.int32) * (1 << k)
    grid = every.reshape((shards, groups) + every.shape[1:])
    mine = lax.dynamic_index_in_dim(grid, place, 1, keepdims=False)
    total = 0.0
    for n in range(LAYERS):
        part = mine[:, n * per_layer : n * per_layer + slots].reshape(-1, wide)
        total = total + matmul_back(part, ada_weight[n])
    total = total.reshape([2] * len(bits_of(shards)) + [slots, rows])
    order = tuple(reversed(range(len(bits_of(shards)))))
    total = total.transpose(order + (len(order), len(order) + 1)).reshape(shards, slots, rows)
    got = [lax.dynamic_index_in_dim(total, me, 0, keepdims=False)]
    for j in range(1, shards):
        sent = lax.dynamic_index_in_dim(total, me ^ j, 0, keepdims=False)
        got.append(swap(sent, "fsdp", shards, j))
    grad_cond = to_absolute(got, "fsdp").transpose(1, 0, 2).reshape(slots, width)
    grad_cond = grad_cond * silu_slope(conditioning)

    def stacked(k, first, last):
        return jnp.stack([sums[n][k][:, first:last] for n in range(LAYERS)]).astype(f32)

    down_sum = jnp.stack(
        [
            jnp.concatenate(
                [
                    sums[n][1][:, inner + q * width : inner + (q + 1) * width]
                    for q in range(ratio)
                ],
                axis=0,
            )
            for n in range(LAYERS)
        ]
    ).astype(f32)
    own_inner = inner // shards
    return (
        block_out,
        grad,
        grad_cond,
        g_ada,
        lax.dynamic_slice_in_dim(g_ada_bias, me * (wide // shards), wide // shards, 1),
        stacked(0, 0, triple),
        stacked(0, triple, triple + width),
        lax.dynamic_slice_in_dim(g_bias, me * rows, rows, 1),
        stacked(1, 0, inner),
        lax.dynamic_slice_in_dim(g_bias, width + me * own_inner, own_inner, 1),
        down_sum,
        lax.dynamic_slice_in_dim(g_bias, width + inner + me * rows, rows, 1),
    )


def solution(mesh):
    in_specs = (
        P(("dp", "fsdp"), None, None),
        P(("dp", "fsdp"), None),
        P(("dp", "fsdp")),
        P(("dp", "fsdp"), None, None),
        P(None, "fsdp", None),
        P(None, "fsdp"),
        P(None, "fsdp", None),
        P(None, "fsdp", None),
        P(None, "fsdp"),
        P(None, "fsdp", None),
        P(None, "fsdp"),
        P(None, "fsdp", None),
        P(None, "fsdp"),
    )
    out_specs = (
        P(("dp", "fsdp"), None, None),
        P(("dp", "fsdp"), None, None),
        P(("dp", "fsdp"), None),
        P(None, "fsdp", None),
        P(None, "fsdp"),
        P(None, "fsdp", None),
        P(None, "fsdp", None),
        P(None, "fsdp"),
        P(None, "fsdp", None),
        P(None, "fsdp"),
        P(None, "fsdp", None),
        P(None, "fsdp"),
    )
    sizes = (mesh.shape["dp"], mesh.shape["fsdp"])
    return jax.shard_map(
        functools.partial(on_device, sizes),
        mesh=mesh,
        in_specs=in_specs,
        out_specs=out_specs,
        check_vma=False,
    )
```

time: 391 us -> 290 us (0.74)
  matrix products: 113 us -> 3.58 us
  Pallas kernels: 0 us -> 78.5 us
  local copies, waits for them, and re-layouts: 77 us -> 25.2 us
  waiting for transfers between devices: 121 us -> 101 us
  starting transfers between devices: 33.1 us -> 51.8 us
  other arithmetic: 38.2 us -> 25.9 us
    pallas_call x0 -> x4, Pallas kernels: none -> 78.5 us  [run_kernel(): pl.pallas_call(functools.partial(kernel, shards, heads), out_shape=[jax.S...]
    dot_general x20 -> x0, matrix products: 76.5 us -> none  [the longest x12 57.4 us: einsum_mixed(): return jnp.einsum(form, left, right, preferred_element_type=jnp.float32)]
    ppermute x38 -> x52, waiting for transfers between devices: 121 us -> 101 us  [swap(): return lax.ppermute(value, axis, [(i, i ^ bit) for i in range(size)])]
    dot_general x10 -> x2, matrix products: 22 us -> 2.44 us  [matmul_back(): jnp.dot(flat, right.T, preferred_element_type=jnp.float32)]
    ppermute x38 -> x52, starting transfers between devices: 33.1 us -> 51.8 us  [swap(): return lax.ppermute(value, axis, [(i, i ^ bit) for i in range(size)])]
    unnamed x313 -> x99, local copies, waits for them, and re-layouts: 26.6 us -> 7.97 us
    dot_general x10 -> x2, matrix products: 14.5 us -> 0.78 us  [outer_total(): jnp.dot(left.reshape(-1, left.shape[-1]).T, right.reshape(-1, right.shape...]
    convert_element_type x8 -> x0, local copies, waits for them, and re-layouts: 11.3 us -> none  [the longest x2 6.51 us: layer_parts(): qkv = matmul_last(attn_in, qkv_weight).astype(jnp.bfloat16)]
  transfers between devices with their start and end apart: 38 -> 52, of which waited for: 19 -> 25; matrix products, arithmetic and copies ran while one was open for 14% -> 15% of each run, Pallas kernels for 0% -> 7%
where the time goes in v3:
time: 290 us; the launch traced here: 289 us
  waiting for transfers between devices  101 us (35%)
  Pallas kernels  78.5 us (27%)
  starting transfers between devices  51.8 us (18%)
  other arithmetic  25.9 us (9%)
  local copies, waits for them, and re-layouts  25.2 us (9%)
  matrix products  3.58 us (1%)
    ppermute x52, waiting for transfers between devices, swap(): return lax.ppermute(value, axis, [(i, i ^ bit) for i in range(size)])  101 us
    pallas_call x4, Pallas kernels, run_kernel(): pl.pallas_call(functools.partial(kernel, shards, heads), out_shape=[jax.S...  78.5 us
    ppermute x52, starting transfers between devices, swap(): return lax.ppermute(value, axis, [(i, i ^ bit) for i in range(size)])  51.8 us
    unnamed x99, local copies, waits for them, and re-layouts  7.97 us
  transfers between devices with their start and end apart: 52, of which 25 were waited for; matrix products, arithmetic and copies ran while one was open for 15% of the time, Pallas kernels for 7%

profile of v3, /device:TPU:0, one launch (start us, length us, event | category | flops | bytes accessed | tf_op | source)
XLA Modules:
  0.0 289.2 jit_solution(16849757401053777510)
XLA Ops:
  0.7 1.9 bitcast_dynamic-update-slice_fusion
  5.2 3.0 %collective-permute-start.8 = (bf16[96,3072]{1,0:T(8,128)(2,1)S(1)}, bf16[96,3072]{1,0:T(8,128)(2,1)S(1)}, u32[]{:S(2)}, u32[]{:S(2)}) collective-permute-start(bf16[96,3072]{1,0:T(8,128)(2,1)S(1)} %get-tuple-element.87.rest_4_.rest_0_), channel_id=1, source_target_pairs={{0,2},{1,3},{2,0},{3,1},{4,6},{5,7},{6,4},{7,5},{8,10},{9,11},{10,... | collective-permute-start | bytes 1769480 | tf_op jit(solution)/shard_map/ppermute | solution.py:59
  14.5 13.7 %collective-permute-done.1 = bf16[2,3456]{1,0:T(2,128)(2,1)S(1)} collective-permute-done((bf16[2,3456]{1,0:T(2,128)(2,1)S(1)}, bf16[2,3456]{1,0:T(2,128)(2,1)S(1)}, u32[]{:S(2)}, u32[]{:S(2)}) %collective-permute-start.1) | collective-permute-done | bytes 13856 | tf_op jit(solution)/shard_map/ppermute | solution.py:59
  37.8 18.2 %collective-permute-done.11.rest_2_ = bf16[96,1536]{1,0:T(8,128)(2,1)} collective-permute-done((bf16[96,1536]{1,0:T(8,128)(2,1)S(1)}, bf16[96,1536]{1,0:T(8,128)(2,1)}, u32[]{:S(2)}, u32[]{:S(2)}) %collective-permute-start.11) | collective-permute-done | bytes 294944 | tf_op jit(solution)/shard_map/ppermute | solution.py:59
  59.2 18.8 %shard_map.220 = (f32[3,256,384]{2,1,0:T(8,128)}, f32[3,256,384]{2,1,0:T(8,128)}, bf16[3,256,1152]{2,1,0:T(8,128)(2,1)}, bf16[3,6,256,256]{3,2,1,0:T(8,128)(2,1)...) custom-call(s32[2]{0:T(128)} %pad_add_fusion.info, ...), custom_call_target="tpu_custom_call" | custom-call | flops 2717908992 | bytes 9437184 | tf_op jit(solution)/shard_map/pallas_call | solution.py:423
  78.9 32.3 %shard_map.221 = (f32[3,256,384]{2,1,0:T(8,128)}, f32[3,256,384]{2,1,0:T(8,128)}, f32[3,3,384]{2,1,0:T(4,128)}, f32[3,3,384]{2,1,0:T(4,128)}, f32[1,384]{1,0:T(1...) custom-call(s32[2]{0:T(128)} %pad_add_fusion.info, ...), custom_call_target="tpu_custom_call" | custom-call | flops 8153726976 | bytes 28311552 | tf_op jit(solution)/shard_map/pallas_call | solution.py:423
  112.7 12.6 %shard_map.222 = (f32[3,256,384]{2,1,0:T(8,128)}, f32[3,3,384]{2,1,0:T(4,128)}, f32[1,1536]{1,0:T(1,128)}, f32[1,384]{1,0:T(1,128)}, bf16[2,96,3072]{2,1,0:T(8,128)(2,1)}, /*index=5*/bf16[2,96,3072]{2,1,0:T(8,128)(2,1)}) custom-call(s32[2]{0:T(128)} %pad_add_fusion.info, f32[3,256,384]{2,1,0:T(8,128)} %get-tuple-element.45.grad, ...), custom_call_target="tpu_custom_call" | custom-call | flops 2717908992 | bytes 9437184 | tf_op jit(solution)/shard_map/pallas_call | solution.py:423
  125.3 14.9 %shard_map.223 = (f32[3,256,384]{2,1,0:T(8,128)}, f32[3,3,384]{2,1,0:T(4,128)}, f32[1,384]{1,0:T(1,128)}, bf16[2,96,1536]{2,1,0:T(8,128)(2,1)}, bf16[2,96,1536]{2,1,0:T(8,128)(2,1)}) custom-call(s32[2]{0:T(128)} %pad_add_fusion.info, f32[3,256,384]{2,1,0:T(8,128)} %get-tuple-element.50.grad, f32[3,256,384]{2,1,0:T(8,128)} %resid.3, ...), custom_call_target="tpu_custom_call" | custom-call | flops 2717908992 | bytes 9437184 | tf_op jit(solution)/shard_map/pallas_call | solution.py:423
  142.1 6.8 %collective-permute-done.16 = bf16[1,9,2304]{2,1,0:T(8,128)(2,1)S(1)} collective-permute-done((bf16[1,9,2304]{2,1,0:T(8,128)(2,1)S(1)}, bf16[1,9,2304]{2,1,0:T(8,128)(2,1)S(1)}, u32[]{:S(2)}, u32[]{:S(2)}) %collective-permute-start.16) | collective-permute-done | bytes 41504 | tf_op jit(solution)/shard_map/ppermute | solution.py:59
  149.3 4.9 %collective-permute-done.17 = bf16[2,9,2304]{2,1,0:T(8,128)(2,1)S(1)} collective-permute-done((bf16[2,9,2304]{2,1,0:T(8,128)(2,1)S(1)}, bf16[2,9,2304]{2,1,0:T(8,128)(2,1)S(1)}, u32[]{:S(2)}, u32[]{:S(2)}) %collective-permute-start.17) | collective-permute-done | bytes 82976 | tf_op jit(solution)/shard_map/ppermute | solution.py:59
  155.5 5.6 %collective-permute-done.18 = bf16[4,9,2304]{2,1,0:T(8,128)(2,1)S(1)} collective-permute-done((bf16[4,9,2304]{2,1,0:T(8,128)(2,1)S(1)}, bf16[4,9,2304]{2,1,0:T(8,128)(2,1)S(1)}, u32[]{:S(2)}, u32[]{:S(2)}) %collective-permute-start.18) | collective-permute-done | bytes 165920 | tf_op jit(solution)/shard_map/ppermute | solution.py:59
  161.3 1.9 collective-permute-start.19
  165.9 2.9 %collective-permute-done.19 = bf16[8,9,2304]{2,0,1:T(8,128)(2,1)S(1)} collective-permute-done((bf16[8,9,2304]{2,0,1:T(8,128)(2,1)S(1)}, bf16[8,9,2304]{2,0,1:T(8,128)(2,1)S(1)}, u32[]{:S(2)}, u32[]{:S(2)}) %collective-permute-start.19) | collective-permute-done | bytes 331808 | tf_op jit(solution)/shard_map/ppermute | solution.py:59
  169.5 3.5 %collective-permute-done.25 = bf16[2,96,768]{2,1,0:T(8,128)(2,1)S(1)} collective-permute-done((bf16[2,96,768]{2,1,0:T(8,128)(2,1)S(1)}, bf16[2,96,768]{2,1,0:T(8,128)(2,1)S(1)}, u32[]{:S(2)}, u32[]{:S(2)}) %collective-permute-start.25) | collective-permute-done | bytes 294944 | tf_op jit(solution)/shard_map/ppermute | solution.py:59
  176.2 2.7 collective-permute-start.33
  179.0 2.9 collective-permute-start.27
  182.1 3.3 %collective-permute-start.34 = (bf16[1,96,384]{2,1,0:T(8,128)(2,1)S(1)}, bf16[1,96,384]{2,1,0:T(8,128)(2,1)S(1)}, u32[]{:S(2)}, u32[]{:S(2)}) collective-permute-start(bf16[1,96,384]{2,1,0:T(8,128)(2,1)S(1)} %broadcast_select_fusion.20), channel_id=1, source_target_pairs={{0,8},{4,12},{8,0},{12,4},{16,24},{20,28},{24,16},{28,20},{1,9},{5... | collective-permute-start | bytes 221192 | tf_op jit(solution)/shard_map/ppermute | solution.py:59
  185.5 3.5 %collective-permute-start.28 = (bf16[1,96,384]{2,1,0:T(8,128)(2,1)S(1)}, bf16[1,96,384]{2,1,0:T(8,128)(2,1)S(1)}, u32[]{:S(2)}, u32[]{:S(2)}) collective-permute-start(bf16[1,96,384]{2,1,0:T(8,128)(2,1)S(1)} %add_convert_fusion.19), channel_id=1, source_target_pairs={{0,16},{4,20},{8,24},{12,28},{16,0},{20,4},{24,8},{28,12},{1,17},{... | collective-permute-start | bytes 221192 | tf_op jit(solution)/shard_map/ppermute | solution.py:59
  190.4 2.0 collective-permute-done.28
  192.8 2.3 collective-permute-done.35
  231.1 2.5 collective-permute-done.30
  233.7 2.4 collective-permute-done.37
  242.7 6.5 %collective-permute-done.40 = bf16[1,96,1536]{2,1,0:T(8,128)(2,1)S(1)} collective-permute-done((bf16[1,96,1536]{2,1,0:T(8,128)(2,1)S(1)}, bf16[1,96,1536]{2,1,0:T(8,128)(2,1)S(1)}, u32[]{:S(2)}, u32[]{:S(2)}) %collective-permute-start.40) | collective-permute-done | bytes 294944 | tf_op jit(solution)/shard_map/ppermute | solution.py:59
  249.4 1.9 collective-permute-start.41
  251.3 2.7 collective-permute-done.47
  254.1 1.9 collective-permute-start.48
  257.6 3.6 %collective-permute-done.48 = bf16[1,96,768]{2,1,0:T(8,128)(2,1)S(1)} collective-permute-done((bf16[1,96,768]{2,1,0:T(8,128)(2,1)S(1)}, bf16[1,96,768]{2,1,0:T(8,128)(2,1)S(1)}, u32[]{:S(2)}, u32[]{:S(2)}) %collective-permute-start.48) | collective-permute-done | bytes 147488 | tf_op jit(solution)/shard_map/ppermute | solution.py:59
  261.2 2.7 collective-permute-start.49
  264.0 5.1 %collective-permute-done.42 = bf16[1,96,768]{2,1,0:T(8,128)(2,1)S(1)} collective-permute-done((bf16[1,96,768]{2,1,0:T(8,128)(2,1)S(1)}, bf16[1,96,768]{2,1,0:T(8,128)(2,1)S(1)}, u32[]{:S(2)}, u32[]{:S(2)}) %collective-permute-start.42) | collective-permute-done | bytes 147488 | tf_op jit(solution)/shard_map/ppermute | solution.py:59
  271.3 3.8 %collective-permute-done.43 = bf16[96,768]{1,0:T(8,128)(2,1)S(1)} collective-permute-done((bf16[96,768]{1,0:T(8,128)(2,1)S(1)}, bf16[96,768]{1,0:T(8,128)(2,1)S(1)}, u32[]{:S(2)}, u32[]{:S(2)}) %collective-permute-start.43) | collective-permute-done | bytes 147488 | tf_op jit(solution)/shard_map/ppermute | solution.py:59
  277.9 5.6 %collective-permute-done.44 = bf16[96,1536]{1,0:T(8,128)(2,1)S(1)} collective-permute-done((bf16[96,1536]{1,0:T(8,128)(2,1)S(1)}, bf16[96,1536]{1,0:T(8,128)(2,1)S(1)}, u32[]{:S(2)}, u32[]{:S(2)}) %collective-permute-start.44) | collective-permute-done | bytes 294944 | tf_op jit(solution)/shard_map/ppermute | solution.py:59
  283.7 3.0 %collective-permute-done.51 = bf16[96,1536]{1,0:T(8,128)(2,1)S(1)} collective-permute-done((bf16[96,1536]{1,0:T(8,128)(2,1)S(1)}, bf16[96,1536]{1,0:T(8,128)(2,1)S(1)}, u32[]{:S(2)}, u32[]{:S(2)}) %collective-permute-start.51) | collective-permute-done | bytes 294944 | tf_op jit(solution)/shard_map/ppermute | solution.py:59
  (339 shorter events, 87.2 us)
Async XLA Ops:
  5.2 32.1 %collective-permute-start.8 = (bf16[96,3072]{1,0:T(8,128)(2,1)S(1)}, bf16[96,3072]{1,0:T(8,128)(2,1)S(1)}, u32[]{:S(2)}, u32[]{:S(2)}) collective-permute-start(bf16[96,3072]{1,0:T(8,128)(2,1)S(1)} %get-tuple-element.87.rest_4_.rest_0_), channel_id=1, source_target_pairs={{0,2},{1,3},{2,0},{3,1},{4,6},{5,7},{6,4},{7,5},{8,10},{9,11},{10,... | collective-permute-start | bytes 1769480 | tf_op jit(solution)/shard_map/ppermute | solution.py:59
  8.2 49.0 %collective-permute-start.7 = (bf16[96,3072]{1,0:T(8,128)(2,1)S(1)}, bf16[96,3072]{1,0:T(8,128)(2,1)S(1)}, u32[]{:S(2)}, u32[]{:S(2)}) collective-permute-start(bf16[96,3072]{1,0:T(8,128)(2,1)S(1)} %get-tuple-element.87.rest_4_.rest_0_), channel_id=1, source_target_pairs={{0,1},{1,0},{2,3},{3,2},{4,5},{5,4},{6,7},{7,6},{8,9},{9,8},{10,11... | collective-permute-start | bytes 1769480 | tf_op jit(solution)/shard_map/ppermute | solution.py:59
  8.3 28.6 %collective-permute-start.5 = (bf16[96,1536]{1,0:T(8,128)(2,1)S(1)}, bf16[96,1536]{1,0:T(8,128)(2,1)}, u32[]{:S(2)}, u32[]{:S(2)}) collective-permute-start(bf16[96,1536]{1,0:T(8,128)(2,1)S(1)} %pad_maximum_fusion.4.rest_0_), channel_id=1, source_target_pairs={{0,2},{1,3},{2,0},{3,1},{4,6},{5,7},{6,4},{7,5},{8,10},{9,11},{10,... | collective-permute-start | bytes 884744 | tf_op jit(solution)/shard_map/ppermute | solution.py:59
  8.4 28.8 %collective-permute-start.4 = (bf16[96,1536]{1,0:T(8,128)(2,1)S(1)}, bf16[96,1536]{1,0:T(8,128)(2,1)}, u32[]{:S(2)}, u32[]{:S(2)}) collective-permute-start(bf16[96,1536]{1,0:T(8,128)(2,1)S(1)} %pad_maximum_fusion.4.rest_0_), channel_id=1, source_target_pairs={{0,1},{1,0},{2,3},{3,2},{4,5},{5,4},{6,7},{7,6},{8,9},{9,8},{10,11... | collective-permute-start | bytes 884744 | tf_op jit(solution)/shard_map/ppermute | solution.py:59
  12.1 16.0 %collective-permute-start.1 = (bf16[2,3456]{1,0:T(2,128)(2,1)S(1)}, bf16[2,3456]{1,0:T(2,128)(2,1)S(1)}, u32[]{:S(2)}, u32[]{:S(2)}) collective-permute-start(bf16[2,3456]{1,0:T(2,128)(2,1)S(1)} %pad_maximum_fusion.16), channel_id=1, source_target_pairs={{0,2},{1,3},{2,0},{3,1},{4,6},{5,7},{6,4},{7,5},{8,10},{9,11},{10,... | collective-permute-start | bytes 41480 | tf_op jit(solution)/shard_map/ppermute | solution.py:59
  35.1 20.9 %collective-permute-start.14 = (bf16[96,3072]{1,0:T(8,128)(2,1)}, bf16[96,3072]{1,0:T(8,128)(2,1)}, u32[]{:S(2)}, u32[]{:S(2)}) collective-permute-start(bf16[96,3072]{1,0:T(8,128)(2,1)} %get-tuple-element.86.rest_4_), channel_id=1, source_target_pairs={{0,2},{1,3},{2,0},{3,1},{4,6},{5,7},{6,4},{7,5},{8,10},{9,11},{10,... | collective-permute-start | bytes 1769480 | tf_op jit(solution)/shard_map/ppermute | solution.py:59
  36.9 19.1 %collective-permute-start.11 = (bf16[96,1536]{1,0:T(8,128)(2,1)S(1)}, bf16[96,1536]{1,0:T(8,128)(2,1)}, u32[]{:S(2)}, u32[]{:S(2)}) collective-permute-start(bf16[96,1536]{1,0:T(8,128)(2,1)S(1)} %pad_maximum_fusion.5.rest_0_), channel_id=1, source_target_pairs={{0,2},{1,3},{2,0},{3,1},{4,6},{5,7},{6,4},{7,5},{8,10},{9,11},{10,... | collective-permute-start | bytes 884744 | tf_op jit(solution)/shard_map/ppermute | solution.py:59
  37.3 20.0 %collective-permute-start.6 = (bf16[96,1536]{1,0:T(8,128)(2,1)}, bf16[96,1536]{1,0:T(8,128)(2,1)S(1)}, u32[]{:S(2)}, u32[]{:S(2)}) collective-permute-start(bf16[96,1536]{1,0:T(8,128)(2,1)} %collective-permute-done.5.rest_2_), channel_id=1, source_target_pairs={{0,1},{1,0},{2,3},{3,2},{4,5},{5,4},{6,7},{7,6},{8,9},{9,8},{10,11... | collective-permute-start | bytes 884744 | tf_op jit(solution)/shard_map/ppermute | solution.py:59
  37.3 21.1 %collective-permute-start.9 = (bf16[96,3072]{1,0:T(8,128)(2,1)S(1)}, bf16[96,3072]{1,0:T(8,128)(2,1)S(1)}, u32[]{:S(2)}, u32[]{:S(2)}) collective-permute-start(bf16[96,3072]{1,0:T(8,128)(2,1)S(1)} %collective-permute-done.8.rest_6_.rest_2_), channel_id=1, source_target_pairs={{0,1},{1,0},{2,3},{3,2},{4,5},{5,4},{6,7},{7,6},{8,9},{9,8},{10,11... | collective-permute-start | bytes 1769480 | tf_op jit(solution)/shard_map/ppermute | solution.py:59
  56.0 22.1 %collective-permute-start.13 = (bf16[96,3072]{1,0:T(8,128)(2,1)}, bf16[96,3072]{1,0:T(8,128)(2,1)}, u32[]{:S(2)}, u32[]{:S(2)}) collective-permute-start(bf16[96,3072]{1,0:T(8,128)(2,1)} %get-tuple-element.86.rest_4_), channel_id=1, source_target_pairs={{0,1},{1,0},{2,3},{3,2},{4,5},{5,4},{6,7},{7,6},{8,9},{9,8},{10,11... | collective-permute-start | bytes 1769480 | tf_op jit(solution)/shard_map/ppermute | solution.py:59
  56.0 22.1 %collective-permute-start.15 = (bf16[96,3072]{1,0:T(8,128)(2,1)}, bf16[96,3072]{1,0:T(8,128)(2,1)}, u32[]{:S(2)}, u32[]{:S(2)}) collective-permute-start(bf16[96,3072]{1,0:T(8,128)(2,1)} %collective-permute-done.14.rest_6_), channel_id=1, source_target_pairs={{0,1},{1,0},{2,3},{3,2},{4,5},{5,4},{6,7},{7,6},{8,9},{9,8},{10,11... | collective-permute-start | bytes 1769480 | tf_op jit(solution)/shard_map/ppermute | solution.py:59
  57.2 20.9 %collective-permute-start.10 = (bf16[96,1536]{1,0:T(8,128)(2,1)S(1)}, bf16[96,1536]{1,0:T(8,128)(2,1)S(1)}, u32[]{:S(2)}, u32[]{:S(2)}) collective-permute-start(bf16[96,1536]{1,0:T(8,128)(2,1)S(1)} %pad_maximum_fusion.5.rest_0_), channel_id=1, source_target_pairs={{0,1},{1,0},{2,3},{3,2},{4,5},{5,4},{6,7},{7,6},{8,9},{9,8},{10,11... | collective-permute-start | bytes 884744 | tf_op jit(solution)/shard_map/ppermute | solution.py:59
  57.3 20.8 %collective-permute-start.12 = (bf16[96,1536]{1,0:T(8,128)(2,1)}, bf16[96,1536]{1,0:T(8,128)(2,1)S(1)}, u32[]{:S(2)}, u32[]{:S(2)}) collective-permute-start(bf16[96,1536]{1,0:T(8,128)(2,1)} %collective-permute-done.11.rest_2_), channel_id=1, source_target_pairs={{0,1},{1,0},{2,3},{3,2},{4,5},{5,4},{6,7},{7,6},{8,9},{9,8},{10,11... | collective-permute-start | bytes 884744 | tf_op jit(solution)/shard_map/ppermute | solution.py:59
  154.4 41.0 %collective-permute-start.38 = (bf16[2,96,3072]{2,1,0:T(8,128)(2,1)}, bf16[2,96,3072]{2,1,0:T(8,128)(2,1)S(1)}, u32[]{:S(2)}, u32[]{:S(2)}) collective-permute-start(bf16[2,96,3072]{2,1,0:T(8,128)(2,1)} %get-tuple-element.71), channel_id=1, source_target_pairs={{0,1},{1,0},{2,3},{3,2},{4,5},{5,4},{6,7},{7,6},{8,9},{9,8},{10,11... | collective-permute-start | bytes 3538952 | tf_op jit(solution)/shard_map/ppermute | solution.py:59
  154.5 43.1 %collective-permute-start.45 = (bf16[2,96,3072]{2,1,0:T(8,128)(2,1)S(1)}, bf16[2,96,3072]{2,1,0:T(8,128)(2,1)S(1)}, u32[]{:S(2)}, u32[]{:S(2)}) collective-permute-start(bf16[2,96,3072]{2,1,0:T(8,128)(2,1)S(1)} %copy-done.39), channel_id=1, source_target_pairs={{0,1},{1,0},{2,3},{3,2},{4,5},{5,4},{6,7},{7,6},{8,9},{9,8},{10,11... | collective-permute-start | bytes 3538952 | tf_op jit(solution)/shard_map/ppermute | solution.py:59
  154.9 8.3 %collective-permute-start.24 = (bf16[2,96,1536]{2,1,0:T(8,128)(2,1)}, bf16[2,96,1536]{2,1,0:T(8,128)(2,1)S(1)}, u32[]{:S(2)}, u32[]{:S(2)}) collective-permute-start(bf16[2,96,1536]{2,1,0:T(8,128)(2,1)} %get-tuple-element.67), channel_id=1, source_target_pairs={{0,1},{1,0},{2,3},{3,2},{4,5},{5,4},{6,7},{7,6},{8,9},{9,8},{10,11... | collective-permute-start | bytes 1769480 | tf_op jit(solution)/shard_map/ppermute | solution.py:59
  155.0 9.8 %collective-permute-start.31 = (bf16[2,96,1536]{2,1,0:T(8,128)(2,1)S(1)}, bf16[2,96,1536]{2,1,0:T(8,128)(2,1)S(1)}, u32[]{:S(2)}, u32[]{:S(2)}) collective-permute-start(bf16[2,96,1536]{2,1,0:T(8,128)(2,1)S(1)} %copy-done.40), channel_id=1, source_target_pairs={{0,1},{1,0},{2,3},{3,2},{4,5},{5,4},{6,7},{7,6},{8,9},{9,8},{10,11... | collective-permute-start | bytes 1769480 | tf_op jit(solution)/shard_map/ppermute | solution.py:59
  163.4 9.5 %collective-permute-start.25 = (bf16[2,96,768]{2,1,0:T(8,128)(2,1)S(1)}, bf16[2,96,768]{2,1,0:T(8,128)(2,1)S(1)}, u32[]{:S(2)}, u32[]{:S(2)}) collective-permute-start(bf16[2,96,768]{2,1,0:T(8,128)(2,1)S(1)} %broadcast_select_fusion.5), channel_id=1, source_target_pairs={{0,4},{4,0},{8,12},{12,8},{16,20},{20,16},{24,28},{28,24},{1,5},{5... | collective-permute-start | bytes 884744 | tf_op jit(solution)/shard_map/ppermute | solution.py:59
  165.1 11.0 %collective-permute-start.32 = (bf16[2,96,768]{2,1,0:T(8,128)(2,1)S(1)}, bf16[2,96,768]{2,1,0:T(8,128)(2,1)S(1)}, u32[]{:S(2)}, u32[]{:S(2)}) collective-permute-start(bf16[2,96,768]{2,1,0:T(8,128)(2,1)S(1)} %broadcast_select_fusion.4), channel_id=1, source_target_pairs={{0,4},{4,0},{8,12},{12,8},{16,20},{20,16},{24,28},{28,24},{1,5},{5... | collective-permute-start | bytes 884744 | tf_op jit(solution)/shard_map/ppermute | solution.py:59
  169.4 32.1 %collective-permute-start.20 = (bf16[16,9,2304]{2,0,1:T(8,128)(2,1)S(1)}, bf16[16,9,2304]{2,0,1:T(8,128)(2,1)S(1)}, u32[]{:S(2)}, u32[]{:S(2)}) collective-permute-start(bf16[16,9,2304]{2,0,1:T(8,128)(2,1)S(1)} %copy.50), channel_id=1, source_target_pairs={{0,1},{1,0},{2,3},{3,2},{4,5},{5,4},{6,7},{7,6},{8,9},{9,8},{10,11... | collective-permute-start | bytes 1990664 | tf_op jit(solution)/shard_map/ppermute | solution.py:59
  196.6 41.3 %collective-permute-start.39 = (bf16[1,96,3072]{2,1,0:T(8,128)(2,1)}, bf16[1,96,3072]{2,1,0:T(8,128)(2,1)}, u32[]{:S(2)}, u32[]{:S(2)}) collective-permute-start(bf16[1,96,3072]{2,1,0:T(8,128)(2,1)} %slice.344), channel_id=1, source_target_pairs={{0,2},{1,3},{2,0},{3,1},{4,6},{5,7},{6,4},{7,5},{8,10},{9,11},{10,... | collective-permute-start | bytes 1769480 | tf_op jit(solution)/shard_map/ppermute | solution.py:59
  198.9 40.9 %collective-permute-start.46 = (bf16[1,96,3072]{2,1,0:T(8,128)(2,1)}, bf16[1,96,3072]{2,1,0:T(8,128)(2,1)}, u32[]{:S(2)}, u32[]{:S(2)}) collective-permute-start(bf16[1,96,3072]{2,1,0:T(8,128)(2,1)} %slice.350), channel_id=1, source_target_pairs={{0,2},{1,3},{2,0},{3,1},{4,6},{5,7},{6,4},{7,5},{8,10},{9,11},{10,... | collective-permute-start | bytes 1769480 | tf_op jit(solution)/shard_map/ppermute | solution.py:59
  218.5 8.3 %collective-permute-start.21 = (f32[3,96]{1,0:T(4,128)}, f32[3,96]{1,0:T(4,128)}, u32[]{:S(2)}, u32[]{:S(2)}) collective-permute-start(f32[3,96]{1,0:T(4,128)} %bitcast.140), channel_id=1, source_target_pairs={{0,1},{1,0},{2,3},{3,2},{4,5},{5,4},{6,7},{7,6},{8,9},{9,8},{10,11... | collective-permute-start | bytes 3464 | tf_op jit(solution)/shard_map/ppermute | solution.py:59
  219.0 9.0 %collective-permute-start.22 = (f32[3,96]{1,0:T(4,128)}, f32[3,96]{1,0:T(4,128)S(1)}, u32[]{:S(2)}, u32[]{:S(2)}) collective-permute-start(f32[3,96]{1,0:T(4,128)} %bitcast.139), channel_id=1, source_target_pairs={{0,2},{1,3},{2,0},{3,1},{4,6},{5,7},{6,4},{7,5},{8,10},{9,11},{10,... | collective-permute-start | bytes 3464 | tf_op jit(solution)/shard_map/ppermute | solution.py:59
  220.6 9.0 %collective-permute-start.23 = (f32[3,96]{1,0:T(4,128)}, f32[3,96]{1,0:T(4,128)}, u32[]{:S(2)}, u32[]{:S(2)}) collective-permute-start(f32[3,96]{1,0:T(4,128)} %bitcast.138), channel_id=1, source_target_pairs={{0,3},{1,2},{2,1},{3,0},{4,7},{5,6},{6,5},{7,4},{8,11},{9,10},{10,... | collective-permute-start | bytes 3464 | tf_op jit(solution)/shard_map/ppermute | solution.py:59
  228.0 8.1 %collective-permute-start.37 = (bf16[96,768]{1,0:T(8,128)(2,1)S(1)}, bf16[96,768]{1,0:T(8,128)(2,1)S(1)}, u32[]{:S(2)}, u32[]{:S(2)}) collective-permute-start(bf16[96,768]{1,0:T(8,128)(2,1)S(1)} %copy-done.26), channel_id=1, source_target_pairs={{0,4},{4,0},{8,12},{12,8},{16,20},{20,16},{24,28},{28,24},{1,5},{5... | collective-permute-start | bytes 442376 | tf_op jit(solution)/shard_map/ppermute | solution.py:59
  239.3 9.9 %collective-permute-start.40 = (bf16[1,96,1536]{2,1,0:T(8,128)(2,1)S(1)}, bf16[1,96,1536]{2,1,0:T(8,128)(2,1)S(1)}, u32[]{:S(2)}, u32[]{:S(2)}) collective-permute-start(bf16[1,96,1536]{2,1,0:T(8,128)(2,1)S(1)} %broadcast_select_fusion.1), channel_id=1, source_target_pairs={{0,4},{4,0},{8,12},{12,8},{16,20},{20,16},{24,28},{28,24},{1,5},{5... | collective-permute-start | bytes 884744 | tf_op jit(solution)/shard_map/ppermute | solution.py:59
  241.1 12.9 %collective-permute-start.47 = (bf16[1,96,1536]{2,1,0:T(8,128)(2,1)S(1)}, bf16[1,96,1536]{2,1,0:T(8,128)(2,1)S(1)}, u32[]{:S(2)}, u32[]{:S(2)}) collective-permute-start(bf16[1,96,1536]{2,1,0:T(8,128)(2,1)S(1)} %broadcast_select_fusion), channel_id=1, source_target_pairs={{0,4},{4,0},{8,12},{12,8},{16,20},{20,16},{24,28},{28,24},{1,5},{5... | collective-permute-start | bytes 884744 | tf_op jit(solution)/shard_map/ppermute | solution.py:59
  256.1 12.9 %collective-permute-start.42 = (bf16[1,96,768]{2,1,0:T(8,128)(2,1)S(1)}, bf16[1,96,768]{2,1,0:T(8,128)(2,1)S(1)}, u32[]{:S(2)}, u32[]{:S(2)}) collective-permute-start(bf16[1,96,768]{2,1,0:T(8,128)(2,1)S(1)} %add_convert_fusion.13), channel_id=1, source_target_pairs={{0,16},{4,20},{8,24},{12,28},{16,0},{20,4},{24,8},{28,12},{1,17},{... | collective-permute-start | bytes 442376 | tf_op jit(solution)/shard_map/ppermute | solution.py:59
  261.2 9.4 %collective-permute-start.49 = (bf16[1,96,768]{2,1,0:T(8,128)(2,1)S(1)}, bf16[1,96,768]{2,1,0:T(8,128)(2,1)S(1)}, u32[]{:S(2)}, u32[]{:S(2)}) collective-permute-start(bf16[1,96,768]{2,1,0:T(8,128)(2,1)S(1)} %add_convert_fusion.11), channel_id=1, source_target_pairs={{0,16},{4,20},{8,24},{12,28},{16,0},{20,4},{24,8},{28,12},{1,17},{... | collective-permute-start | bytes 442376 | tf_op jit(solution)/shard_map/ppermute | solution.py:59
  275.1 8.5 %collective-permute-start.44 = (bf16[96,1536]{1,0:T(8,128)(2,1)S(1)}, bf16[96,1536]{1,0:T(8,128)(2,1)S(1)}, u32[]{:S(2)}, u32[]{:S(2)}) collective-permute-start(bf16[96,1536]{1,0:T(8,128)(2,1)S(1)} %pad_maximum_fusion.7), channel_id=1, source_target_pairs={{0,4},{4,0},{8,12},{12,8},{16,20},{20,16},{24,28},{28,24},{1,5},{5... | collective-permute-start | bytes 884744 | tf_op jit(solution)/shard_map/ppermute | solution.py:59
  276.7 10.0 %collective-permute-start.51 = (bf16[96,1536]{1,0:T(8,128)(2,1)S(1)}, bf16[96,1536]{1,0:T(8,128)(2,1)S(1)}, u32[]{:S(2)}, u32[]{:S(2)}) collective-permute-start(bf16[96,1536]{1,0:T(8,128)(2,1)S(1)} %pad_maximum_fusion.8), channel_id=1, source_target_pairs={{0,4},{4,0},{8,12},{12,8},{16,20},{20,16},{24,28},{28,24},{1,5},{5... | collective-permute-start | bytes 884744 | tf_op jit(solution)/shard_map/ppermute | solution.py:59
  (64 other events, 500.9 us)

commit v4 on v3

--- a/solution.py
+++ b/solution.py
@@ -407,6 +407,51 @@
         emit_attn(shards, me, a_qkv, a_proj, keep, send)
 
 
+def unpack_kernel(flag, *refs):
+    g_qkv, g_proj, g_up, g_down = refs[-4:]
+    triple, width, inner = g_qkv.shape[2], g_proj.shape[2], g_up.shape[2]
+    rows, edge = g_qkv.shape[1], (triple + width) // 2
+
+    def write(first):
+        for n in range(LAYERS):
+            low, high = refs[2 * n + first], refs[2 * n + 1 - first]
+            g_qkv[n, :, :edge] = low[:, :edge].astype(jnp.float32)
+            g_qkv[n, :, edge:] = high[:, : triple - edge].astype(jnp.float32)
+            g_proj[n] = high[:, triple - edge : edge].astype(jnp.float32)
+            g_up[n] = low[:, edge:].astype(jnp.float32)
+            for q in range(inner // width):
+                part = high[:, edge + q * width : edge + (q + 1) * width]
+                g_down[n, q * rows : (q + 1) * rows, :] = part.astype(jnp.float32)
+
+    @pl.when(flag[0] == 0)
+    def _():
+        write(0)
+
+    @pl.when(flag[0] != 0)
+    def _():
+        write(1)
+
+
+def unpack_call(flag, sums, sizes):
+    triple, width, inner = sizes
+    rows = sums[0][0].shape[0]
+    shapes = [
+        (LAYERS, rows, triple),
+        (LAYERS, rows, width),
+        (LAYERS, rows, inner),
+        (LAYERS, inner // width * rows, width),
+    ]
+    parts = [half for pair in sums for half in pair]
+    return pl.pallas_call(
+        unpack_kernel,
+        out_shape=[jax.ShapeDtypeStruct(s, jnp.float32) for s in shapes],
+        in_specs=[pl.BlockSpec(memory_space=pltpu.SMEM)]
+        + [pl.BlockSpec(memory_space=pltpu.VMEM)] * len(parts),
+        out_specs=[pl.BlockSpec(memory_space=pltpu.VMEM)] * len(shapes),
+        name="unpack",
+    )(flag, *parts)
+
+
 def per_slot(shape):
     rest = (0,) * (len(shape) - 1)
     return pl.BlockSpec((1,) + tuple(shape[1:]), lambda slot, info: (slot,) + rest)
@@ -545,48 +590,79 @@
     return blocks[0]
 
 
-def reduce_message(kept, sent, plan):
-    f32, wire = jnp.float32, kept.dtype
-    value, trail = kept, []
-    for n, (axis, size, bit, kind) in enumerate(plan):
-        if kind == "rows":
-            if n == 0:
-                stay, go = kept, sent
-            else:
-                half = value.shape[0] // 2
-                stay, go = value[:half], value[half:]
-        elif kind == "columns":
-            half = value.shape[-1] // 2
-            upper = has_bit(axis, bit)
-            low, high = value[..., :half], value[..., half:]
-            stay, go = jnp.where(upper, high, low), jnp.where(upper, low, high)
+def halves_of(left, right, kind, upper):
+    if kind == "rows":
+        half = left.shape[0] // 2
+        return left[:half] + right[:half], left[half:] + right[half:]
+    if kind == "columns":
+        half = left.shape[-1] // 2
+        low = left[..., :half] + right[..., :half]
+        high = left[..., half:] + right[..., half:]
+        return jnp.where(upper, high, low), jnp.where(upper, low, high)
+    value = left + right
+    return value, value
+
+
+def run_stages(left, right, plan):
+    trail = []
+    for axis, size, bit, kind in plan:
+        stay, go = halves_of(left, right, kind, has_bit(axis, bit))
+        left, right = stay, swap(go, axis, size, bit)
+        if kind == "columns":
             trail.append((axis, size, bit))
-        else:
-            stay, go = value, value
-        got = swap(go, axis, size, bit)
-        value = (stay.astype(f32) + got.astype(f32)).astype(wire)
-    value = value[0]
-    for axis, size, bit in reversed(trail):
-        other = swap(value, axis, size, bit)
-        upper = has_bit(axis, bit)
-        value = jnp.concatenate(
-            [jnp.where(upper, other, value), jnp.where(upper, value, other)], axis=-1
-        )
-    return value
-
-
-def message_plan(groups, shards, columns, dp_early):
-    shard_stages = [("fsdp", shards, bit, "rows") for bit in bits_of(shards)]
-    group_stages = []
-    for bit in bits_of(groups):
+    return left, right, trail
+
+
+def widen(value, axis, size, bit):
+    other = swap(value, axis, size, bit)
+    upper = has_bit(axis, bit)
+    return jnp.where(upper, other, value), jnp.where(upper, value, other)
+
+
+def early_plans(groups, shards):
+    first, *others = [("fsdp", shards, bit, "rows") for bit in bits_of(shards)]
+    cut = [("dp", groups, 1, "columns")]
+    return first, cut + others, others + cut
+
+
+def late_plan(groups, columns):
+    plan = []
+    for bit in bits_of(groups)[1:]:
         if 2 * bit < groups and (columns // 2) % 128 == 0:
             columns //= 2
-            group_stages.append(("dp", groups, bit, "columns"))
+            plan.append(("dp", groups, bit, "columns"))
         else:
-            group_stages.append(("dp", groups, bit, "full"))
-    if dp_early:
-        return shard_stages[:1] + group_stages[:1] + shard_stages[1:] + group_stages[1:]
-    return shard_stages + group_stages
+            plan.append(("dp", groups, bit, "full"))
+    return plan
+
+
+def early_sum(kept, sent, first, plan):
+    got = swap(sent, *first[:3])
+    left, right, _ = run_stages(kept, got, plan)
+    return left, right
+
+
+def late_sum(attn, mlp, groups):
+    value = jnp.concatenate([attn[0][0] + attn[1][0], mlp[0][0] + mlp[1][0]], axis=-1)
+    left, right, trail = value, None, []
+    plan = late_plan(groups, value.shape[-1])
+    for axis, size, bit, kind in plan:
+        if right is None:
+            half = left.shape[-1] // 2
+            upper = has_bit(axis, bit)
+            stay, go = left, left
+            if kind == "columns":
+                low, high = left[:, :half], left[:, half:]
+                stay, go = jnp.where(upper, high, low), jnp.where(upper, low, high)
+        else:
+            stay, go = halves_of(left, right, kind, has_bit(axis, bit))
+        left, right = stay, swap(go, axis, size, bit)
+        if kind == "columns":
+            trail.append((axis, size, bit))
+    value = left if right is None else left + right
+    for stage in reversed(trail):
+        value = jnp.concatenate(widen(value, *stage), axis=-1)
+    return value, swap(value, "dp", groups, 1)
 
 
 def on_device(
@@ -663,13 +739,12 @@
         saved.append(kept)
     sums = [None] * LAYERS
     small_rows = [None] * LAYERS
-    attn_stages = message_plan(groups, shards, triple + width, True)
-    mlp_stages = message_plan(groups, shards, 2 * inner, False)
+    first, attn_plan_of, mlp_plan_of = early_plans(groups, shards)
 
     def reduce_layer(n, attn_pair, mlp_pair):
-        mlp = reduce_message(*mlp_pair, mlp_stages)
-        attn = reduce_message(*attn_pair, attn_stages)
-        sums[n] = (attn, mlp)
+        mlp = early_sum(*mlp_pair, first, mlp_plan_of)
+        attn = early_sum(*attn_pair, first, attn_plan_of)
+        sums[n] = late_sum(attn, mlp, groups)
 
     def note_rows(n, gada_attn, gada_mlp, bias_grads):
         flat = jnp.concatenate([gada_attn, gada_mlp], axis=1).reshape(slots, wide)
@@ -729,21 +804,8 @@
     grad_cond = to_absolute(got, "fsdp").transpose(1, 0, 2).reshape(slots, width)
     grad_cond = grad_cond * silu_slope(conditioning)
 
-    def stacked(k, first, last):
-        return jnp.stack([sums[n][k][:, first:last] for n in range(LAYERS)]).astype(f32)
-
-    down_sum = jnp.stack(
-        [
-            jnp.concatenate(
-                [
-                    sums[n][1][:, inner + q * width : inner + (q + 1) * width]
-                    for q in range(ratio)
-                ],
-                axis=0,
-            )
-            for n in range(LAYERS)
-        ]
-    ).astype(f32)
+    upper = has_bit("dp", 1).astype(jnp.int32)[None]
+    g_qkv, g_proj, g_up, down_sum = unpack_call(upper, sums, (triple, width, inner))
     own_inner = inner // shards
     return (
         block_out,
@@ -751,10 +813,10 @@
         grad_cond,
         g_ada,
         lax.dynamic_slice_in_dim(g_ada_bias, me * (wide // shards), wide // shards, 1),
-        stacked(0, 0, triple),
-        stacked(0, triple, triple + width),
+        g_qkv,
+        g_proj,
         lax.dynamic_slice_in_dim(g_bias, me * rows, rows, 1),
-        stacked(1, 0, inner),
+        g_up,
         lax.dynamic_slice_in_dim(g_bias, width + me * own_inner, own_inner, 1),
         down_sum,
         lax.dynamic_slice_in_dim(g_bias, width + inner + me * rows, rows, 1),

time: 290 us -> 283 us (0.976)
  starting transfers between devices: 51.8 us -> 37.4 us
  waiting for transfers between devices: 101 us -> 105 us
  Pallas kernels: 78.5 us -> 81.9 us
  other arithmetic: 25.9 us -> 22.5 us
    ppermute x52 -> x44, starting transfers between devices: 51.8 us -> 37.4 us  [swap(): return lax.ppermute(value, axis, [(i, i ^ bit) for i in range(size)])]
    convert_element_type x20 -> x0, other arithmetic: 8.17 us -> none  [the longest x16 4.28 us: reduce_message(): value = (stay.astype(f32) + got.astype(f32)).astype(wire)]
    add x0 -> x12, other arithmetic: none -> 5.86 us  [the longest x2 2.24 us: late_sum(): mlp[0][0] + mlp[1][0]]
    ppermute x52 -> x44, waiting for transfers between devices: 101 us -> 105 us  [swap(): return lax.ppermute(value, axis, [(i, i ^ bit) for i in range(size)])]
    pallas_call x0 -> x1, Pallas kernels: none -> 3.44 us  [unpack_call(): pl.pallas_call(unpack_kernel, out_shape=[jax.ShapeDtypeStruct(s, jnp.floa...]
    reshape x2, local copies, waits for them, and re-layouts: 0.15 us -> 3.17 us  [on_device(): part = mine[:, n * per_layer:n * per_layer + slots].reshape(-1, wide)]
    unnamed x99 -> x87, local copies, waits for them, and re-layouts: 7.97 us -> 7.58 us
  transfers between devices with their start and end apart: 52 -> 44, of which waited for: 25 -> 22; matrix products, arithmetic and copies ran while one was open for 15% -> 16% of each run, Pallas kernels for 7% -> 7%
where the time goes in v4:
time: 283 us; the launch traced here: 282 us
  waiting for transfers between devices  105 us (37%)
  Pallas kernels  81.9 us (29%)
  starting transfers between devices  37.4 us (13%)
  local copies, waits for them, and re-layouts  26.7 us (9%)
  other arithmetic  22.5 us (8%)
  matrix products  5.48 us (2%)
    ppermute x44, waiting for transfers between devices, swap(): return lax.ppermute(value, axis, [(i, i ^ bit) for i in range(size)])  105 us
    pallas_call x4, Pallas kernels, run_kernel(): pl.pallas_call(functools.partial(kernel, shards, heads), out_shape=[jax.S...  78.5 us
    ppermute x44, starting transfers between devices, swap(): return lax.ppermute(value, axis, [(i, i ^ bit) for i in range(size)])  37.4 us
    unnamed x87, local copies, waits for them, and re-layouts  7.58 us
  transfers between devices with their start and end apart: 44, of which 22 were waited for; matrix products, arithmetic and copies ran while one was open for 16% of the time, Pallas kernels for 7%

profile of v4, /device:TPU:0, one launch (start us, length us, event | category | flops | bytes accessed | tf_op | source)
XLA Modules:
  0.0 281.6 jit_solution(4169822594730180458)
XLA Ops:
  0.7 1.9 bitcast_dynamic-update-slice_fusion
  5.2 3.0 %collective-permute-start.8 = (bf16[96,3072]{1,0:T(8,128)(2,1)S(1)}, bf16[96,3072]{1,0:T(8,128)(2,1)S(1)}, u32[]{:S(2)}, u32[]{:S(2)}) collective-permute-start(bf16[96,3072]{1,0:T(8,128)(2,1)S(1)} %get-tuple-element.99.rest_4_.rest_0_), channel_id=1, source_target_pairs={{0,2},{1,3},{2,0},{3,1},{4,6},{5,7},{6,4},{7,5},{8,10},{9,11},{10,... | collective-permute-start | bytes 1769480 | tf_op jit(solution)/shard_map/ppermute | solution.py:59
  14.5 13.7 %collective-permute-done.1 = bf16[2,3456]{1,0:T(2,128)(2,1)S(1)} collective-permute-done((bf16[2,3456]{1,0:T(2,128)(2,1)S(1)}, bf16[2,3456]{1,0:T(2,128)(2,1)S(1)}, u32[]{:S(2)}, u32[]{:S(2)}) %collective-permute-start.1) | collective-permute-done | bytes 13856 | tf_op jit(solution)/shard_map/ppermute | solution.py:59
  30.9 1.8 collective-permute-start.3
  37.8 18.2 %collective-permute-done.11.rest_2_ = bf16[96,1536]{1,0:T(8,128)(2,1)} collective-permute-done((bf16[96,1536]{1,0:T(8,128)(2,1)S(1)}, bf16[96,1536]{1,0:T(8,128)(2,1)}, u32[]{:S(2)}, u32[]{:S(2)}) %collective-permute-start.11) | collective-permute-done | bytes 294944 | tf_op jit(solution)/shard_map/ppermute | solution.py:59
  59.2 18.8 %shard_map.220 = (f32[3,256,384]{2,1,0:T(8,128)}, f32[3,256,384]{2,1,0:T(8,128)}, bf16[3,256,1152]{2,1,0:T(8,128)(2,1)}, bf16[3,6,256,256]{3,2,1,0:T(8,128)(2,1)...) custom-call(s32[2]{0:T(128)} %pad_add_fusion.info, ...), custom_call_target="tpu_custom_call" | custom-call | flops 2717908992 | bytes 9437184 | tf_op jit(solution)/shard_map/pallas_call | solution.py:468
  78.9 32.2 %shard_map.221 = (f32[3,256,384]{2,1,0:T(8,128)}, f32[3,256,384]{2,1,0:T(8,128)}, f32[3,3,384]{2,1,0:T(4,128)}, f32[3,3,384]{2,1,0:T(4,128)}, f32[1,384]{1,0:T(1...) custom-call(s32[2]{0:T(128)} %pad_add_fusion.info, ...), custom_call_target="tpu_custom_call" | custom-call | flops 8153726976 | bytes 28311552 | tf_op jit(solution)/shard_map/pallas_call | solution.py:468
  112.6 12.5 %shard_map.222 = (f32[3,256,384]{2,1,0:T(8,128)}, f32[3,3,384]{2,1,0:T(4,128)}, f32[1,1536]{1,0:T(1,128)}, f32[1,384]{1,0:T(1,128)}, bf16[2,96,3072]{2,1,0:T(8,128)(2,1)}, /*index=5*/bf16[2,96,3072]{2,1,0:T(8,128)(2,1)}) custom-call(s32[2]{0:T(128)} %pad_add_fusion.info, f32[3,256,384]{2,1,0:T(8,128)} %get-tuple-element.49.grad, ...), custom_call_target="tpu_custom_call" | custom-call | flops 2717908992 | bytes 9437184 | tf_op jit(solution)/shard_map/pallas_call | solution.py:468
  125.3 14.9 %shard_map.223 = (f32[3,256,384]{2,1,0:T(8,128)}, f32[3,3,384]{2,1,0:T(4,128)}, f32[1,384]{1,0:T(1,128)}, bf16[2,96,1536]{2,1,0:T(8,128)(2,1)}, bf16[2,96,1536]{2,1,0:T(8,128)(2,1)}) custom-call(s32[2]{0:T(128)} %pad_add_fusion.info, f32[3,256,384]{2,1,0:T(8,128)} %get-tuple-element.54.grad, f32[3,256,384]{2,1,0:T(8,128)} %resid.3, ...), custom_call_target="tpu_custom_call" | custom-call | flops 2717908992 | bytes 9437184 | tf_op jit(solution)/shard_map/pallas_call | solution.py:468
  142.0 6.8 %collective-permute-done.16 = bf16[1,9,2304]{2,1,0:T(8,128)(2,1)S(1)} collective-permute-done((bf16[1,9,2304]{2,1,0:T(8,128)(2,1)S(1)}, bf16[1,9,2304]{2,1,0:T(8,128)(2,1)S(1)}, u32[]{:S(2)}, u32[]{:S(2)}) %collective-permute-start.16) | collective-permute-done | bytes 41504 | tf_op jit(solution)/shard_map/ppermute | solution.py:59
  149.2 4.9 %collective-permute-done.17 = bf16[2,9,2304]{2,1,0:T(8,128)(2,1)S(1)} collective-permute-done((bf16[2,9,2304]{2,1,0:T(8,128)(2,1)S(1)}, bf16[2,9,2304]{2,1,0:T(8,128)(2,1)S(1)}, u32[]{:S(2)}, u32[]{:S(2)}) %collective-permute-start.17) | collective-permute-done | bytes 82976 | tf_op jit(solution)/shard_map/ppermute | solution.py:59
  155.3 5.6 %collective-permute-done.18 = bf16[4,9,2304]{2,1,0:T(8,128)(2,1)S(1)} collective-permute-done((bf16[4,9,2304]{2,1,0:T(8,128)(2,1)S(1)}, bf16[4,9,2304]{2,1,0:T(8,128)(2,1)S(1)}, u32[]{:S(2)}, u32[]{:S(2)}) %collective-permute-start.18) | collective-permute-done | bytes 165920 | tf_op jit(solution)/shard_map/ppermute | solution.py:59
  161.2 1.9 collective-permute-start.19
  165.5 3.3 %collective-permute-done.19 = bf16[8,9,2304]{2,0,1:T(8,128)(2,1)S(1)} collective-permute-done((bf16[8,9,2304]{2,0,1:T(8,128)(2,1)S(1)}, bf16[8,9,2304]{2,0,1:T(8,128)(2,1)S(1)}, u32[]{:S(2)}, u32[]{:S(2)}) %collective-permute-start.19) | collective-permute-done | bytes 331808 | tf_op jit(solution)/shard_map/ppermute | solution.py:59
  169.4 3.3 %collective-permute-done.38 = bf16[2,96,768]{2,1,0:T(8,128)(2,1)S(1)} collective-permute-done((bf16[2,96,768]{2,1,0:T(8,128)(2,1)S(1)}, bf16[2,96,768]{2,1,0:T(8,128)(2,1)S(1)}, u32[]{:S(2)}, u32[]{:S(2)}) %collective-permute-start.38) | collective-permute-done | bytes 294944 | tf_op jit(solution)/shard_map/ppermute | solution.py:59
  173.9 2.0 collective-permute-done.28
  178.9 2.2 collective-permute-done.29
  192.2 2.1 reshape.177
  194.3 2.1 reshape.178
  214.6 1.8 collective-permute-start.26
  216.5 6.7 %collective-permute-done.36 = bf16[1,96,1536]{2,1,0:T(8,128)(2,1)S(1)} collective-permute-done((bf16[1,96,1536]{2,1,0:T(8,128)(2,1)S(1)}, bf16[1,96,1536]{2,1,0:T(8,128)(2,1)S(1)}, u32[]{:S(2)}, u32[]{:S(2)}) %collective-permute-start.36) | collective-permute-done | bytes 294944 | tf_op jit(solution)/shard_map/ppermute | solution.py:59
  224.3 3.9 %collective-permute-start.40 = (bf16[96,1152]{1,0:T(8,128)(2,1)S(1)}, bf16[96,1152]{1,0:T(8,128)(2,1)S(1)}, u32[]{:S(2)}, u32[]{:S(2)}) collective-permute-start(bf16[96,1152]{1,0:T(8,128)(2,1)S(1)} %broadcast_select_fusion.10), channel_id=1, source_target_pairs={{0,8},{4,12},{8,0},{12,4},{16,24},{20,28},{24,16},{28,20},{1,9},{5... | collective-permute-start | bytes 663560 | tf_op jit(solution)/shard_map/ppermute | solution.py:59
  230.0 3.9 %collective-permute-start.30 = (bf16[96,1152]{1,0:T(8,128)(2,1)S(1)}, bf16[96,1152]{1,0:T(8,128)(2,1)S(1)}, u32[]{:S(2)}, u32[]{:S(2)}) collective-permute-start(bf16[96,1152]{1,0:T(8,128)(2,1)S(1)} %broadcast_select_fusion.13), channel_id=1, source_target_pairs={{0,8},{4,12},{8,0},{12,4},{16,24},{20,28},{24,16},{28,20},{1,9},{5... | collective-permute-start | bytes 663560 | tf_op jit(solution)/shard_map/ppermute | solution.py:59
  234.1 2.6 collective-permute-start.41
  236.7 6.6 %collective-permute-done.30 = bf16[96,1152]{1,0:T(8,128)(2,1)S(1)} collective-permute-done((bf16[96,1152]{1,0:T(8,128)(2,1)S(1)}, bf16[96,1152]{1,0:T(8,128)(2,1)S(1)}, u32[]{:S(2)}, u32[]{:S(2)}) %collective-permute-start.30) | collective-permute-done | bytes 221216 | tf_op jit(solution)/shard_map/ppermute | solution.py:59
  244.6 5.9 %collective-permute-done.41 = bf16[96,1152]{1,0:T(8,128)(2,1)S(1)} collective-permute-done((bf16[96,1152]{1,0:T(8,128)(2,1)S(1)}, bf16[96,1152]{1,0:T(8,128)(2,1)S(1)}, u32[]{:S(2)}, u32[]{:S(2)}) %collective-permute-start.41) | collective-permute-done | bytes 221216 | tf_op jit(solution)/shard_map/ppermute | solution.py:59
  251.4 4.6 %collective-permute-done.31 = bf16[96,1152]{1,0:T(8,128)(2,1)S(1)} collective-permute-done((bf16[96,1152]{1,0:T(8,128)(2,1)S(1)}, bf16[96,1152]{1,0:T(8,128)(2,1)S(1)}, u32[]{:S(2)}, u32[]{:S(2)}) %collective-permute-start.31) | collective-permute-done | bytes 221216 | tf_op jit(solution)/shard_map/ppermute | solution.py:59
  256.1 2.2 collective-permute-done.42
  258.7 4.2 %collective-permute-done.32 = bf16[96,1152]{1,0:T(8,128)(2,1)S(1)} collective-permute-done((bf16[96,1152]{1,0:T(8,128)(2,1)S(1)}, bf16[96,1152]{1,0:T(8,128)(2,1)S(1)}, u32[]{:S(2)}, u32[]{:S(2)}) %collective-permute-start.32) | collective-permute-done | bytes 221216 | tf_op jit(solution)/shard_map/ppermute | solution.py:59
  266.9 4.4 %collective-permute-done.43.refs_3_ = bf16[96,2304]{1,0:T(8,128)(2,1)S(1)} collective-permute-done((bf16[96,2304]{1,0:T(8,128)(2,1)S(1)}, bf16[96,2304]{1,0:T(8,128)(2,1)S(1)}, u32[]{:S(2)}, u32[]{:S(2)}) %collective-permute-start.43) | collective-permute-done | bytes 442400 | tf_op jit(solution)/shard_map/ppermute | solution.py:59
  271.4 6.0 %collective-permute-done.33.refs_1_ = bf16[96,2304]{1,0:T(8,128)(2,1)S(1)} collective-permute-done((bf16[96,2304]{1,0:T(8,128)(2,1)S(1)}, bf16[96,2304]{1,0:T(8,128)(2,1)S(1)}, u32[]{:S(2)}, u32[]{:S(2)}) %collective-permute-start.33) | collective-permute-done | bytes 442400 | tf_op jit(solution)/shard_map/ppermute | solution.py:59
  278.2 3.4 %unpack.1 = (f32[2,96,1152]{2,1,0:T(8,128)}, f32[2,96,384]{2,1,0:T(8,128)}, f32[2,96,1536]{2,1,0:T(8,128)}, f32[2,384,384]{2,1,0:T(8,128)}) custom-call(s32[1]{0:T(128)} %bitcast.37.flag, bf16[96,2304]{1,0:T(8,128)(2,1)} %copy-done.3, bf16[96,2304]{1,0:T(8,128)(2,1)} %copy-done.17, bf16[96,2304]{1,0:T(8,128)(2,1)} %copy-done.2, bf16[96,2304]{1,0:T(8,128)(2,1)} %copy-done.16), custom_call_target="tpu_custom_call" | custom-call | tf_op jit(solution)/shard_map/unpack/pallas_call | solution.py:445
  (280 shorter events, 71.5 us)
Async XLA Ops:
  5.2 32.1 %collective-permute-start.8 = (bf16[96,3072]{1,0:T(8,128)(2,1)S(1)}, bf16[96,3072]{1,0:T(8,128)(2,1)S(1)}, u32[]{:S(2)}, u32[]{:S(2)}) collective-permute-start(bf16[96,3072]{1,0:T(8,128)(2,1)S(1)} %get-tuple-element.99.rest_4_.rest_0_), channel_id=1, source_target_pairs={{0,2},{1,3},{2,0},{3,1},{4,6},{5,7},{6,4},{7,5},{8,10},{9,11},{10,... | collective-permute-start | bytes 1769480 | tf_op jit(solution)/shard_map/ppermute | solution.py:59
  8.2 48.9 %collective-permute-start.7 = (bf16[96,3072]{1,0:T(8,128)(2,1)S(1)}, bf16[96,3072]{1,0:T(8,128)(2,1)S(1)}, u32[]{:S(2)}, u32[]{:S(2)}) collective-permute-start(bf16[96,3072]{1,0:T(8,128)(2,1)S(1)} %get-tuple-element.99.rest_4_.rest_0_), channel_id=1, source_target_pairs={{0,1},{1,0},{2,3},{3,2},{4,5},{5,4},{6,7},{7,6},{8,9},{9,8},{10,11... | collective-permute-start | bytes 1769480 | tf_op jit(solution)/shard_map/ppermute | solution.py:59
  8.3 28.6 %collective-permute-start.5 = (bf16[96,1536]{1,0:T(8,128)(2,1)S(1)}, bf16[96,1536]{1,0:T(8,128)(2,1)}, u32[]{:S(2)}, u32[]{:S(2)}) collective-permute-start(bf16[96,1536]{1,0:T(8,128)(2,1)S(1)} %pad_maximum_fusion.6.rest_0_), channel_id=1, source_target_pairs={{0,2},{1,3},{2,0},{3,1},{4,6},{5,7},{6,4},{7,5},{8,10},{9,11},{10,... | collective-permute-start | bytes 884744 | tf_op jit(solution)/shard_map/ppermute | solution.py:59
  8.4 28.8 %collective-permute-start.4 = (bf16[96,1536]{1,0:T(8,128)(2,1)S(1)}, bf16[96,1536]{1,0:T(8,128)(2,1)}, u32[]{:S(2)}, u32[]{:S(2)}) collective-permute-start(bf16[96,1536]{1,0:T(8,128)(2,1)S(1)} %pad_maximum_fusion.6.rest_0_), channel_id=1, source_target_pairs={{0,1},{1,0},{2,3},{3,2},{4,5},{5,4},{6,7},{7,6},{8,9},{9,8},{10,11... | collective-permute-start | bytes 884744 | tf_op jit(solution)/shard_map/ppermute | solution.py:59
  12.1 16.0 %collective-permute-start.1 = (bf16[2,3456]{1,0:T(2,128)(2,1)S(1)}, bf16[2,3456]{1,0:T(2,128)(2,1)S(1)}, u32[]{:S(2)}, u32[]{:S(2)}) collective-permute-start(bf16[2,3456]{1,0:T(2,128)(2,1)S(1)} %pad_maximum_fusion.14), channel_id=1, source_target_pairs={{0,2},{1,3},{2,0},{3,1},{4,6},{5,7},{6,4},{7,5},{8,10},{9,11},{10,... | collective-permute-start | bytes 41480 | tf_op jit(solution)/shard_map/ppermute | solution.py:59
  35.1 20.9 %collective-permute-start.14 = (bf16[96,3072]{1,0:T(8,128)(2,1)}, bf16[96,3072]{1,0:T(8,128)(2,1)}, u32[]{:S(2)}, u32[]{:S(2)}) collective-permute-start(bf16[96,3072]{1,0:T(8,128)(2,1)} %get-tuple-element.98.rest_4_), channel_id=1, source_target_pairs={{0,2},{1,3},{2,0},{3,1},{4,6},{5,7},{6,4},{7,5},{8,10},{9,11},{10,... | collective-permute-start | bytes 1769480 | tf_op jit(solution)/shard_map/ppermute | solution.py:59
  36.9 19.1 %collective-permute-start.11 = (bf16[96,1536]{1,0:T(8,128)(2,1)S(1)}, bf16[96,1536]{1,0:T(8,128)(2,1)}, u32[]{:S(2)}, u32[]{:S(2)}) collective-permute-start(bf16[96,1536]{1,0:T(8,128)(2,1)S(1)} %pad_maximum_fusion.7.rest_0_), channel_id=1, source_target_pairs={{0,2},{1,3},{2,0},{3,1},{4,6},{5,7},{6,4},{7,5},{8,10},{9,11},{10,... | collective-permute-start | bytes 884744 | tf_op jit(solution)/shard_map/ppermute | solution.py:59
  37.3 20.0 %collective-permute-start.6 = (bf16[96,1536]{1,0:T(8,128)(2,1)}, bf16[96,1536]{1,0:T(8,128)(2,1)S(1)}, u32[]{:S(2)}, u32[]{:S(2)}) collective-permute-start(bf16[96,1536]{1,0:T(8,128)(2,1)} %collective-permute-done.5.rest_2_), channel_id=1, source_target_pairs={{0,1},{1,0},{2,3},{3,2},{4,5},{5,4},{6,7},{7,6},{8,9},{9,8},{10,11... | collective-permute-start | bytes 884744 | tf_op jit(solution)/shard_map/ppermute | solution.py:59
  37.3 21.1 %collective-permute-start.9 = (bf16[96,3072]{1,0:T(8,128)(2,1)S(1)}, bf16[96,3072]{1,0:T(8,128)(2,1)S(1)}, u32[]{:S(2)}, u32[]{:S(2)}) collective-permute-start(bf16[96,3072]{1,0:T(8,128)(2,1)S(1)} %collective-permute-done.8.rest_6_.rest_2_), channel_id=1, source_target_pairs={{0,1},{1,0},{2,3},{3,2},{4,5},{5,4},{6,7},{7,6},{8,9},{9,8},{10,11... | collective-permute-start | bytes 1769480 | tf_op jit(solution)/shard_map/ppermute | solution.py:59
  56.0 22.1 %collective-permute-start.13 = (bf16[96,3072]{1,0:T(8,128)(2,1)}, bf16[96,3072]{1,0:T(8,128)(2,1)}, u32[]{:S(2)}, u32[]{:S(2)}) collective-permute-start(bf16[96,3072]{1,0:T(8,128)(2,1)} %get-tuple-element.98.rest_4_), channel_id=1, source_target_pairs={{0,1},{1,0},{2,3},{3,2},{4,5},{5,4},{6,7},{7,6},{8,9},{9,8},{10,11... | collective-permute-start | bytes 1769480 | tf_op jit(solution)/shard_map/ppermute | solution.py:59
  56.0 22.1 %collective-permute-start.15 = (bf16[96,3072]{1,0:T(8,128)(2,1)}, bf16[96,3072]{1,0:T(8,128)(2,1)}, u32[]{:S(2)}, u32[]{:S(2)}) collective-permute-start(bf16[96,3072]{1,0:T(8,128)(2,1)} %collective-permute-done.14.rest_6_), channel_id=1, source_target_pairs={{0,1},{1,0},{2,3},{3,2},{4,5},{5,4},{6,7},{7,6},{8,9},{9,8},{10,11... | collective-permute-start | bytes 1769480 | tf_op jit(solution)/shard_map/ppermute | solution.py:59
  57.2 20.9 %collective-permute-start.10 = (bf16[96,1536]{1,0:T(8,128)(2,1)S(1)}, bf16[96,1536]{1,0:T(8,128)(2,1)S(1)}, u32[]{:S(2)}, u32[]{:S(2)}) collective-permute-start(bf16[96,1536]{1,0:T(8,128)(2,1)S(1)} %pad_maximum_fusion.7.rest_0_), channel_id=1, source_target_pairs={{0,1},{1,0},{2,3},{3,2},{4,5},{5,4},{6,7},{7,6},{8,9},{9,8},{10,11... | collective-permute-start | bytes 884744 | tf_op jit(solution)/shard_map/ppermute | solution.py:59
  57.3 20.8 %collective-permute-start.12 = (bf16[96,1536]{1,0:T(8,128)(2,1)}, bf16[96,1536]{1,0:T(8,128)(2,1)S(1)}, u32[]{:S(2)}, u32[]{:S(2)}) collective-permute-start(bf16[96,1536]{1,0:T(8,128)(2,1)} %collective-permute-done.11.rest_2_), channel_id=1, source_target_pairs={{0,1},{1,0},{2,3},{3,2},{4,5},{5,4},{6,7},{7,6},{8,9},{9,8},{10,11... | collective-permute-start | bytes 884744 | tf_op jit(solution)/shard_map/ppermute | solution.py:59
  154.3 27.5 %collective-permute-start.34 = (bf16[2,96,3072]{2,1,0:T(8,128)(2,1)S(1)}, bf16[2,96,3072]{2,1,0:T(8,128)(2,1)S(1)}, u32[]{:S(2)}, u32[]{:S(2)}) collective-permute-start(bf16[2,96,3072]{2,1,0:T(8,128)(2,1)S(1)} %copy-done.33), channel_id=1, source_target_pairs={{0,1},{1,0},{2,3},{3,2},{4,5},{5,4},{6,7},{7,6},{8,9},{9,8},{10,11... | collective-permute-start | bytes 3538952 | tf_op jit(solution)/shard_map/ppermute | solution.py:59
  154.8 9.8 %collective-permute-start.27 = (bf16[2,96,1536]{2,1,0:T(8,128)(2,1)}, bf16[2,96,1536]{2,1,0:T(8,128)(2,1)S(1)}, u32[]{:S(2)}, u32[]{:S(2)}) collective-permute-start(bf16[2,96,1536]{2,1,0:T(8,128)(2,1)} %get-tuple-element.73), channel_id=1, source_target_pairs={{0,1},{1,0},{2,3},{3,2},{4,5},{5,4},{6,7},{7,6},{8,9},{9,8},{10,11... | collective-permute-start | bytes 1769480 | tf_op jit(solution)/shard_map/ppermute | solution.py:59
  154.9 29.0 %collective-permute-start.24 = (bf16[2,96,3072]{2,1,0:T(8,128)(2,1)S(1)}, bf16[2,96,3072]{2,1,0:T(8,128)(2,1)S(1)}, u32[]{:S(2)}, u32[]{:S(2)}) collective-permute-start(bf16[2,96,3072]{2,1,0:T(8,128)(2,1)S(1)} %copy-done.34), channel_id=1, source_target_pairs={{0,1},{1,0},{2,3},{3,2},{4,5},{5,4},{6,7},{7,6},{8,9},{9,8},{10,11... | collective-permute-start | bytes 3538952 | tf_op jit(solution)/shard_map/ppermute | solution.py:59
  163.3 9.5 %collective-permute-start.38 = (bf16[2,96,768]{2,1,0:T(8,128)(2,1)S(1)}, bf16[2,96,768]{2,1,0:T(8,128)(2,1)S(1)}, u32[]{:S(2)}, u32[]{:S(2)}) collective-permute-start(bf16[2,96,768]{2,1,0:T(8,128)(2,1)S(1)} %get-tuple-element.91), channel_id=1, source_target_pairs={{0,4},{4,0},{8,12},{12,8},{16,20},{20,16},{24,28},{28,24},{1,5},{5... | collective-permute-start | bytes 884744 | tf_op jit(solution)/shard_map/ppermute | solution.py:59
  164.7 11.2 %collective-permute-start.28 = (bf16[2,96,768]{2,1,0:T(8,128)(2,1)S(1)}, bf16[2,96,768]{2,1,0:T(8,128)(2,1)S(1)}, u32[]{:S(2)}, u32[]{:S(2)}) collective-permute-start(bf16[2,96,768]{2,1,0:T(8,128)(2,1)S(1)} %get-tuple-element.93), channel_id=1, source_target_pairs={{0,4},{4,0},{8,12},{12,8},{16,20},{20,16},{24,28},{28,24},{1,5},{5... | collective-permute-start | bytes 884744 | tf_op jit(solution)/shard_map/ppermute | solution.py:59
  169.3 16.5 %collective-permute-start.20 = (bf16[16,9,2304]{2,0,1:T(8,128)(2,1)S(1)}, bf16[16,9,2304]{2,0,1:T(8,128)(2,1)S(1)}, u32[]{:S(2)}, u32[]{:S(2)}) collective-permute-start(bf16[16,9,2304]{2,0,1:T(8,128)(2,1)S(1)} %copy.50), channel_id=1, source_target_pairs={{0,1},{1,0},{2,3},{3,2},{4,5},{5,4},{6,7},{7,6},{8,9},{9,8},{10,11... | collective-permute-start | bytes 1990664 | tf_op jit(solution)/shard_map/ppermute | solution.py:59
  182.8 29.2 %collective-permute-start.35 = (bf16[1,96,3072]{2,1,0:T(8,128)(2,1)}, bf16[1,96,3072]{2,1,0:T(8,128)(2,1)}, u32[]{:S(2)}, u32[]{:S(2)}) collective-permute-start(bf16[1,96,3072]{2,1,0:T(8,128)(2,1)} %get-tuple-element.83), channel_id=1, source_target_pairs={{0,2},{1,3},{2,0},{3,1},{4,6},{5,7},{6,4},{7,5},{8,10},{9,11},{10,... | collective-permute-start | bytes 1769480 | tf_op jit(solution)/shard_map/ppermute | solution.py:59
  184.8 28.7 %collective-permute-start.25 = (bf16[1,96,3072]{2,1,0:T(8,128)(2,1)}, bf16[1,96,3072]{2,1,0:T(8,128)(2,1)}, u32[]{:S(2)}, u32[]{:S(2)}) collective-permute-start(bf16[1,96,3072]{2,1,0:T(8,128)(2,1)} %get-tuple-element.85), channel_id=1, source_target_pairs={{0,2},{1,3},{2,0},{3,1},{4,6},{5,7},{6,4},{7,5},{8,10},{9,11},{10,... | collective-permute-start | bytes 1769480 | tf_op jit(solution)/shard_map/ppermute | solution.py:59
  203.9 60.9 %collective-permute-start.21 = (f32[3,96]{1,0:T(4,128)S(1)}, f32[3,96]{1,0:T(4,128)S(1)}, u32[]{:S(2)}, u32[]{:S(2)}) collective-permute-start(f32[3,96]{1,0:T(4,128)S(1)} %bitcast.140), channel_id=1, source_target_pairs={{0,1},{1,0},{2,3},{3,2},{4,5},{5,4},{6,7},{7,6},{8,9},{9,8},{10,11... | collective-permute-start | bytes 3464 | tf_op jit(solution)/shard_map/ppermute | solution.py:59
  203.9 60.8 %collective-permute-start.22 = (f32[3,96]{1,0:T(4,128)S(1)}, f32[3,96]{1,0:T(4,128)}, u32[]{:S(2)}, u32[]{:S(2)}) collective-permute-start(f32[3,96]{1,0:T(4,128)S(1)} %bitcast.142), channel_id=1, source_target_pairs={{0,2},{1,3},{2,0},{3,1},{4,6},{5,7},{6,4},{7,5},{8,10},{9,11},{10,... | collective-permute-start | bytes 3464 | tf_op jit(solution)/shard_map/ppermute | solution.py:59
  205.6 59.8 %collective-permute-start.23 = (f32[3,96]{1,0:T(4,128)}, f32[3,96]{1,0:T(4,128)}, u32[]{:S(2)}, u32[]{:S(2)}) collective-permute-start(f32[3,96]{1,0:T(4,128)} %bitcast.123), channel_id=1, source_target_pairs={{0,3},{1,2},{2,1},{3,0},{4,7},{5,6},{6,5},{7,4},{8,11},{9,10},{10,... | collective-permute-start | bytes 3464 | tf_op jit(solution)/shard_map/ppermute | solution.py:59
  213.2 9.9 %collective-permute-start.36 = (bf16[1,96,1536]{2,1,0:T(8,128)(2,1)S(1)}, bf16[1,96,1536]{2,1,0:T(8,128)(2,1)S(1)}, u32[]{:S(2)}, u32[]{:S(2)}) collective-permute-start(bf16[1,96,1536]{2,1,0:T(8,128)(2,1)S(1)} %broadcast_select_fusion.4), channel_id=1, source_target_pairs={{0,4},{4,0},{8,12},{12,8},{16,20},{20,16},{24,28},{28,24},{1,5},{5... | collective-permute-start | bytes 884744 | tf_op jit(solution)/shard_map/ppermute | solution.py:59
  214.6 14.2 %collective-permute-start.26 = (bf16[1,96,1536]{2,1,0:T(8,128)(2,1)S(1)}, bf16[1,96,1536]{2,1,0:T(8,128)(2,1)S(1)}, u32[]{:S(2)}, u32[]{:S(2)}) collective-permute-start(bf16[1,96,1536]{2,1,0:T(8,128)(2,1)S(1)} %broadcast_select_fusion.5), channel_id=1, source_target_pairs={{0,4},{4,0},{8,12},{12,8},{16,20},{20,16},{24,28},{28,24},{1,5},{5... | collective-permute-start | bytes 884744 | tf_op jit(solution)/shard_map/ppermute | solution.py:59
  224.3 9.6 %collective-permute-start.40 = (bf16[96,1152]{1,0:T(8,128)(2,1)S(1)}, bf16[96,1152]{1,0:T(8,128)(2,1)S(1)}, u32[]{:S(2)}, u32[]{:S(2)}) collective-permute-start(bf16[96,1152]{1,0:T(8,128)(2,1)S(1)} %broadcast_select_fusion.10), channel_id=1, source_target_pairs={{0,8},{4,12},{8,0},{12,4},{16,24},{20,28},{24,16},{28,20},{1,9},{5... | collective-permute-start | bytes 663560 | tf_op jit(solution)/shard_map/ppermute | solution.py:59
  230.0 13.3 %collective-permute-start.30 = (bf16[96,1152]{1,0:T(8,128)(2,1)S(1)}, bf16[96,1152]{1,0:T(8,128)(2,1)S(1)}, u32[]{:S(2)}, u32[]{:S(2)}) collective-permute-start(bf16[96,1152]{1,0:T(8,128)(2,1)S(1)} %broadcast_select_fusion.13), channel_id=1, source_target_pairs={{0,8},{4,12},{8,0},{12,4},{16,24},{20,28},{24,16},{28,20},{1,9},{5... | collective-permute-start | bytes 663560 | tf_op jit(solution)/shard_map/ppermute | solution.py:59
  234.1 16.4 %collective-permute-start.41 = (bf16[96,1152]{1,0:T(8,128)(2,1)S(1)}, bf16[96,1152]{1,0:T(8,128)(2,1)S(1)}, u32[]{:S(2)}, u32[]{:S(2)}) collective-permute-start(bf16[96,1152]{1,0:T(8,128)(2,1)S(1)} %select_add_fusion), channel_id=1, source_target_pairs={{0,16},{4,20},{8,24},{12,28},{16,0},{20,4},{24,8},{28,12},{1,17},{... | collective-permute-start | bytes 663560 | tf_op jit(solution)/shard_map/ppermute | solution.py:59
  243.4 12.6 %collective-permute-start.31 = (bf16[96,1152]{1,0:T(8,128)(2,1)S(1)}, bf16[96,1152]{1,0:T(8,128)(2,1)S(1)}, u32[]{:S(2)}, u32[]{:S(2)}) collective-permute-start(bf16[96,1152]{1,0:T(8,128)(2,1)S(1)} %select_add_fusion.1), channel_id=1, source_target_pairs={{0,16},{4,20},{8,24},{12,28},{16,0},{20,4},{24,8},{28,12},{1,17},{... | collective-permute-start | bytes 663560 | tf_op jit(solution)/shard_map/ppermute | solution.py:59
  258.4 13.0 %collective-permute-start.43 = (bf16[96,2304]{1,0:T(8,128)(2,1)S(1)}, bf16[96,2304]{1,0:T(8,128)(2,1)S(1)}, u32[]{:S(2)}, u32[]{:S(2)}) collective-permute-start(bf16[96,2304]{1,0:T(8,128)(2,1)S(1)} %pad_maximum_fusion.5.refs_2_), channel_id=1, source_target_pairs={{0,4},{4,0},{8,12},{12,8},{16,20},{20,16},{24,28},{28,24},{1,5},{5... | collective-permute-start | bytes 1327112 | tf_op jit(solution)/shard_map/ppermute | solution.py:59
  263.1 14.3 %collective-permute-start.33 = (bf16[96,2304]{1,0:T(8,128)(2,1)S(1)}, bf16[96,2304]{1,0:T(8,128)(2,1)S(1)}, u32[]{:S(2)}, u32[]{:S(2)}) collective-permute-start(bf16[96,2304]{1,0:T(8,128)(2,1)S(1)} %pad_maximum_fusion.4.refs_0_), channel_id=1, source_target_pairs={{0,4},{4,0},{8,12},{12,8},{16,20},{20,16},{24,28},{28,24},{1,5},{5... | collective-permute-start | bytes 1327112 | tf_op jit(solution)/shard_map/ppermute | solution.py:59
  (50 other events, 457.4 us)

commit v5 on v4

--- a/solution.py
+++ b/solution.py
@@ -452,6 +452,67 @@
     )(flag, *parts)
 
 
+def small_kernel(starts, act, *refs):
+    out, work = refs[-2:]
+    work[...] = jnp.zeros_like(work[...])
+    for part, start in zip(refs[:-2], starts):
+        work[:LAYERS, start : start + part.shape[1]] = part[...].astype(jnp.float32)
+    work[LAYERS : LAYERS + act.shape[0], : act.shape[1]] = act[...].astype(jnp.float32)
+    out[...] = work[...].astype(out.dtype)
+
+
+def small_call(act, parts):
+    starts, total = [], 0
+    for part in parts:
+        starts.append(total)
+        total += -(-part.shape[1] // 128) * 128
+    shape = (-(-(LAYERS + act.shape[0]) // 16) * 16, max(total, act.shape[1]))
+    out = pl.pallas_call(
+        functools.partial(small_kernel, starts),
+        out_shape=jax.ShapeDtypeStruct(shape, jnp.bfloat16),
+        in_specs=[pl.BlockSpec(memory_space=pltpu.VMEM)] * (1 + len(parts)),
+        out_specs=pl.BlockSpec(memory_space=pltpu.VMEM),
+        scratch_shapes=[pltpu.VMEM(shape, jnp.float32)],
+        name="small_rows",
+    )(act, *parts)
+    return out, starts
+
+
+def gad_kernel(*refs):
+    out, work = refs[-2:]
+    if work.shape[0] > LAYERS * (refs[0].shape[0] + 1):
+        work[...] = jnp.zeros_like(work[...])
+    for n in range(LAYERS):
+        attn, mlp, proj, up, down = refs[5 * n : 5 * n + 5]
+        slots, _, width = attn.shape
+        base = n * (slots + 1)
+        for s in range(slots):
+            for k in range(3):
+                row = slice(base + s, base + s + 1)
+                work[row, k * width : (k + 1) * width] = attn[s, k : k + 1, :]
+                work[row, (3 + k) * width : (4 + k) * width] = mlp[s, k : k + 1, :]
+        row = slice(base + slots, base + slots + 1)
+        inner = up.shape[1]
+        work[row, :width] = proj[...]
+        work[row, width : width + inner] = up[...]
+        work[row, width + inner :] = down[...]
+    out[...] = work[...].astype(out.dtype)
+
+
+def gad_call(layers, wide):
+    slots = layers[0][0].shape[0]
+    shape = (-(-LAYERS * (slots + 1) // 8) * 8, wide)
+    parts = [part for layer in layers for part in layer]
+    return pl.pallas_call(
+        gad_kernel,
+        out_shape=jax.ShapeDtypeStruct(shape, jnp.bfloat16),
+        in_specs=[pl.BlockSpec(memory_space=pltpu.VMEM)] * len(parts),
+        out_specs=pl.BlockSpec(memory_space=pltpu.VMEM),
+        scratch_shapes=[pltpu.VMEM(shape, jnp.float32)],
+        name="gad_rows",
+    )(*parts)
+
+
 def per_slot(shape):
     rest = (0,) * (len(shape) - 1)
     return pl.BlockSpec((1,) + tuple(shape[1:]), lambda slot, info: (slot,) + rest)
@@ -563,13 +624,15 @@
     return [pieces[j] for j in range(size)]
 
 
-def gather_all(value, stages):
+def gather_all(value, stages, fast=False):
     for axis, size, bit in stages:
         other = swap(value, axis, size, bit)
         upper = has_bit(axis, bit)
-        value = jnp.concatenate(
-            [jnp.where(upper, other, value), jnp.where(upper, value, other)], axis=0
-        )
+        both = [jnp.where(upper, other, value), jnp.where(upper, value, other)]
+        if fast:
+            value = jnp.stack(both, axis=1).reshape((-1,) + value.shape[1:])
+        else:
+            value = jnp.concatenate(both, axis=0)
     return value
 
 
@@ -692,10 +755,9 @@
     shard_stages = [("fsdp", shards, bit) for bit in bits_of(shards)]
 
     act = jax.nn.silu(conditioning).astype(bf16)
-    shard_bias = jnp.concatenate([ada_bias, proj_bias, up_bias, down_bias], axis=1)
-    bias_width = shard_bias.shape[1]
-    small = jnp.concatenate([act.reshape(-1), shard_bias.reshape(-1)])[None]
-    small = gather_all(small, shard_stages)
+    parts = (ada_bias, proj_bias, up_bias, down_bias)
+    small, starts = small_call(act, parts)
+    small = gather_all(small[None], shard_stages[::-1], fast=True)
 
     attn_pieces, mlp_pieces = [], []
     for n in range(LAYERS):
@@ -705,8 +767,13 @@
         pack = jnp.concatenate([up_weight[n]] + blocks, axis=1)
         mlp_pieces.append(gather_rel(pack, "fsdp", shards))
 
-    act_group = small[:, : slots * width].reshape(shards * slots, width)
-    biases = small[:, slots * width :].reshape(shards, LAYERS, bias_width)
+    act_group = small[:, LAYERS : LAYERS + slots, :width].reshape(shards * slots, width)
+    group_stages = [("dp", groups, bit) for bit in bits_of(groups)[:1] + bits_of(groups)[:0:-1]]
+    acts = gather_all(act_group.reshape(1, shards, slots, width), group_stages)
+    counts = len(group_stages), len(shard_stages)
+    acts = acts.reshape([2] * sum(counts) + [slots, width])
+    order = list(range(sum(counts)))[: counts[0] - 1 : -1] + list(range(counts[0]))
+    acts = acts.transpose(order + [sum(counts), sum(counts) + 1]).reshape(-1, slots, width)
     act_cols = lax.dynamic_slice(act_group, (0, me * rows), (shards * slots, rows))
     partial = jnp.stack(
         [jnp.dot(act_cols, ada_weight[n], preferred_element_type=f32) for n in range(LAYERS)]
@@ -716,11 +783,11 @@
         for j in range(shards)
     ]
     ada = scatter_sum(blocks, "fsdp", shards).reshape(LAYERS, slots, wide)
-    cut = [0]
-    for part in (ada_bias, proj_bias, up_bias, down_bias):
-        cut.append(cut[-1] + part.shape[1])
     bias_of = [
-        [biases[:, n, cut[k] : cut[k + 1]].reshape(-1).astype(f32) for k in range(4)]
+        [
+            small[:, n, start : start + part.shape[1]].reshape(-1).astype(f32)
+            for part, start in zip(parts, starts)
+        ]
         for n in range(LAYERS)
     ]
     modulation = [(ada[n] + bias_of[n][0]).reshape(slots, 6, width) for n in range(LAYERS)]
@@ -746,17 +813,13 @@
         attn = early_sum(*attn_pair, first, attn_plan_of)
         sums[n] = late_sum(attn, mlp, groups)
 
-    def note_rows(n, gada_attn, gada_mlp, bias_grads):
-        flat = jnp.concatenate([gada_attn, gada_mlp], axis=1).reshape(slots, wide)
-        small_rows[n] = jnp.concatenate([flat, jnp.concatenate(bias_grads, axis=1)], axis=0)
-
     outs = last_block_call(
         dims, info, current, cotangent, modulation[top], bias_rows[top],
         attn_pieces[top], mlp_pieces[top],
     )
     block_out, grad, gada_attn, gada_mlp, b_proj, b_up, b_down = outs[:7]
     reduce_layer(top, outs[7:9], outs[9:11])
-    note_rows(top, gada_attn, gada_mlp, (b_proj, b_up, b_down))
+    small_rows[top] = (gada_attn, gada_mlp, b_proj, b_up, b_down)
     for n in reversed(range(top)):
         one, qkv, probs, mixed, attn, hidden, slope, branch = saved[n]
         g1, gada_mlp, b_up, b_down, *mlp_pair = mlp_back_call(
@@ -766,34 +829,45 @@
             dims, info, g1, inputs[n], modulation[n], qkv, probs, mixed, attn, attn_pieces[n]
         )
         reduce_layer(n, attn_pair, mlp_pair)
-        note_rows(n, gada_attn, gada_mlp, (b_proj, b_up, b_down))
-
-    flat = act.reshape(-1)
-    flat = jnp.pad(flat, (0, -flat.shape[0] % wide)).reshape(-1, wide)
-    message = jnp.concatenate([row.astype(bf16) for row in small_rows] + [flat], axis=0)
-    stages = [("dp", groups, bit) for bit in reversed(bits_of(groups))]
-    stages += [("fsdp", shards, bit) for bit in reversed(bits_of(shards))]
+        small_rows[n] = (gada_attn, gada_mlp, b_proj, b_up, b_down)
+
+    message = gad_call(small_rows, wide)
+    stages = group_stages + shard_stages[::-1]
     every = gather_all(message[None], stages)
     per_layer = slots + 1
-    gads = [every[:, n * per_layer : n * per_layer + slots] for n in range(LAYERS)]
-    acts = every[:, LAYERS * per_layer :].reshape(every.shape[0], -1)[:, : slots * width]
-    acts = acts.reshape(-1, width)
-    acts_cols = lax.dynamic_slice(acts, (0, me * rows), (acts.shape[0], rows))
-    g_ada = jnp.stack([outer_total(acts_cols, gads[n].reshape(-1, wide)) for n in range(LAYERS)])
-    totals = jnp.sum(every[:, : LAYERS * per_layer].astype(f32), axis=0)
-    totals = totals.reshape(LAYERS, per_layer, wide)
-    g_ada_bias = jnp.sum(totals[:, :slots], axis=1)
-    g_bias = totals[:, slots]
-
-    place = jnp.int32(0)
-    for k, bit in enumerate(reversed(bits_of(groups))):
-        place = place + has_bit("dp", bit).astype(jnp.int32) * (1 << k)
-    grid = every.reshape((shards, groups) + every.shape[1:])
-    mine = lax.dynamic_index_in_dim(grid, place, 1, keepdims=False)
+    acts_cols = lax.dynamic_slice(acts, (0, 0, me * rows), acts.shape[:2] + (rows,))
+    tail_rows = message.shape[0] - slots
+    flat = every.reshape(-1, wide)
+    g_ada = jnp.stack(
+        [
+            outer_total(
+                jnp.pad(
+                    acts_cols, ((0, 0), (n * per_layer, tail_rows - n * per_layer), (0, 0))
+                ).reshape(-1, rows),
+                flat,
+            )
+            for n in range(LAYERS)
+        ]
+    )
+    totals = jnp.sum(every.astype(f32), axis=0)
+    g_ada_bias = jnp.stack(
+        [jnp.sum(totals[n * per_layer : n * per_layer + slots], axis=0) for n in range(LAYERS)]
+    )
+    g_bias = jnp.stack([totals[n * per_layer + slots] for n in range(LAYERS)])
+
+    begin = [
+        has_bit(axis, bit).astype(jnp.int32) if axis == "dp" else jnp.int32(0)
+        for axis, _, bit in reversed(stages)
+    ]
+    extent = [1 if axis == "dp" else 2 for axis, _, _ in stages[::-1]]
+    grid = every.reshape([2] * len(stages) + list(message.shape))
+    zero = jnp.int32(0)
+    mine = lax.dynamic_slice(grid, begin + [zero, zero], extent + list(message.shape))
+    mine = mine.reshape(-1, wide)
     total = 0.0
     for n in range(LAYERS):
-        part = mine[:, n * per_layer : n * per_layer + slots].reshape(-1, wide)
-        total = total + matmul_back(part, ada_weight[n])
+        part = matmul_back(mine, ada_weight[n]).reshape(shards, -1, rows)
+        total = total + part[:, n * per_layer : n * per_layer + slots]
     total = total.reshape([2] * len(bits_of(shards)) + [slots, rows])
     order = tuple(reversed(range(len(bits_of(shards)))))
     total = total.transpose(order + (len(order), len(order) + 1)).reshape(shards, slots, rows)

time: 283 us -> 281 us (level)
  waiting for transfers between devices: 105 us -> 122 us
  local copies, waits for them, and re-layouts: 26.7 us -> 11.7 us
  other arithmetic: 22.5 us -> 12.4 us
  starting transfers between devices: 37.4 us -> 45.5 us
  matrix products: 5.48 us -> 1.74 us
    ppermute x44 -> x47, waiting for transfers between devices: 105 us -> 122 us  [swap(): return lax.ppermute(value, axis, [(i, i ^ bit) for i in range(size)])]
    reshape x11 -> x2, local copies, waits for them, and re-layouts: 9.9 us -> 0.05 us  [the longest x1 0.03 us: on_device(): acts.transpose(order + [sum(counts), sum(counts) + 1])]
    ppermute x44 -> x47, starting transfers between devices: 37.4 us -> 45.5 us  [swap(): return lax.ppermute(value, axis, [(i, i ^ bit) for i in range(size)])]
    concatenate x11 -> x8, other arithmetic: 4.14 us -> 0.34 us  [gather_all(): value = jnp.concatenate(both, axis=0)]
    unnamed x87 -> x49, local copies, waits for them, and re-layouts: 7.58 us -> 6.45 us
  transfers between devices with their start and end apart: 44 -> 47, of which waited for: 22 -> 24; matrix products, arithmetic and copies ran while one was open for 16% -> 7% of each run, Pallas kernels for 7% -> 29%
where the time goes in v5:
time: 281 us; the launch traced here: 280 us
  waiting for transfers between devices  122 us (43%)
  Pallas kernels  84.6 us (30%)
  starting transfers between devices  45.5 us (16%)
  other arithmetic  12.4 us (4%)
  local copies, waits for them, and re-layouts  11.7 us (4%)
    ppermute x47, waiting for transfers between devices, swap(): return lax.ppermute(value, axis, [(i, i ^ bit) for i in range(size)])  122 us
    pallas_call x4, Pallas kernels, run_kernel(): pl.pallas_call(functools.partial(kernel, shards, heads), out_shape=[jax.S...  78.4 us
    ppermute x47, starting transfers between devices, swap(): return lax.ppermute(value, axis, [(i, i ^ bit) for i in range(size)])  45.5 us
    unnamed x49, local copies, waits for them, and re-layouts  6.45 us
  transfers between devices with their start and end apart: 47, of which 24 were waited for; matrix products, arithmetic and copies ran while one was open for 7% of the time, Pallas kernels for 29%

profile of v5, /device:TPU:0, one launch (start us, length us, event | category | flops | bytes accessed | tf_op | source)
XLA Modules:
  0.0 280.0 jit_solution(7474405836402977081)
XLA Ops:
  2.9 3.1 %collective-permute-start.5 = (bf16[96,1536]{1,0:T(8,128)(2,1)S(1)}, bf16[96,1536]{1,0:T(8,128)(2,1)}, u32[]{:S(2)}, u32[]{:S(2)}) collective-permute-start(bf16[96,1536]{1,0:T(8,128)(2,1)S(1)} %pad_maximum_fusion.5.rest_0_), channel_id=1, source_target_pairs={{0,2},{1,3},{2,0},{3,1},{4,6},{5,7},{6,4},{7,5},{8,10},{9,11},{10,... | collective-permute-start | bytes 884744 | tf_op jit(solution)/shard_map/ppermute | solution.py:59
  14.9 11.5 %collective-permute-done = bf16[1,16,1280]{2,1,0:T(8,128)(2,1)S(1)} collective-permute-done((bf16[1,16,1280]{2,1,0:T(8,128)(2,1)}, bf16[1,16,1280]{2,1,0:T(8,128)(2,1)S(1)}, u32[]{:S(2)}, u32[]{:S(2)}) %collective-permute-start) | collective-permute-done | bytes 40992 | tf_op jit(solution)/shard_map/ppermute | solution.py:59
  39.1 7.5 %collective-permute-done.11.rest_2_ = bf16[96,1536]{1,0:T(8,128)(2,1)} collective-permute-done((bf16[96,1536]{1,0:T(8,128)(2,1)}, bf16[96,1536]{1,0:T(8,128)(2,1)}, u32[]{:S(2)}, u32[]{:S(2)}) %collective-permute-start.11) | collective-permute-done | bytes 294944 | tf_op jit(solution)/shard_map/ppermute | solution.py:59
  46.6 10.7 %collective-permute-done.14.rest_6_ = bf16[96,3072]{1,0:T(8,128)(2,1)} collective-permute-done((bf16[96,3072]{1,0:T(8,128)(2,1)}, bf16[96,3072]{1,0:T(8,128)(2,1)}, u32[]{:S(2)}, u32[]{:S(2)}) %collective-permute-start.14) | collective-permute-done | bytes 589856 | tf_op jit(solution)/shard_map/ppermute | solution.py:59
  61.1 18.8 %shard_map.220 = (f32[3,256,384]{2,1,0:T(8,128)}, f32[3,256,384]{2,1,0:T(8,128)}, bf16[3,256,1152]{2,1,0:T(8,128)(2,1)}, bf16[3,6,256,256]{3,2,1,0:T(8,128)(2,1)...) custom-call(s32[2]{0:T(128)} %pad_add_fusion.info, ...), custom_call_target="tpu_custom_call" | custom-call | flops 2717908992 | bytes 9437184 | tf_op jit(solution)/shard_map/pallas_call | solution.py:529
  80.8 32.2 %shard_map.221 = (f32[3,256,384]{2,1,0:T(8,128)}, f32[3,256,384]{2,1,0:T(8,128)}, f32[3,3,384]{2,1,0:T(4,128)}, f32[3,3,384]{2,1,0:T(4,128)}, f32[1,384]{1,0:T(1...) custom-call(s32[2]{0:T(128)} %pad_add_fusion.info, ...), custom_call_target="tpu_custom_call" | custom-call | flops 8153726976 | bytes 28311552 | tf_op jit(solution)/shard_map/pallas_call | solution.py:529
  113.0 12.6 %shard_map.222 = (f32[3,256,384]{2,1,0:T(8,128)}, f32[3,3,384]{2,1,0:T(4,128)}, f32[1,1536]{1,0:T(1,128)}, f32[1,384]{1,0:T(1,128)}, bf16[2,96,3072]{2,1,0:T(8,128)(2,1)}, /*index=5*/bf16[2,96,3072]{2,1,0:T(8,128)(2,1)}) custom-call(s32[2]{0:T(128)} %pad_add_fusion.info, f32[3,256,384]{2,1,0:T(8,128)} %get-tuple-element.49.grad, ...), custom_call_target="tpu_custom_call" | custom-call | flops 2717908992 | bytes 9437184 | tf_op jit(solution)/shard_map/pallas_call | solution.py:529
  125.6 14.7 %shard_map.223 = (f32[3,256,384]{2,1,0:T(8,128)}, f32[3,3,384]{2,1,0:T(4,128)}, f32[1,384]{1,0:T(1,128)}, bf16[2,96,1536]{2,1,0:T(8,128)(2,1)}, bf16[2,96,1536]{2,1,0:T(8,128)(2,1)}) custom-call(s32[2]{0:T(128)} %pad_add_fusion.info, f32[3,256,384]{2,1,0:T(8,128)} %get-tuple-element.54.grad, f32[3,256,384]{2,1,0:T(8,128)} %resid.3, ...), custom_call_target="tpu_custom_call" | custom-call | flops 2717908992 | bytes 9437184 | tf_op jit(solution)/shard_map/pallas_call | solution.py:529
  142.6 3.4 %collective-permute-done.16 = bf16[1,8,2304]{2,1,0:T(8,128)(2,1)S(1)} collective-permute-done((bf16[1,8,2304]{2,1,0:T(8,128)(2,1)}, bf16[1,8,2304]{2,1,0:T(8,128)(2,1)S(1)}, u32[]{:S(2)}, u32[]{:S(2)}) %collective-permute-start.16) | collective-permute-done | bytes 36896 | tf_op jit(solution)/shard_map/ppermute | solution.py:59
  146.9 3.0 %collective-permute-start.25 = (bf16[2,4,3,384]{3,2,1,0:T(4,128)(2,1)S(1)}, bf16[2,4,3,384]{3,2,1,0:T(4,128)(2,1)S(1)}, u32[]{:S(2)}, u32[]{:S(2)}) collective-permute-start(bf16[2,4,3,384]{3,2,1,0:T(4,128)(2,1)S(1)} %pad_maximum_fusion.16), channel_id=1, source_target_pairs={{0,16},{4,20},{8,24},{12,28},{16,0},{20,4},{24,8},{28,12},{1,17},{... | collective-permute-start | bytes 55304 | tf_op jit(solution)/shard_map/ppermute | solution.py:59
  149.8 2.2 collective-permute-done.17
  154.2 2.1 collective-permute-start.26
  157.4 2.7 collective-permute-start.19
  161.5 3.4 %collective-permute-done.19 = bf16[8,8,2304]{2,1,0:T(8,128)(2,1)S(1)} collective-permute-done((bf16[8,8,2304]{2,1,0:T(8,128)(2,1)S(1)}, bf16[8,8,2304]{2,1,0:T(8,128)(2,1)S(1)}, u32[]{:S(2)}, u32[]{:S(2)}) %collective-permute-start.19) | collective-permute-done | bytes 294944 | tf_op jit(solution)/shard_map/ppermute | solution.py:59
  165.0 2.5 collective-permute-start.31
  168.7 6.5 %collective-permute-done.31 = bf16[2,96,768]{2,1,0:T(8,128)(2,1)S(1)} collective-permute-done((bf16[2,96,768]{2,1,0:T(8,128)(2,1)S(1)}, bf16[2,96,768]{2,1,0:T(8,128)(2,1)S(1)}, u32[]{:S(2)}, u32[]{:S(2)}) %collective-permute-start.31) | collective-permute-done | bytes 294944 | tf_op jit(solution)/shard_map/ppermute | solution.py:59
  175.5 2.8 %collective-permute-done.41 = bf16[2,96,768]{2,1,0:T(8,128)(2,1)S(1)} collective-permute-done((bf16[2,96,768]{2,1,0:T(8,128)(2,1)S(1)}, bf16[2,96,768]{2,1,0:T(8,128)(2,1)S(1)}, u32[]{:S(2)}, u32[]{:S(2)}) %collective-permute-start.41) | collective-permute-done | bytes 294944 | tf_op jit(solution)/shard_map/ppermute | solution.py:59
  178.7 2.2 collective-permute-done.32
  180.9 2.6 collective-permute-done.42
  192.0 12.7 %collective-permute-done.28 = bf16[1,96,3072]{2,1,0:T(8,128)(2,1)S(1)} collective-permute-done((bf16[1,96,3072]{2,1,0:T(8,128)(2,1)S(1)}, bf16[1,96,3072]{2,1,0:T(8,128)(2,1)S(1)}, u32[]{:S(2)}, u32[]{:S(2)}) %collective-permute-start.28) | collective-permute-done | bytes 589856 | tf_op jit(solution)/shard_map/ppermute | solution.py:59
  206.5 10.2 %collective-permute-done.38 = bf16[1,96,3072]{2,1,0:T(8,128)(2,1)S(1)} collective-permute-done((bf16[1,96,3072]{2,1,0:T(8,128)(2,1)S(1)}, bf16[1,96,3072]{2,1,0:T(8,128)(2,1)S(1)}, u32[]{:S(2)}, u32[]{:S(2)}) %collective-permute-start.38) | collective-permute-done | bytes 589856 | tf_op jit(solution)/shard_map/ppermute | solution.py:59
  219.6 5.6 %collective-permute-done.39 = bf16[1,96,1536]{2,1,0:T(8,128)(2,1)S(1)} collective-permute-done((bf16[1,96,1536]{2,1,0:T(8,128)(2,1)S(1)}, bf16[1,96,1536]{2,1,0:T(8,128)(2,1)S(1)}, u32[]{:S(2)}, u32[]{:S(2)}) %collective-permute-start.39) | collective-permute-done | bytes 294944 | tf_op jit(solution)/shard_map/ppermute | solution.py:59
  226.4 5.1 %collective-permute-start.34 = (bf16[96,1152]{1,0:T(8,128)(2,1)S(1)}, bf16[96,1152]{1,0:T(8,128)(2,1)S(1)}, u32[]{:S(2)}, u32[]{:S(2)}) collective-permute-start(bf16[96,1152]{1,0:T(8,128)(2,1)S(1)} %select_add_fusion.1), channel_id=1, source_target_pairs={{0,16},{4,20},{8,24},{12,28},{16,0},{20,4},{24,8},{28,12},{1,17},{... | collective-permute-start | bytes 663560 | tf_op jit(solution)/shard_map/ppermute | solution.py:59
  231.5 3.0 %collective-permute-done.43 = bf16[96,1152]{1,0:T(8,128)(2,1)S(1)} collective-permute-done((bf16[96,1152]{1,0:T(8,128)(2,1)S(1)}, bf16[96,1152]{1,0:T(8,128)(2,1)S(1)}, u32[]{:S(2)}, u32[]{:S(2)}) %collective-permute-start.43) | collective-permute-done | bytes 221216 | tf_op jit(solution)/shard_map/ppermute | solution.py:59
  234.6 4.0 %collective-permute-start.44 = (bf16[96,1152]{1,0:T(8,128)(2,1)S(1)}, bf16[96,1152]{1,0:T(8,128)(2,1)S(1)}, u32[]{:S(2)}, u32[]{:S(2)}) collective-permute-start(bf16[96,1152]{1,0:T(8,128)(2,1)S(1)} %select_add_fusion), channel_id=1, source_target_pairs={{0,16},{4,20},{8,24},{12,28},{16,0},{20,4},{24,8},{28,12},{1,17},{... | collective-permute-start | bytes 663560 | tf_op jit(solution)/shard_map/ppermute | solution.py:59
  238.6 7.9 %collective-permute-done.34 = bf16[96,1152]{1,0:T(8,128)(2,1)S(1)} collective-permute-done((bf16[96,1152]{1,0:T(8,128)(2,1)S(1)}, bf16[96,1152]{1,0:T(8,128)(2,1)S(1)}, u32[]{:S(2)}, u32[]{:S(2)}) %collective-permute-start.34) | collective-permute-done | bytes 221216 | tf_op jit(solution)/shard_map/ppermute | solution.py:59
  247.4 2.4 collective-permute-done.44
  249.9 5.0 %collective-permute-done.35 = bf16[96,1152]{1,0:T(8,128)(2,1)S(1)} collective-permute-done((bf16[96,1152]{1,0:T(8,128)(2,1)S(1)}, bf16[96,1152]{1,0:T(8,128)(2,1)S(1)}, u32[]{:S(2)}, u32[]{:S(2)}) %collective-permute-start.35) | collective-permute-done | bytes 221216 | tf_op jit(solution)/shard_map/ppermute | solution.py:59
  255.1 4.1 %collective-permute-done.45 = bf16[96,1152]{1,0:T(8,128)(2,1)S(1)} collective-permute-done((bf16[96,1152]{1,0:T(8,128)(2,1)S(1)}, bf16[96,1152]{1,0:T(8,128)(2,1)S(1)}, u32[]{:S(2)}, u32[]{:S(2)}) %collective-permute-start.45) | collective-permute-done | bytes 221216 | tf_op jit(solution)/shard_map/ppermute | solution.py:59
  261.6 6.5 %collective-permute-done.36.refs_1_ = bf16[96,2304]{1,0:T(8,128)(2,1)S(1)} collective-permute-done((bf16[96,2304]{1,0:T(8,128)(2,1)S(1)}, bf16[96,2304]{1,0:T(8,128)(2,1)S(1)}, u32[]{:S(2)}, u32[]{:S(2)}) %collective-permute-start.36) | collective-permute-done | bytes 442400 | tf_op jit(solution)/shard_map/ppermute | solution.py:59
  268.1 7.7 %collective-permute-done.46.refs_3_ = bf16[96,2304]{1,0:T(8,128)(2,1)S(1)} collective-permute-done((bf16[96,2304]{1,0:T(8,128)(2,1)S(1)}, bf16[96,2304]{1,0:T(8,128)(2,1)S(1)}, u32[]{:S(2)}, u32[]{:S(2)}) %collective-permute-start.46) | collective-permute-done | bytes 442400 | tf_op jit(solution)/shard_map/ppermute | solution.py:59
  276.6 3.4 %unpack.1 = (f32[2,96,1152]{2,1,0:T(8,128)}, f32[2,96,384]{2,1,0:T(8,128)}, f32[2,96,1536]{2,1,0:T(8,128)}, f32[2,384,384]{2,1,0:T(8,128)}) custom-call(s32[1]{0:T(128)} %bitcast.47.flag, bf16[96,2304]{1,0:T(8,128)(2,1)} %copy-done, bf16[96,2304]{1,0:T(8,128)(2,1)} %copy-done.13, bf16[96,2304]{1,0:T(8,128)(2,1)} %copy-done.1, bf16[96,2304]{1,0:T(8,128)(2,1)} %copy-done.14), custom_call_target="tpu_custom_call" | custom-call | tf_op jit(solution)/shard_map/unpack/pallas_call | solution.py:445
  (227 shorter events, 55.8 us)
Async XLA Ops:
  2.9 35.3 %collective-permute-start.5 = (bf16[96,1536]{1,0:T(8,128)(2,1)S(1)}, bf16[96,1536]{1,0:T(8,128)(2,1)}, u32[]{:S(2)}, u32[]{:S(2)}) collective-permute-start(bf16[96,1536]{1,0:T(8,128)(2,1)S(1)} %pad_maximum_fusion.5.rest_0_), channel_id=1, source_target_pairs={{0,2},{1,3},{2,0},{3,1},{4,6},{5,7},{6,4},{7,5},{8,10},{9,11},{10,... | collective-permute-start | bytes 884744 | tf_op jit(solution)/shard_map/ppermute | solution.py:59
  5.9 32.6 %collective-permute-start.4 = (bf16[96,1536]{1,0:T(8,128)(2,1)S(1)}, bf16[96,1536]{1,0:T(8,128)(2,1)}, u32[]{:S(2)}, u32[]{:S(2)}) collective-permute-start(bf16[96,1536]{1,0:T(8,128)(2,1)S(1)} %pad_maximum_fusion.5.rest_0_), channel_id=1, source_target_pairs={{0,1},{1,0},{2,3},{3,2},{4,5},{5,4},{6,7},{7,6},{8,9},{9,8},{10,11... | collective-permute-start | bytes 884744 | tf_op jit(solution)/shard_map/ppermute | solution.py:59
  9.3 29.3 %collective-permute-start.8 = (bf16[96,3072]{1,0:T(8,128)(2,1)S(1)}, bf16[96,3072]{1,0:T(8,128)(2,1)S(1)}, u32[]{:S(2)}, u32[]{:S(2)}) collective-permute-start(bf16[96,3072]{1,0:T(8,128)(2,1)S(1)} %get-tuple-element.105.rest_4_.rest_0_), channel_id=1, source_target_pairs={{0,2},{1,3},{2,0},{3,1},{4,6},{5,7},{6,4},{7,5},{8,10},{9,11},{10,... | collective-permute-start | bytes 1769480 | tf_op jit(solution)/shard_map/ppermute | solution.py:59
  9.4 49.1 %collective-permute-start.7 = (bf16[96,3072]{1,0:T(8,128)(2,1)S(1)}, bf16[96,3072]{1,0:T(8,128)(2,1)S(1)}, u32[]{:S(2)}, u32[]{:S(2)}) collective-permute-start(bf16[96,3072]{1,0:T(8,128)(2,1)S(1)} %get-tuple-element.105.rest_4_.rest_0_), channel_id=1, source_target_pairs={{0,1},{1,0},{2,3},{3,2},{4,5},{5,4},{6,7},{7,6},{8,9},{9,8},{10,11... | collective-permute-start | bytes 1769480 | tf_op jit(solution)/shard_map/ppermute | solution.py:59
  11.9 14.6 %collective-permute-start = (bf16[1,16,1280]{2,1,0:T(8,128)(2,1)}, bf16[1,16,1280]{2,1,0:T(8,128)(2,1)S(1)}, u32[]{:S(2)}, u32[]{:S(2)}) collective-permute-start(bf16[1,16,1280]{2,1,0:T(8,128)(2,1)} %bitcast.130), channel_id=1, source_target_pairs={{0,2},{1,3},{2,0},{3,1},{4,6},{5,7},{6,4},{7,5},{8,10},{9,11},{10,... | collective-permute-start | bytes 122888 | tf_op jit(solution)/shard_map/ppermute | solution.py:59
  36.4 10.2 %collective-permute-start.11 = (bf16[96,1536]{1,0:T(8,128)(2,1)}, bf16[96,1536]{1,0:T(8,128)(2,1)}, u32[]{:S(2)}, u32[]{:S(2)}) collective-permute-start(bf16[96,1536]{1,0:T(8,128)(2,1)} %pad_maximum_fusion.6.rest_0_), channel_id=1, source_target_pairs={{0,2},{1,3},{2,0},{3,1},{4,6},{5,7},{6,4},{7,5},{8,10},{9,11},{10,... | collective-permute-start | bytes 884744 | tf_op jit(solution)/shard_map/ppermute | solution.py:59
  38.2 19.1 %collective-permute-start.14 = (bf16[96,3072]{1,0:T(8,128)(2,1)}, bf16[96,3072]{1,0:T(8,128)(2,1)}, u32[]{:S(2)}, u32[]{:S(2)}) collective-permute-start(bf16[96,3072]{1,0:T(8,128)(2,1)} %get-tuple-element.104.rest_4_), channel_id=1, source_target_pairs={{0,2},{1,3},{2,0},{3,1},{4,6},{5,7},{6,4},{7,5},{8,10},{9,11},{10,... | collective-permute-start | bytes 1769480 | tf_op jit(solution)/shard_map/ppermute | solution.py:59
  38.6 19.4 %collective-permute-start.6 = (bf16[96,1536]{1,0:T(8,128)(2,1)}, bf16[96,1536]{1,0:T(8,128)(2,1)}, u32[]{:S(2)}, u32[]{:S(2)}) collective-permute-start(bf16[96,1536]{1,0:T(8,128)(2,1)} %collective-permute-done.5.rest_2_), channel_id=1, source_target_pairs={{0,1},{1,0},{2,3},{3,2},{4,5},{5,4},{6,7},{7,6},{8,9},{9,8},{10,11... | collective-permute-start | bytes 884744 | tf_op jit(solution)/shard_map/ppermute | solution.py:59
  38.6 20.8 %collective-permute-start.9 = (bf16[96,3072]{1,0:T(8,128)(2,1)S(1)}, bf16[96,3072]{1,0:T(8,128)(2,1)S(1)}, u32[]{:S(2)}, u32[]{:S(2)}) collective-permute-start(bf16[96,3072]{1,0:T(8,128)(2,1)S(1)} %collective-permute-done.8.rest_6_.rest_2_), channel_id=1, source_target_pairs={{0,1},{1,0},{2,3},{3,2},{4,5},{5,4},{6,7},{7,6},{8,9},{9,8},{10,11... | collective-permute-start | bytes 1769480 | tf_op jit(solution)/shard_map/ppermute | solution.py:59
  46.6 33.4 %collective-permute-start.13 = (bf16[96,3072]{1,0:T(8,128)(2,1)}, bf16[96,3072]{1,0:T(8,128)(2,1)}, u32[]{:S(2)}, u32[]{:S(2)}) collective-permute-start(bf16[96,3072]{1,0:T(8,128)(2,1)} %get-tuple-element.104.rest_4_), channel_id=1, source_target_pairs={{0,1},{1,0},{2,3},{3,2},{4,5},{5,4},{6,7},{7,6},{8,9},{9,8},{10,11... | collective-permute-start | bytes 1769480 | tf_op jit(solution)/shard_map/ppermute | solution.py:59
  57.3 22.7 %collective-permute-start.15 = (bf16[96,3072]{1,0:T(8,128)(2,1)}, bf16[96,3072]{1,0:T(8,128)(2,1)}, u32[]{:S(2)}, u32[]{:S(2)}) collective-permute-start(bf16[96,3072]{1,0:T(8,128)(2,1)} %collective-permute-done.14.rest_6_), channel_id=1, source_target_pairs={{0,1},{1,0},{2,3},{3,2},{4,5},{5,4},{6,7},{7,6},{8,9},{9,8},{10,11... | collective-permute-start | bytes 1769480 | tf_op jit(solution)/shard_map/ppermute | solution.py:59
  58.0 22.0 %collective-permute-start.10 = (bf16[96,1536]{1,0:T(8,128)(2,1)}, bf16[96,1536]{1,0:T(8,128)(2,1)S(1)}, u32[]{:S(2)}, u32[]{:S(2)}) collective-permute-start(bf16[96,1536]{1,0:T(8,128)(2,1)} %pad_maximum_fusion.6.rest_0_), channel_id=1, source_target_pairs={{0,1},{1,0},{2,3},{3,2},{4,5},{5,4},{6,7},{7,6},{8,9},{9,8},{10,11... | collective-permute-start | bytes 884744 | tf_op jit(solution)/shard_map/ppermute | solution.py:59
  58.6 21.4 %collective-permute-start.12 = (bf16[96,1536]{1,0:T(8,128)(2,1)}, bf16[96,1536]{1,0:T(8,128)(2,1)S(1)}, u32[]{:S(2)}, u32[]{:S(2)}) collective-permute-start(bf16[96,1536]{1,0:T(8,128)(2,1)} %collective-permute-done.11.rest_2_), channel_id=1, source_target_pairs={{0,1},{1,0},{2,3},{3,2},{4,5},{5,4},{6,7},{7,6},{8,9},{9,8},{10,11... | collective-permute-start | bytes 884744 | tf_op jit(solution)/shard_map/ppermute | solution.py:59
  59.4 82.4 %collective-permute-start.24 = (bf16[1,4,3,384]{3,2,1,0:T(4,128)(2,1)S(1)}, bf16[1,4,3,384]{3,2,1,0:T(4,128)(2,1)S(1)}, u32[]{:S(2)}, u32[]{:S(2)}) collective-permute-start(bf16[1,4,3,384]{3,2,1,0:T(4,128)(2,1)S(1)} %get-tuple-element.128), channel_id=1, source_target_pairs={{0,4},{4,0},{8,12},{12,8},{16,20},{20,16},{24,28},{28,24},{1,5},{5... | collective-permute-start | bytes 27656 | tf_op jit(solution)/shard_map/ppermute | solution.py:59
  161.0 26.5 %collective-permute-start.27 = (bf16[2,96,3072]{2,1,0:T(8,128)(2,1)}, bf16[2,96,3072]{2,1,0:T(8,128)(2,1)S(1)}, u32[]{:S(2)}, u32[]{:S(2)}) collective-permute-start(bf16[2,96,3072]{2,1,0:T(8,128)(2,1)} %get-tuple-element.71), channel_id=1, source_target_pairs={{0,1},{1,0},{2,3},{3,2},{4,5},{5,4},{6,7},{7,6},{8,9},{9,8},{10,11... | collective-permute-start | bytes 3538952 | tf_op jit(solution)/shard_map/ppermute | solution.py:59
  161.0 27.7 %collective-permute-start.37 = (bf16[2,96,3072]{2,1,0:T(8,128)(2,1)}, bf16[2,96,3072]{2,1,0:T(8,128)(2,1)S(1)}, u32[]{:S(2)}, u32[]{:S(2)}) collective-permute-start(bf16[2,96,3072]{2,1,0:T(8,128)(2,1)} %get-tuple-element.75), channel_id=1, source_target_pairs={{0,1},{1,0},{2,3},{3,2},{4,5},{5,4},{6,7},{7,6},{8,9},{9,8},{10,11... | collective-permute-start | bytes 3538952 | tf_op jit(solution)/shard_map/ppermute | solution.py:59
  165.0 10.2 %collective-permute-start.31 = (bf16[2,96,768]{2,1,0:T(8,128)(2,1)S(1)}, bf16[2,96,768]{2,1,0:T(8,128)(2,1)S(1)}, u32[]{:S(2)}, u32[]{:S(2)}) collective-permute-start(bf16[2,96,768]{2,1,0:T(8,128)(2,1)S(1)} %get-tuple-element.99), channel_id=1, source_target_pairs={{0,4},{4,0},{8,12},{12,8},{16,20},{20,16},{24,28},{28,24},{1,5},{5... | collective-permute-start | bytes 884744 | tf_op jit(solution)/shard_map/ppermute | solution.py:59
  167.6 10.7 %collective-permute-start.41 = (bf16[2,96,768]{2,1,0:T(8,128)(2,1)S(1)}, bf16[2,96,768]{2,1,0:T(8,128)(2,1)S(1)}, u32[]{:S(2)}, u32[]{:S(2)}) collective-permute-start(bf16[2,96,768]{2,1,0:T(8,128)(2,1)S(1)} %get-tuple-element.97), channel_id=1, source_target_pairs={{0,4},{4,0},{8,12},{12,8},{16,20},{20,16},{24,28},{28,24},{1,5},{5... | collective-permute-start | bytes 884744 | tf_op jit(solution)/shard_map/ppermute | solution.py:59
  168.6 15.0 %collective-permute-start.20 = (bf16[16,8,2304]{2,1,0:T(8,128)(2,1)S(1)}, bf16[16,8,2304]{2,1,0:T(8,128)(2,1)S(1)}, u32[]{:S(2)}, u32[]{:S(2)}) collective-permute-start(bf16[16,8,2304]{2,1,0:T(8,128)(2,1)S(1)} %pad_maximum_fusion.2), channel_id=1, source_target_pairs={{0,1},{1,0},{2,3},{3,2},{4,5},{5,4},{6,7},{7,6},{8,9},{9,8},{10,11... | collective-permute-start | bytes 1769480 | tf_op jit(solution)/shard_map/ppermute | solution.py:59
  184.6 76.1 %collective-permute-start.21 = (f32[3,96]{1,0:T(4,128)S(1)}, f32[3,96]{1,0:T(4,128)S(1)}, u32[]{:S(2)}, u32[]{:S(2)}) collective-permute-start(f32[3,96]{1,0:T(4,128)S(1)} %bitcast.139), channel_id=1, source_target_pairs={{0,1},{1,0},{2,3},{3,2},{4,5},{5,4},{6,7},{7,6},{8,9},{9,8},{10,11... | collective-permute-start | bytes 3464 | tf_op jit(solution)/shard_map/ppermute | solution.py:59
  184.7 76.1 %collective-permute-start.22 = (f32[3,96]{1,0:T(4,128)S(1)}, f32[3,96]{1,0:T(4,128)S(1)}, u32[]{:S(2)}, u32[]{:S(2)}) collective-permute-start(f32[3,96]{1,0:T(4,128)S(1)} %bitcast.138), channel_id=1, source_target_pairs={{0,2},{1,3},{2,0},{3,1},{4,6},{5,7},{6,4},{7,5},{8,10},{9,11},{10,... | collective-permute-start | bytes 3464 | tf_op jit(solution)/shard_map/ppermute | solution.py:59
  185.0 75.8 %collective-permute-start.23 = (f32[3,96]{1,0:T(4,128)S(1)}, f32[3,96]{1,0:T(4,128)S(1)}, u32[]{:S(2)}, u32[]{:S(2)}) collective-permute-start(f32[3,96]{1,0:T(4,128)S(1)} %bitcast.137), channel_id=1, source_target_pairs={{0,3},{1,2},{2,1},{3,0},{4,7},{5,6},{6,5},{7,4},{8,11},{9,10},{10,... | collective-permute-start | bytes 3464 | tf_op jit(solution)/shard_map/ppermute | solution.py:59
  188.4 16.3 %collective-permute-start.28 = (bf16[1,96,3072]{2,1,0:T(8,128)(2,1)S(1)}, bf16[1,96,3072]{2,1,0:T(8,128)(2,1)S(1)}, u32[]{:S(2)}, u32[]{:S(2)}) collective-permute-start(bf16[1,96,3072]{2,1,0:T(8,128)(2,1)S(1)} %get-tuple-element.95), channel_id=1, source_target_pairs={{0,2},{1,3},{2,0},{3,1},{4,6},{5,7},{6,4},{7,5},{8,10},{9,11},{10,... | collective-permute-start | bytes 1769480 | tf_op jit(solution)/shard_map/ppermute | solution.py:59
  189.6 27.0 %collective-permute-start.38 = (bf16[1,96,3072]{2,1,0:T(8,128)(2,1)S(1)}, bf16[1,96,3072]{2,1,0:T(8,128)(2,1)S(1)}, u32[]{:S(2)}, u32[]{:S(2)}) collective-permute-start(bf16[1,96,3072]{2,1,0:T(8,128)(2,1)S(1)} %get-tuple-element.93), channel_id=1, source_target_pairs={{0,2},{1,3},{2,0},{3,1},{4,6},{5,7},{6,4},{7,5},{8,10},{9,11},{10,... | collective-permute-start | bytes 1769480 | tf_op jit(solution)/shard_map/ppermute | solution.py:59
  204.7 13.8 %collective-permute-start.29 = (bf16[1,96,1536]{2,1,0:T(8,128)(2,1)S(1)}, bf16[1,96,1536]{2,1,0:T(8,128)(2,1)S(1)}, u32[]{:S(2)}, u32[]{:S(2)}) collective-permute-start(bf16[1,96,1536]{2,1,0:T(8,128)(2,1)S(1)} %broadcast_select_fusion.7), channel_id=1, source_target_pairs={{0,4},{4,0},{8,12},{12,8},{16,20},{20,16},{24,28},{28,24},{1,5},{5... | collective-permute-start | bytes 884744 | tf_op jit(solution)/shard_map/ppermute | solution.py:59
  216.7 8.5 %collective-permute-start.39 = (bf16[1,96,1536]{2,1,0:T(8,128)(2,1)S(1)}, bf16[1,96,1536]{2,1,0:T(8,128)(2,1)S(1)}, u32[]{:S(2)}, u32[]{:S(2)}) collective-permute-start(bf16[1,96,1536]{2,1,0:T(8,128)(2,1)S(1)} %broadcast_select_fusion.6), channel_id=1, source_target_pairs={{0,4},{4,0},{8,12},{12,8},{16,20},{20,16},{24,28},{28,24},{1,5},{5... | collective-permute-start | bytes 884744 | tf_op jit(solution)/shard_map/ppermute | solution.py:59
  225.4 9.2 %collective-permute-start.43 = (bf16[96,1152]{1,0:T(8,128)(2,1)S(1)}, bf16[96,1152]{1,0:T(8,128)(2,1)S(1)}, u32[]{:S(2)}, u32[]{:S(2)}) collective-permute-start(bf16[96,1152]{1,0:T(8,128)(2,1)S(1)} %broadcast_select_fusion.12), channel_id=1, source_target_pairs={{0,8},{4,12},{8,0},{12,4},{16,24},{20,28},{24,16},{28,20},{1,9},{5... | collective-permute-start | bytes 663560 | tf_op jit(solution)/shard_map/ppermute | solution.py:59
  226.4 20.1 %collective-permute-start.34 = (bf16[96,1152]{1,0:T(8,128)(2,1)S(1)}, bf16[96,1152]{1,0:T(8,128)(2,1)S(1)}, u32[]{:S(2)}, u32[]{:S(2)}) collective-permute-start(bf16[96,1152]{1,0:T(8,128)(2,1)S(1)} %select_add_fusion.1), channel_id=1, source_target_pairs={{0,16},{4,20},{8,24},{12,28},{16,0},{20,4},{24,8},{28,12},{1,17},{... | collective-permute-start | bytes 663560 | tf_op jit(solution)/shard_map/ppermute | solution.py:59
  234.6 15.2 %collective-permute-start.44 = (bf16[96,1152]{1,0:T(8,128)(2,1)S(1)}, bf16[96,1152]{1,0:T(8,128)(2,1)S(1)}, u32[]{:S(2)}, u32[]{:S(2)}) collective-permute-start(bf16[96,1152]{1,0:T(8,128)(2,1)S(1)} %select_add_fusion), channel_id=1, source_target_pairs={{0,16},{4,20},{8,24},{12,28},{16,0},{20,4},{24,8},{28,12},{1,17},{... | collective-permute-start | bytes 663560 | tf_op jit(solution)/shard_map/ppermute | solution.py:59
  249.9 9.3 %collective-permute-start.45 = (bf16[96,1152]{1,0:T(8,128)(2,1)S(1)}, bf16[96,1152]{1,0:T(8,128)(2,1)S(1)}, u32[]{:S(2)}, u32[]{:S(2)}) collective-permute-start(bf16[96,1152]{1,0:T(8,128)(2,1)S(1)} %add.228), channel_id=1, source_target_pairs={{0,8},{4,12},{8,0},{12,4},{16,24},{20,28},{24,16},{28,20},{1,9},{5... | collective-permute-start | bytes 663560 | tf_op jit(solution)/shard_map/ppermute | solution.py:59
  255.0 13.1 %collective-permute-start.36 = (bf16[96,2304]{1,0:T(8,128)(2,1)S(1)}, bf16[96,2304]{1,0:T(8,128)(2,1)S(1)}, u32[]{:S(2)}, u32[]{:S(2)}) collective-permute-start(bf16[96,2304]{1,0:T(8,128)(2,1)S(1)} %pad_maximum_fusion.3.refs_0_), channel_id=1, source_target_pairs={{0,4},{4,0},{8,12},{12,8},{16,20},{20,16},{24,28},{28,24},{1,5},{5... | collective-permute-start | bytes 1327112 | tf_op jit(solution)/shard_map/ppermute | solution.py:59
  259.3 16.5 %collective-permute-start.46 = (bf16[96,2304]{1,0:T(8,128)(2,1)S(1)}, bf16[96,2304]{1,0:T(8,128)(2,1)S(1)}, u32[]{:S(2)}, u32[]{:S(2)}) collective-permute-start(bf16[96,2304]{1,0:T(8,128)(2,1)S(1)} %pad_maximum_fusion.4.refs_2_), channel_id=1, source_target_pairs={{0,4},{4,0},{8,12},{12,8},{16,20},{20,16},{24,28},{28,24},{1,5},{5... | collective-permute-start | bytes 1327112 | tf_op jit(solution)/shard_map/ppermute | solution.py:59
  (36 other events, 241.0 us)

commit v6 on v5

--- a/solution.py
+++ b/solution.py
@@ -478,6 +478,31 @@
     return out, starts
 
 
+def pack_kernel(qkv, proj, up, down, *outs):
+    rows, triple = qkv.shape[1:]
+    inner, width = up.shape[2], down.shape[2]
+    for n in range(LAYERS):
+        attn, mlp = outs[2 * n], outs[2 * n + 1]
+        attn[:, :triple] = qkv[n]
+        attn[:, triple:] = proj[n]
+        mlp[:, :inner] = up[n]
+        for q in range(inner // width):
+            mlp[:, inner + q * width : inner + (q + 1) * width] = down[n, q * rows : (q + 1) * rows, :]
+
+
+def pack_call(qkv, proj, up, down):
+    rows, triple = qkv.shape[1:]
+    inner, width = up.shape[2], down.shape[2]
+    shapes = [(rows, triple + width), (rows, 2 * inner)] * LAYERS
+    return pl.pallas_call(
+        pack_kernel,
+        out_shape=[jax.ShapeDtypeStruct(s, qkv.dtype) for s in shapes],
+        in_specs=[pl.BlockSpec(memory_space=pltpu.VMEM)] * 4,
+        out_specs=[pl.BlockSpec(memory_space=pltpu.VMEM)] * len(shapes),
+        name="pack_weights",
+    )(qkv, proj, up, down)
+
+
 def gad_kernel(*refs):
     out, work = refs[-2:]
     if work.shape[0] > LAYERS * (refs[0].shape[0] + 1):
@@ -750,7 +775,6 @@
     rows = qkv_weight.shape[1]
     triple, inner = qkv_weight.shape[2], up_weight.shape[2]
     wide = ada_weight.shape[2]
-    ratio = inner // width
     me = lax.axis_index("fsdp")
     shard_stages = [("fsdp", shards, bit) for bit in bits_of(shards)]
 
@@ -760,12 +784,10 @@
     small = gather_all(small[None], shard_stages[::-1], fast=True)
 
     attn_pieces, mlp_pieces = [], []
+    packs = pack_call(qkv_weight, proj_weight, up_weight, down_weight)
     for n in range(LAYERS):
-        pack = jnp.concatenate([qkv_weight[n], proj_weight[n]], axis=1)
-        attn_pieces.append(gather_rel(pack, "fsdp", shards))
-        blocks = [down_weight[n, q * rows : (q + 1) * rows] for q in range(ratio)]
-        pack = jnp.concatenate([up_weight[n]] + blocks, axis=1)
-        mlp_pieces.append(gather_rel(pack, "fsdp", shards))
+        attn_pieces.append(gather_rel(packs[2 * n], "fsdp", shards))
+        mlp_pieces.append(gather_rel(packs[2 * n + 1], "fsdp", shards))
 
     act_group = small[:, LAYERS : LAYERS + slots, :width].reshape(shards * slots, width)
     group_stages = [("dp", groups, bit) for bit in bits_of(groups)[:1] + bits_of(groups)[:0:-1]]

time: 281 us -> 273 us (0.972); the launches traced: 280 us -> 269 us
  local copies, waits for them, and re-layouts: 11.7 us -> 5.5 us
  starting transfers between devices: 45.5 us -> 42 us
    ppermute x47, starting transfers between devices: 45.5 us -> 42 us  [swap(): return lax.ppermute(value, axis, [(i, i ^ bit) for i in range(size)])]
    unnamed x49 -> x41, local copies, waits for them, and re-layouts: 6.45 us -> 3.02 us
  transfers between devices with their start and end apart: 47 -> 47, of which waited for: 24 -> 23; matrix products, arithmetic and copies ran while one was open for 7% -> 5% of each run, Pallas kernels for 29% -> 31%
where the time goes in v6:
time: 273 us; the launch traced here: 269 us
  waiting for transfers between devices  120 us (44%)
  Pallas kernels  87.3 us (32%)
  starting transfers between devices  42 us (15%)
  other arithmetic  10.9 us (4%)
  local copies, waits for them, and re-layouts  5.5 us (2%)
    ppermute x47, waiting for transfers between devices, swap(): return lax.ppermute(value, axis, [(i, i ^ bit) for i in range(size)])  120 us
    pallas_call x4, Pallas kernels, run_kernel(): pl.pallas_call(functools.partial(kernel, shards, heads), out_shape=[jax.S...  78.4 us
    ppermute x47, starting transfers between devices, swap(): return lax.ppermute(value, axis, [(i, i ^ bit) for i in range(size)])  42 us
  transfers between devices with their start and end apart: 47, of which 23 were waited for; matrix products, arithmetic and copies ran while one was open for 5% of the time, Pallas kernels for 31%

profile of v6, /device:TPU:0, one launch (start us, length us, event | category | flops | bytes accessed | tf_op | source)
XLA Modules:
  0.0 269.0 jit_solution(16992900610966394817)
XLA Ops:
  3.3 3.0 %collective-permute-start = (bf16[1,16,1280]{2,1,0:T(8,128)(2,1)}, bf16[1,16,1280]{2,1,0:T(8,128)(2,1)S(1)}, u32[]{:S(2)}, u32[]{:S(2)}) collective-permute-start(bf16[1,16,1280]{2,1,0:T(8,128)(2,1)} %bitcast.102), channel_id=1, source_target_pairs={{0,2},{1,3},{2,0},{3,1},{4,6},{5,7},{6,4},{7,5},{8,10},{9,11},{10,... | collective-permute-start | bytes 122888 | tf_op jit(solution)/shard_map/ppermute | solution.py:59
  6.3 2.7 %pack_weights.1 = (bf16[96,1536]{1,0:T(8,128)(2,1)}, bf16[96,3072]{1,0:T(8,128)(2,1)}, bf16[96,1536]{1,0:T(8,128)(2,1)}, bf16[96,3072]{1,0:T(8,128)(2,1)}) custom-call(bf16[2,96,1152]{2,1,0:T(8,128)(2,1)} %qkv.1, bf16[2,96,384]{2,1,0:T(8,128)(2,1)} %proj.1, bf16[2,96,1536]{2,1,0:T(8,128)(2,1)} %up.1, bf16[2,384,384]{2,1,0:T(8,128)(2,1)} %down.1), custom_call_target="tpu_custom_call" | custom-call | tf_op jit(solution)/shard_map/pack_weights/pallas_call | solution.py:497
  9.1 2.0 collective-permute-start.8
  18.4 13.1 %collective-permute-done.3 = f32[1,6,2304]{2,0,1:T(1,128)S(1)} collective-permute-done((f32[1,6,2304]{2,0,1:T(1,128)S(1)}, f32[1,6,2304]{2,0,1:T(1,128)S(1)}, u32[]{:S(2)}, u32[]{:S(2)}) %collective-permute-start.3) | collective-permute-done | bytes 55328 | tf_op jit(solution)/shard_map/ppermute | solution.py:59
  31.8 7.3 %collective-permute-done.11.rest_2_ = bf16[96,1536]{1,0:T(8,128)(2,1)S(1)} collective-permute-done((bf16[96,1536]{1,0:T(8,128)(2,1)S(1)}, bf16[96,1536]{1,0:T(8,128)(2,1)S(1)}, u32[]{:S(2)}, u32[]{:S(2)}) %collective-permute-start.11) | collective-permute-done | bytes 294944 | tf_op jit(solution)/shard_map/ppermute | solution.py:59
  40.4 12.1 %collective-permute-done.14.rest_6_ = bf16[96,3072]{1,0:T(8,128)(2,1)} collective-permute-done((bf16[96,3072]{1,0:T(8,128)(2,1)}, bf16[96,3072]{1,0:T(8,128)(2,1)}, u32[]{:S(2)}, u32[]{:S(2)}) %collective-permute-start.14) | collective-permute-done | bytes 589856 | tf_op jit(solution)/shard_map/ppermute | solution.py:59
  56.1 18.8 %shard_map.220 = (f32[3,256,384]{2,1,0:T(8,128)}, f32[3,256,384]{2,1,0:T(8,128)}, bf16[3,256,1152]{2,1,0:T(8,128)(2,1)}, bf16[3,6,256,256]{3,2,1,0:T(8,128)(2,1)...) custom-call(s32[2]{0:T(128)} %pad_add_fusion.info, ...), custom_call_target="tpu_custom_call" | custom-call | flops 2717908992 | bytes 9437184 | tf_op jit(solution)/shard_map/pallas_call | solution.py:554
  75.8 32.2 %shard_map.221 = (f32[3,256,384]{2,1,0:T(8,128)}, f32[3,256,384]{2,1,0:T(8,128)}, f32[3,3,384]{2,1,0:T(4,128)}, f32[3,3,384]{2,1,0:T(4,128)}, f32[1,384]{1,0:T(1...) custom-call(s32[2]{0:T(128)} %pad_add_fusion.info, ...), custom_call_target="tpu_custom_call" | custom-call | flops 8153726976 | bytes 28311552 | tf_op jit(solution)/shard_map/pallas_call | solution.py:554
  108.1 12.6 %shard_map.222 = (f32[3,256,384]{2,1,0:T(8,128)}, f32[3,3,384]{2,1,0:T(4,128)}, f32[1,1536]{1,0:T(1,128)}, f32[1,384]{1,0:T(1,128)}, bf16[2,96,3072]{2,1,0:T(8,128)(2,1)}, /*index=5*/bf16[2,96,3072]{2,1,0:T(8,128)(2,1)}) custom-call(s32[2]{0:T(128)} %pad_add_fusion.info, f32[3,256,384]{2,1,0:T(8,128)} %get-tuple-element.57.grad, ...), custom_call_target="tpu_custom_call" | custom-call | flops 2717908992 | bytes 9437184 | tf_op jit(solution)/shard_map/pallas_call | solution.py:554
  120.7 14.7 %shard_map.223 = (f32[3,256,384]{2,1,0:T(8,128)}, f32[3,3,384]{2,1,0:T(4,128)}, f32[1,384]{1,0:T(1,128)}, bf16[2,96,1536]{2,1,0:T(8,128)(2,1)}, bf16[2,96,1536]{2,1,0:T(8,128)(2,1)}) custom-call(s32[2]{0:T(128)} %pad_add_fusion.info, f32[3,256,384]{2,1,0:T(8,128)} %get-tuple-element.62.grad, f32[3,256,384]{2,1,0:T(8,128)} %resid.3, ...), custom_call_target="tpu_custom_call" | custom-call | flops 2717908992 | bytes 9437184 | tf_op jit(solution)/shard_map/pallas_call | solution.py:554
  136.9 4.1 %collective-permute-done.16 = bf16[1,8,2304]{2,1,0:T(8,128)(2,1)S(1)} collective-permute-done((bf16[1,8,2304]{2,1,0:T(8,128)(2,1)}, bf16[1,8,2304]{2,1,0:T(8,128)(2,1)S(1)}, u32[]{:S(2)}, u32[]{:S(2)}) %collective-permute-start.16) | collective-permute-done | bytes 36896 | tf_op jit(solution)/shard_map/ppermute | solution.py:59
  141.9 3.0 %collective-permute-start.25 = (bf16[2,4,3,384]{3,2,1,0:T(4,128)(2,1)S(1)}, bf16[2,4,3,384]{3,2,1,0:T(4,128)(2,1)S(1)}, u32[]{:S(2)}, u32[]{:S(2)}) collective-permute-start(bf16[2,4,3,384]{3,2,1,0:T(4,128)(2,1)S(1)} %pad_maximum_fusion.14), channel_id=1, source_target_pairs={{0,16},{4,20},{8,24},{12,28},{16,0},{20,4},{24,8},{28,12},{1,17},{... | collective-permute-start | bytes 55304 | tf_op jit(solution)/shard_map/ppermute | solution.py:59
  144.9 2.2 collective-permute-done.17
  149.2 2.0 collective-permute-start.26
  155.5 3.8 %collective-permute-done.19 = bf16[8,8,2304]{2,1,0:T(8,128)(2,1)S(1)} collective-permute-done((bf16[8,8,2304]{2,1,0:T(8,128)(2,1)S(1)}, bf16[8,8,2304]{2,1,0:T(8,128)(2,1)S(1)}, u32[]{:S(2)}, u32[]{:S(2)}) %collective-permute-start.19) | collective-permute-done | bytes 294944 | tf_op jit(solution)/shard_map/ppermute | solution.py:59
  159.4 3.3 %collective-permute-start.31 = (bf16[2,96,768]{2,1,0:T(8,128)(2,1)S(1)}, bf16[2,96,768]{2,1,0:T(8,128)(2,1)S(1)}, u32[]{:S(2)}, u32[]{:S(2)}) collective-permute-start(bf16[2,96,768]{2,1,0:T(8,128)(2,1)S(1)} %get-tuple-element.107), channel_id=1, source_target_pairs={{0,4},{4,0},{8,12},{12,8},{16,20},{20,16},{24,28},{28,24},{1,5},{5... | collective-permute-start | bytes 884744 | tf_op jit(solution)/shard_map/ppermute | solution.py:59
  163.9 6.5 %collective-permute-done.31 = bf16[2,96,768]{2,1,0:T(8,128)(2,1)S(1)} collective-permute-done((bf16[2,96,768]{2,1,0:T(8,128)(2,1)S(1)}, bf16[2,96,768]{2,1,0:T(8,128)(2,1)S(1)}, u32[]{:S(2)}, u32[]{:S(2)}) %collective-permute-start.31) | collective-permute-done | bytes 294944 | tf_op jit(solution)/shard_map/ppermute | solution.py:59
  171.1 2.5 collective-permute-done.41
  174.2 2.0 collective-permute-done.32
  176.2 2.6 collective-permute-done.42
  187.3 12.6 %collective-permute-done.28 = bf16[1,96,3072]{2,1,0:T(8,128)(2,1)S(1)} collective-permute-done((bf16[1,96,3072]{2,1,0:T(8,128)(2,1)S(1)}, bf16[1,96,3072]{2,1,0:T(8,128)(2,1)S(1)}, u32[]{:S(2)}, u32[]{:S(2)}) %collective-permute-start.28) | collective-permute-done | bytes 589856 | tf_op jit(solution)/shard_map/ppermute | solution.py:59
  201.8 10.2 %collective-permute-done.38 = bf16[1,96,3072]{2,1,0:T(8,128)(2,1)S(1)} collective-permute-done((bf16[1,96,3072]{2,1,0:T(8,128)(2,1)S(1)}, bf16[1,96,3072]{2,1,0:T(8,128)(2,1)S(1)}, u32[]{:S(2)}, u32[]{:S(2)}) %collective-permute-start.38) | collective-permute-done | bytes 589856 | tf_op jit(solution)/shard_map/ppermute | solution.py:59
  214.9 5.6 %collective-permute-done.39 = bf16[1,96,1536]{2,1,0:T(8,128)(2,1)S(1)} collective-permute-done((bf16[1,96,1536]{2,1,0:T(8,128)(2,1)S(1)}, bf16[1,96,1536]{2,1,0:T(8,128)(2,1)S(1)}, u32[]{:S(2)}, u32[]{:S(2)}) %collective-permute-start.39) | collective-permute-done | bytes 294944 | tf_op jit(solution)/shard_map/ppermute | solution.py:59
  221.6 4.0 %collective-permute-start.34 = (bf16[96,1152]{1,0:T(8,128)(2,1)S(1)}, bf16[96,1152]{1,0:T(8,128)(2,1)S(1)}, u32[]{:S(2)}, u32[]{:S(2)}) collective-permute-start(bf16[96,1152]{1,0:T(8,128)(2,1)S(1)} %select_add_fusion.1), channel_id=1, source_target_pairs={{0,16},{4,20},{8,24},{12,28},{16,0},{20,4},{24,8},{28,12},{1,17},{... | collective-permute-start | bytes 663560 | tf_op jit(solution)/shard_map/ppermute | solution.py:59
  225.6 5.4 %collective-permute-done.43 = bf16[96,1152]{1,0:T(8,128)(2,1)S(1)} collective-permute-done((bf16[96,1152]{1,0:T(8,128)(2,1)S(1)}, bf16[96,1152]{1,0:T(8,128)(2,1)S(1)}, u32[]{:S(2)}, u32[]{:S(2)}) %collective-permute-start.43) | collective-permute-done | bytes 221216 | tf_op jit(solution)/shard_map/ppermute | solution.py:59
  232.7 7.4 %collective-permute-done.34 = bf16[96,1152]{1,0:T(8,128)(2,1)S(1)} collective-permute-done((bf16[96,1152]{1,0:T(8,128)(2,1)S(1)}, bf16[96,1152]{1,0:T(8,128)(2,1)S(1)}, u32[]{:S(2)}, u32[]{:S(2)}) %collective-permute-start.34) | collective-permute-done | bytes 221216 | tf_op jit(solution)/shard_map/ppermute | solution.py:59
  241.7 2.1 collective-permute-done.44
  244.0 2.7 collective-permute-done.35
  246.9 4.0 %collective-permute-done.45 = bf16[96,1152]{1,0:T(8,128)(2,1)S(1)} collective-permute-done((bf16[96,1152]{1,0:T(8,128)(2,1)S(1)}, bf16[96,1152]{1,0:T(8,128)(2,1)S(1)}, u32[]{:S(2)}, u32[]{:S(2)}) %collective-permute-start.45) | collective-permute-done | bytes 221216 | tf_op jit(solution)/shard_map/ppermute | solution.py:59
  254.2 4.0 %collective-permute-done.36.refs_1_ = bf16[96,2304]{1,0:T(8,128)(2,1)S(1)} collective-permute-done((bf16[96,2304]{1,0:T(8,128)(2,1)S(1)}, bf16[96,2304]{1,0:T(8,128)(2,1)S(1)}, u32[]{:S(2)}, u32[]{:S(2)}) %collective-permute-start.36) | collective-permute-done | bytes 442400 | tf_op jit(solution)/shard_map/ppermute | solution.py:59
  258.2 6.6 %collective-permute-done.46.refs_3_ = bf16[96,2304]{1,0:T(8,128)(2,1)S(1)} collective-permute-done((bf16[96,2304]{1,0:T(8,128)(2,1)S(1)}, bf16[96,2304]{1,0:T(8,128)(2,1)S(1)}, u32[]{:S(2)}, u32[]{:S(2)}) %collective-permute-start.46) | collective-permute-done | bytes 442400 | tf_op jit(solution)/shard_map/ppermute | solution.py:59
  265.6 3.4 %unpack.1 = (f32[2,96,1152]{2,1,0:T(8,128)}, f32[2,96,384]{2,1,0:T(8,128)}, f32[2,96,1536]{2,1,0:T(8,128)}, f32[2,384,384]{2,1,0:T(8,128)}) custom-call(s32[1]{0:T(128)} %bitcast.33.flag, bf16[96,2304]{1,0:T(8,128)(2,1)} %copy-done, bf16[96,2304]{1,0:T(8,128)(2,1)} %copy-done.10, bf16[96,2304]{1,0:T(8,128)(2,1)} %copy-done.1, bf16[96,2304]{1,0:T(8,128)(2,1)} %copy-done.11), custom_call_target="tpu_custom_call" | custom-call | tf_op jit(solution)/shard_map/unpack/pallas_call | solution.py:445
  (215 shorter events, 48.5 us)
Async XLA Ops:
  3.3 8.6 %collective-permute-start = (bf16[1,16,1280]{2,1,0:T(8,128)(2,1)}, bf16[1,16,1280]{2,1,0:T(8,128)(2,1)S(1)}, u32[]{:S(2)}, u32[]{:S(2)}) collective-permute-start(bf16[1,16,1280]{2,1,0:T(8,128)(2,1)} %bitcast.102), channel_id=1, source_target_pairs={{0,2},{1,3},{2,0},{3,1},{4,6},{5,7},{6,4},{7,5},{8,10},{9,11},{10,... | collective-permute-start | bytes 122888 | tf_op jit(solution)/shard_map/ppermute | solution.py:59
  9.0 30.7 %collective-permute-start.5 = (bf16[96,1536]{1,0:T(8,128)(2,1)}, bf16[96,1536]{1,0:T(8,128)(2,1)}, u32[]{:S(2)}, u32[]{:S(2)}) collective-permute-start(bf16[96,1536]{1,0:T(8,128)(2,1)} %get-tuple-element.51.rest_0_), channel_id=1, source_target_pairs={{0,2},{1,3},{2,0},{3,1},{4,6},{5,7},{6,4},{7,5},{8,10},{9,11},{10,... | collective-permute-start | bytes 884744 | tf_op jit(solution)/shard_map/ppermute | solution.py:59
  9.0 31.3 %collective-permute-start.4 = (bf16[96,1536]{1,0:T(8,128)(2,1)}, bf16[96,1536]{1,0:T(8,128)(2,1)}, u32[]{:S(2)}, u32[]{:S(2)}) collective-permute-start(bf16[96,1536]{1,0:T(8,128)(2,1)} %get-tuple-element.51.rest_0_), channel_id=1, source_target_pairs={{0,1},{1,0},{2,3},{3,2},{4,5},{5,4},{6,7},{7,6},{8,9},{9,8},{10,11... | collective-permute-start | bytes 884744 | tf_op jit(solution)/shard_map/ppermute | solution.py:59
  9.1 30.6 %collective-permute-start.8 = (bf16[96,3072]{1,0:T(8,128)(2,1)}, bf16[96,3072]{1,0:T(8,128)(2,1)S(1)}, u32[]{:S(2)}, u32[]{:S(2)}) collective-permute-start(bf16[96,3072]{1,0:T(8,128)(2,1)} %get-tuple-element.52.rest_4_.rest_0_), channel_id=1, source_target_pairs={{0,2},{1,3},{2,0},{3,1},{4,6},{5,7},{6,4},{7,5},{8,10},{9,11},{10,... | collective-permute-start | bytes 1769480 | tf_op jit(solution)/shard_map/ppermute | solution.py:59
  11.0 42.7 %collective-permute-start.7 = (bf16[96,3072]{1,0:T(8,128)(2,1)}, bf16[96,3072]{1,0:T(8,128)(2,1)S(1)}, u32[]{:S(2)}, u32[]{:S(2)}) collective-permute-start(bf16[96,3072]{1,0:T(8,128)(2,1)} %get-tuple-element.52.rest_4_.rest_0_), channel_id=1, source_target_pairs={{0,1},{1,0},{2,3},{3,2},{4,5},{5,4},{6,7},{7,6},{8,9},{9,8},{10,11... | collective-permute-start | bytes 1769480 | tf_op jit(solution)/shard_map/ppermute | solution.py:59
  16.5 15.0 %collective-permute-start.3 = (f32[1,6,2304]{2,0,1:T(1,128)S(1)}, f32[1,6,2304]{2,0,1:T(1,128)S(1)}, u32[]{:S(2)}, u32[]{:S(2)}) collective-permute-start(f32[1,6,2304]{2,0,1:T(1,128)S(1)} %get-tuple-element.130), channel_id=1, source_target_pairs={{0,2},{1,3},{2,0},{3,1},{4,6},{5,7},{6,4},{7,5},{8,10},{9,11},{10,... | collective-permute-start | bytes 165896 | tf_op jit(solution)/shard_map/ppermute | solution.py:59
  39.1 13.4 %collective-permute-start.14 = (bf16[96,3072]{1,0:T(8,128)(2,1)}, bf16[96,3072]{1,0:T(8,128)(2,1)}, u32[]{:S(2)}, u32[]{:S(2)}) collective-permute-start(bf16[96,3072]{1,0:T(8,128)(2,1)} %get-tuple-element.55.rest_4_), channel_id=1, source_target_pairs={{0,2},{1,3},{2,0},{3,1},{4,6},{5,7},{6,4},{7,5},{8,10},{9,11},{10,... | collective-permute-start | bytes 1769480 | tf_op jit(solution)/shard_map/ppermute | solution.py:59
  39.7 13.5 %collective-permute-start.6 = (bf16[96,1536]{1,0:T(8,128)(2,1)}, bf16[96,1536]{1,0:T(8,128)(2,1)}, u32[]{:S(2)}, u32[]{:S(2)}) collective-permute-start(bf16[96,1536]{1,0:T(8,128)(2,1)} %collective-permute-done.5.rest_2_), channel_id=1, source_target_pairs={{0,1},{1,0},{2,3},{3,2},{4,5},{5,4},{6,7},{7,6},{8,9},{9,8},{10,11... | collective-permute-start | bytes 884744 | tf_op jit(solution)/shard_map/ppermute | solution.py:59
  39.7 14.8 %collective-permute-start.9 = (bf16[96,3072]{1,0:T(8,128)(2,1)S(1)}, bf16[96,3072]{1,0:T(8,128)(2,1)S(1)}, u32[]{:S(2)}, u32[]{:S(2)}) collective-permute-start(bf16[96,3072]{1,0:T(8,128)(2,1)S(1)} %collective-permute-done.8.rest_6_.rest_2_), channel_id=1, source_target_pairs={{0,1},{1,0},{2,3},{3,2},{4,5},{5,4},{6,7},{7,6},{8,9},{9,8},{10,11... | collective-permute-start | bytes 1769480 | tf_op jit(solution)/shard_map/ppermute | solution.py:59
  40.3 34.6 %collective-permute-start.13 = (bf16[96,3072]{1,0:T(8,128)(2,1)}, bf16[96,3072]{1,0:T(8,128)(2,1)S(1)}, u32[]{:S(2)}, u32[]{:S(2)}) collective-permute-start(bf16[96,3072]{1,0:T(8,128)(2,1)} %get-tuple-element.55.rest_4_), channel_id=1, source_target_pairs={{0,1},{1,0},{2,3},{3,2},{4,5},{5,4},{6,7},{7,6},{8,9},{9,8},{10,11... | collective-permute-start | bytes 1769480 | tf_op jit(solution)/shard_map/ppermute | solution.py:59
  52.5 22.4 %collective-permute-start.15 = (bf16[96,3072]{1,0:T(8,128)(2,1)}, bf16[96,3072]{1,0:T(8,128)(2,1)}, u32[]{:S(2)}, u32[]{:S(2)}) collective-permute-start(bf16[96,3072]{1,0:T(8,128)(2,1)} %collective-permute-done.14.rest_6_), channel_id=1, source_target_pairs={{0,1},{1,0},{2,3},{3,2},{4,5},{5,4},{6,7},{7,6},{8,9},{9,8},{10,11... | collective-permute-start | bytes 1769480 | tf_op jit(solution)/shard_map/ppermute | solution.py:59
  53.2 21.7 %collective-permute-start.10 = (bf16[96,1536]{1,0:T(8,128)(2,1)}, bf16[96,1536]{1,0:T(8,128)(2,1)S(1)}, u32[]{:S(2)}, u32[]{:S(2)}) collective-permute-start(bf16[96,1536]{1,0:T(8,128)(2,1)} %get-tuple-element.54.rest_0_), channel_id=1, source_target_pairs={{0,1},{1,0},{2,3},{3,2},{4,5},{5,4},{6,7},{7,6},{8,9},{9,8},{10,11... | collective-permute-start | bytes 884744 | tf_op jit(solution)/shard_map/ppermute | solution.py:59
  53.7 21.2 %collective-permute-start.12 = (bf16[96,1536]{1,0:T(8,128)(2,1)}, bf16[96,1536]{1,0:T(8,128)(2,1)}, u32[]{:S(2)}, u32[]{:S(2)}) collective-permute-start(bf16[96,1536]{1,0:T(8,128)(2,1)} %copy-done.17), channel_id=1, source_target_pairs={{0,1},{1,0},{2,3},{3,2},{4,5},{5,4},{6,7},{7,6},{8,9},{9,8},{10,11... | collective-permute-start | bytes 884744 | tf_op jit(solution)/shard_map/ppermute | solution.py:59
  54.6 82.3 %collective-permute-start.24 = (bf16[1,4,3,384]{3,2,1,0:T(4,128)(2,1)S(1)}, bf16[1,4,3,384]{3,2,1,0:T(4,128)(2,1)S(1)}, u32[]{:S(2)}, u32[]{:S(2)}) collective-permute-start(bf16[1,4,3,384]{3,2,1,0:T(4,128)(2,1)S(1)} %get-tuple-element.124), channel_id=1, source_target_pairs={{0,4},{4,0},{8,12},{12,8},{16,20},{20,16},{24,28},{28,24},{1,5},{5... | collective-permute-start | bytes 27656 | tf_op jit(solution)/shard_map/ppermute | solution.py:59
  154.5 8.2 %collective-permute-start.40 = (bf16[2,96,1536]{2,1,0:T(8,128)(2,1)S(1)}, bf16[2,96,1536]{2,1,0:T(8,128)(2,1)S(1)}, u32[]{:S(2)}, u32[]{:S(2)}) collective-permute-start(bf16[2,96,1536]{2,1,0:T(8,128)(2,1)S(1)} %copy-done.14), channel_id=1, source_target_pairs={{0,1},{1,0},{2,3},{3,2},{4,5},{5,4},{6,7},{7,6},{8,9},{9,8},{10,11... | collective-permute-start | bytes 1769480 | tf_op jit(solution)/shard_map/ppermute | solution.py:59
  155.0 27.7 %collective-permute-start.27 = (bf16[2,96,3072]{2,1,0:T(8,128)(2,1)}, bf16[2,96,3072]{2,1,0:T(8,128)(2,1)S(1)}, u32[]{:S(2)}, u32[]{:S(2)}) collective-permute-start(bf16[2,96,3072]{2,1,0:T(8,128)(2,1)} %get-tuple-element.79), channel_id=1, source_target_pairs={{0,1},{1,0},{2,3},{3,2},{4,5},{5,4},{6,7},{7,6},{8,9},{9,8},{10,11... | collective-permute-start | bytes 3538952 | tf_op jit(solution)/shard_map/ppermute | solution.py:59
  155.1 29.2 %collective-permute-start.37 = (bf16[2,96,3072]{2,1,0:T(8,128)(2,1)}, bf16[2,96,3072]{2,1,0:T(8,128)(2,1)S(1)}, u32[]{:S(2)}, u32[]{:S(2)}) collective-permute-start(bf16[2,96,3072]{2,1,0:T(8,128)(2,1)} %get-tuple-element.83), channel_id=1, source_target_pairs={{0,1},{1,0},{2,3},{3,2},{4,5},{5,4},{6,7},{7,6},{8,9},{9,8},{10,11... | collective-permute-start | bytes 3538952 | tf_op jit(solution)/shard_map/ppermute | solution.py:59
  159.4 11.0 %collective-permute-start.31 = (bf16[2,96,768]{2,1,0:T(8,128)(2,1)S(1)}, bf16[2,96,768]{2,1,0:T(8,128)(2,1)S(1)}, u32[]{:S(2)}, u32[]{:S(2)}) collective-permute-start(bf16[2,96,768]{2,1,0:T(8,128)(2,1)S(1)} %get-tuple-element.107), channel_id=1, source_target_pairs={{0,4},{4,0},{8,12},{12,8},{16,20},{20,16},{24,28},{28,24},{1,5},{5... | collective-permute-start | bytes 884744 | tf_op jit(solution)/shard_map/ppermute | solution.py:59
  162.8 10.8 %collective-permute-start.41 = (bf16[2,96,768]{2,1,0:T(8,128)(2,1)S(1)}, bf16[2,96,768]{2,1,0:T(8,128)(2,1)S(1)}, u32[]{:S(2)}, u32[]{:S(2)}) collective-permute-start(bf16[2,96,768]{2,1,0:T(8,128)(2,1)S(1)} %get-tuple-element.105), channel_id=1, source_target_pairs={{0,4},{4,0},{8,12},{12,8},{16,20},{20,16},{24,28},{28,24},{1,5},{5... | collective-permute-start | bytes 884744 | tf_op jit(solution)/shard_map/ppermute | solution.py:59
  163.8 15.0 %collective-permute-start.20 = (bf16[16,8,2304]{2,1,0:T(8,128)(2,1)S(1)}, bf16[16,8,2304]{2,1,0:T(8,128)(2,1)S(1)}, u32[]{:S(2)}, u32[]{:S(2)}) collective-permute-start(bf16[16,8,2304]{2,1,0:T(8,128)(2,1)S(1)} %pad_maximum_fusion.2), channel_id=1, source_target_pairs={{0,1},{1,0},{2,3},{3,2},{4,5},{5,4},{6,7},{7,6},{8,9},{9,8},{10,11... | collective-permute-start | bytes 1769480 | tf_op jit(solution)/shard_map/ppermute | solution.py:59
  179.8 73.5 %collective-permute-start.21 = (f32[3,96]{1,0:T(4,128)S(1)}, f32[3,96]{1,0:T(4,128)S(1)}, u32[]{:S(2)}, u32[]{:S(2)}) collective-permute-start(f32[3,96]{1,0:T(4,128)S(1)} %bitcast.111), channel_id=1, source_target_pairs={{0,1},{1,0},{2,3},{3,2},{4,5},{5,4},{6,7},{7,6},{8,9},{9,8},{10,11... | collective-permute-start | bytes 3464 | tf_op jit(solution)/shard_map/ppermute | solution.py:59
  179.9 73.5 %collective-permute-start.22 = (f32[3,96]{1,0:T(4,128)S(1)}, f32[3,96]{1,0:T(4,128)S(1)}, u32[]{:S(2)}, u32[]{:S(2)}) collective-permute-start(f32[3,96]{1,0:T(4,128)S(1)} %bitcast.110), channel_id=1, source_target_pairs={{0,2},{1,3},{2,0},{3,1},{4,6},{5,7},{6,4},{7,5},{8,10},{9,11},{10,... | collective-permute-start | bytes 3464 | tf_op jit(solution)/shard_map/ppermute | solution.py:59
  180.5 72.9 %collective-permute-start.23 = (f32[3,96]{1,0:T(4,128)S(1)}, f32[3,96]{1,0:T(4,128)S(1)}, u32[]{:S(2)}, u32[]{:S(2)}) collective-permute-start(f32[3,96]{1,0:T(4,128)S(1)} %bitcast.109), channel_id=1, source_target_pairs={{0,3},{1,2},{2,1},{3,0},{4,7},{5,6},{6,5},{7,4},{8,11},{9,10},{10,... | collective-permute-start | bytes 3464 | tf_op jit(solution)/shard_map/ppermute | solution.py:59
  183.6 16.3 %collective-permute-start.28 = (bf16[1,96,3072]{2,1,0:T(8,128)(2,1)S(1)}, bf16[1,96,3072]{2,1,0:T(8,128)(2,1)S(1)}, u32[]{:S(2)}, u32[]{:S(2)}) collective-permute-start(bf16[1,96,3072]{2,1,0:T(8,128)(2,1)S(1)} %get-tuple-element.103), channel_id=1, source_target_pairs={{0,2},{1,3},{2,0},{3,1},{4,6},{5,7},{6,4},{7,5},{8,10},{9,11},{10,... | collective-permute-start | bytes 1769480 | tf_op jit(solution)/shard_map/ppermute | solution.py:59
  184.9 27.0 %collective-permute-start.38 = (bf16[1,96,3072]{2,1,0:T(8,128)(2,1)S(1)}, bf16[1,96,3072]{2,1,0:T(8,128)(2,1)S(1)}, u32[]{:S(2)}, u32[]{:S(2)}) collective-permute-start(bf16[1,96,3072]{2,1,0:T(8,128)(2,1)S(1)} %get-tuple-element.101), channel_id=1, source_target_pairs={{0,2},{1,3},{2,0},{3,1},{4,6},{5,7},{6,4},{7,5},{8,10},{9,11},{10,... | collective-permute-start | bytes 1769480 | tf_op jit(solution)/shard_map/ppermute | solution.py:59
  200.0 13.8 %collective-permute-start.29 = (bf16[1,96,1536]{2,1,0:T(8,128)(2,1)S(1)}, bf16[1,96,1536]{2,1,0:T(8,128)(2,1)S(1)}, u32[]{:S(2)}, u32[]{:S(2)}) collective-permute-start(bf16[1,96,1536]{2,1,0:T(8,128)(2,1)S(1)} %broadcast_select_fusion.7), channel_id=1, source_target_pairs={{0,4},{4,0},{8,12},{12,8},{16,20},{20,16},{24,28},{28,24},{1,5},{5... | collective-permute-start | bytes 884744 | tf_op jit(solution)/shard_map/ppermute | solution.py:59
  212.0 8.5 %collective-permute-start.39 = (bf16[1,96,1536]{2,1,0:T(8,128)(2,1)S(1)}, bf16[1,96,1536]{2,1,0:T(8,128)(2,1)S(1)}, u32[]{:S(2)}, u32[]{:S(2)}) collective-permute-start(bf16[1,96,1536]{2,1,0:T(8,128)(2,1)S(1)} %broadcast_select_fusion.6), channel_id=1, source_target_pairs={{0,4},{4,0},{8,12},{12,8},{16,20},{20,16},{24,28},{28,24},{1,5},{5... | collective-permute-start | bytes 884744 | tf_op jit(solution)/shard_map/ppermute | solution.py:59
  220.6 10.3 %collective-permute-start.43 = (bf16[96,1152]{1,0:T(8,128)(2,1)S(1)}, bf16[96,1152]{1,0:T(8,128)(2,1)S(1)}, u32[]{:S(2)}, u32[]{:S(2)}) collective-permute-start(bf16[96,1152]{1,0:T(8,128)(2,1)S(1)} %broadcast_select_fusion.12), channel_id=1, source_target_pairs={{0,8},{4,12},{8,0},{12,4},{16,24},{20,28},{24,16},{28,20},{1,9},{5... | collective-permute-start | bytes 663560 | tf_op jit(solution)/shard_map/ppermute | solution.py:59
  221.6 18.4 %collective-permute-start.34 = (bf16[96,1152]{1,0:T(8,128)(2,1)S(1)}, bf16[96,1152]{1,0:T(8,128)(2,1)S(1)}, u32[]{:S(2)}, u32[]{:S(2)}) collective-permute-start(bf16[96,1152]{1,0:T(8,128)(2,1)S(1)} %select_add_fusion.1), channel_id=1, source_target_pairs={{0,16},{4,20},{8,24},{12,28},{16,0},{20,4},{24,8},{28,12},{1,17},{... | collective-permute-start | bytes 663560 | tf_op jit(solution)/shard_map/ppermute | solution.py:59
  231.0 12.8 %collective-permute-start.44 = (bf16[96,1152]{1,0:T(8,128)(2,1)S(1)}, bf16[96,1152]{1,0:T(8,128)(2,1)S(1)}, u32[]{:S(2)}, u32[]{:S(2)}) collective-permute-start(bf16[96,1152]{1,0:T(8,128)(2,1)S(1)} %select_add_fusion), channel_id=1, source_target_pairs={{0,16},{4,20},{8,24},{12,28},{16,0},{20,4},{24,8},{28,12},{1,17},{... | collective-permute-start | bytes 663560 | tf_op jit(solution)/shard_map/ppermute | solution.py:59
  246.8 11.3 %collective-permute-start.36 = (bf16[96,2304]{1,0:T(8,128)(2,1)S(1)}, bf16[96,2304]{1,0:T(8,128)(2,1)S(1)}, u32[]{:S(2)}, u32[]{:S(2)}) collective-permute-start(bf16[96,2304]{1,0:T(8,128)(2,1)S(1)} %pad_maximum_fusion.3.refs_0_), channel_id=1, source_target_pairs={{0,4},{4,0},{8,12},{12,8},{16,20},{20,16},{24,28},{28,24},{1,5},{5... | collective-permute-start | bytes 1327112 | tf_op jit(solution)/shard_map/ppermute | solution.py:59
  251.0 13.8 %collective-permute-start.46 = (bf16[96,2304]{1,0:T(8,128)(2,1)S(1)}, bf16[96,2304]{1,0:T(8,128)(2,1)S(1)}, u32[]{:S(2)}, u32[]{:S(2)}) collective-permute-start(bf16[96,2304]{1,0:T(8,128)(2,1)S(1)} %pad_maximum_fusion.4.refs_2_), channel_id=1, source_target_pairs={{0,4},{4,0},{8,12},{12,8},{16,20},{20,16},{24,28},{28,24},{1,5},{5... | collective-permute-start | bytes 1327112 | tf_op jit(solution)/shard_map/ppermute | solution.py:59
  (34 other events, 201.3 us)
